TPU v7x, 512 devices: a whole 4x8x8 slice. The times are simulated.
512 devices in a mesh: grp: 2 (over x_hi), dp: 16 (over x_lo, z), mp: 16 (over y, core).
Axes of the slice: x: 4 (x_hi: 2, x_lo: 2; x = x_hi * 2 + x_lo), y: 8, z: 8, core: 2. Of those that a mesh axis runs over, the one named last changes fastest.
Arguments:
- captured: bfloat16 [3, 1024, 8192], P(None, 'mp', ('grp', 'dp')), may hold values from -9 to 9
- unite_weight: bfloat16 [3, 8192, 8192], P(None, ('grp', 'dp'), 'mp'), may hold values from -0.0390625 to 0.0390625
- heads: bfloat16 [2, 16000, 8192], P('grp', 'dp', 'mp'), may hold values from -10 to 10, as said below
- final_hidden: bfloat16 [1024, 8192], P('dp', 'mp'), may hold values from -9 to 9
- target_gain: float32 [8192], P('mp'), may hold values from 0.1 to 1.9
- draft_gain: float32 [8192], P('mp'), may hold values from 0.1 to 1.9
- lengths: int32 [16], replicated, may hold values from 32 to 64
Outputs:
- grad_terms: bfloat16 [2, 16000, 8192], P('grp', 'dp', 'mp')
- token_loss: float32 [1024], P('mp')
Inputs may be any that keep to these rules, and one draw needn't show every extreme that they name: `heads`: each row of a head has its own scale.
All inputs are finite; a program needn't handle non-finite values.
Results may differ from a plain program's by a relative error of at most 0.0051.
Values may be sent and summed in bfloat16 or wider, within the bound.
No kernel may reach another device: no remote copies, remote signals or barrier semaphores. Data moves between devices by JAX's collectives and lax.ppermute only.
A program may use at most 64 MiB of HBM per device.

v0:
```python
import jax
import jax.numpy as jnp
from jax import lax
from jax.sharding import PartitionSpec as P

EPSILON = 1e-05


def in_order(tiles, dim):
    tiles = jnp.moveaxis(tiles, 0, dim)
    dims = tiles.shape
    return tiles.reshape(*dims[:dim], dims[dim] * dims[dim + 1], *dims[dim + 2 :])


def copy_for_each(shard, axis):
    copies = jnp.broadcast_to(shard, (lax.axis_size(axis), *shard.shape))
    return lax.all_to_all(copies, axis, split_axis=0, concat_axis=0, tiled=True)


def gathered_copies(shard, axis, dim):
    return in_order(copy_for_each(shard, axis), dim)


def over_copies(shard, axis):
    return copy_for_each(shard, axis).sum(axis=0)


def in_one(arrays, axis):
    vector, at, outs = (jnp.concatenate([a.reshape(-1) for a in arrays]), 0, [])
    so_far = over_copies(vector, axis)
    for a in arrays:
        outs.append(so_far[at : at + a.size].reshape(a.shape))
        at += a.size
    return tuple(outs)


def gathered_once(shard, axis):
    leaves = jax.tree.leaves(shard)
    sequence = sorted(range(len(leaves)), key=lambda k: -leaves[k].size)
    width = (1, *leaves[sequence[0]].shape)[-1]
    lines = [
        jnp.pad(leaves[k].reshape(-1), (0, -leaves[k].size % width)).reshape(-1, width)
        for k in sequence
    ]
    both, at, found = (copy_for_each(jnp.concatenate(lines), axis), 0, {})
    for k, line in zip(sequence, lines):
        piece = both[:, at : at + len(line)].reshape(len(both), -1)
        found[k] = piece[:, : leaves[k].size].reshape(-1, *leaves[k].shape)
        at += len(line)
    numbers = iter(range(len(leaves)))
    return jax.tree.map(lambda _: found[next(numbers)], shard)


def combined_pairwise(pieces, combine):
    while len(jax.tree.leaves(pieces)[0]) > 1:
        pieces = jax.vmap(combine)(
            *(jax.tree.map(lambda part: part[side::2], pieces) for side in (0, 1))
        )
    return jax.tree.map(lambda part: part[0], pieces)


def merged(shard, axis, combine):
    pieces = gathered_once(shard, axis)
    return combined_pairwise(pieces, combine)


def partner(shard, axis, stride):
    return lax.ppermute(shard, axis, [(i, i ^ 1 << stride) for i in range(lax.axis_size(axis))])


def per_device(captured, unite_weight, heads, final_hidden, target_gain, draft_gain, lengths):
    model_width = final_hidden.shape[1] * lax.axis_size("mp")
    slab_length = final_hidden.shape[0]
    is_target = lax.axis_index("grp") == 0
    head_rows = heads[0]
    segment = gathered_copies(captured, "mp", 1)
    running = jnp.dot(segment[0], unite_weight[0], preferred_element_type=jnp.float32)
    for layer_index in range(1, segment.shape[0]):
        running = running + jnp.dot(
            segment[layer_index], unite_weight[layer_index], preferred_element_type=jnp.float32
        )
    united = lax.psum(running, ("grp", "dp"))
    last_values = gathered_copies(final_hidden, "dp", 0).astype(jnp.float32)
    square_sums = in_one(
        (jnp.sum(united * united, axis=1), jnp.sum(last_values * last_values, axis=1)), "mp"
    )
    draft_scale = lax.rsqrt(square_sums[0] / model_width + EPSILON)
    target_scale = lax.rsqrt(square_sums[1] / model_width + EPSILON)
    draft_rows = (united * draft_scale[:, None] * draft_gain[None, :]).astype(jnp.bfloat16)
    target_rows = (last_values * target_scale[:, None] * target_gain[None, :]).astype(jnp.bfloat16)
    own_rows = jnp.where(is_target, target_rows, draft_rows)
    row_share = own_rows.shape[0] // lax.axis_size("mp")
    logits = lax.psum_scatter(
        jnp.einsum("td,vd->tv", own_rows, head_rows, preferred_element_type=jnp.float32),
        "mp",
        scatter_dimension=0,
        tiled=True,
    )
    local_max = jnp.max(logits, axis=1)
    local_total = jnp.sum(jnp.exp(logits - local_max[:, None]), axis=1)

    def combine(first_pair, second_pair):
        joined_max = jnp.maximum(first_pair[0], second_pair[0])
        joined_total = first_pair[1] * jnp.exp(first_pair[0] - joined_max) + second_pair[
            1
        ] * jnp.exp(second_pair[0] - joined_max)
        return (joined_max, joined_total)

    row_max, row_total = merged((local_max, local_total), "dp", combine)
    shifted = logits - row_max[:, None]
    probabilities = jnp.exp(shifted) / row_total[:, None]
    log_probs = shifted - jnp.log(row_total)[:, None]
    outgoing = jnp.where(is_target, probabilities, log_probs)
    incoming = partner(outgoing, "grp", 0)
    target_probs = jnp.where(is_target, probabilities, incoming)
    draft_logs = jnp.where(is_target, incoming, log_probs)
    token_index = lax.axis_index("mp") * row_share + lax.iota(jnp.int32, row_share)
    slab_index = token_index // slab_length
    position = token_index - slab_index * slab_length
    matches = slab_index[:, None] == lax.iota(jnp.int32, lengths.shape[0])[None, :]
    valid_len = jnp.sum(jnp.where(matches, lengths[None, :], 0), axis=1)
    valid_mask = (position < valid_len).astype(jnp.float32)
    valid_total = jnp.sum(lengths).astype(jnp.float32)
    cross_term = over_copies(jnp.sum(target_probs * draft_logs, axis=1), "dp")
    token_loss = -valid_mask * cross_term
    mixed = jnp.where(is_target, probabilities, probabilities - target_probs)
    weighted = (mixed * (valid_mask / valid_total)[:, None]).astype(jnp.bfloat16)
    summed = jnp.einsum(
        "tv,td->vd",
        lax.all_gather(weighted, "mp", axis=0, tiled=True),
        draft_rows,
        preferred_element_type=jnp.float32,
    )
    sign_factor = jnp.where(is_target, -1.0, 1.0).astype(jnp.float32)
    grad_terms = (sign_factor * summed).astype(jnp.bfloat16)[None]
    return (grad_terms, token_loss)


def solution(mesh):
    in_specs = (
        P(None, "mp", ("grp", "dp")),
        P(None, ("grp", "dp"), "mp"),
        P("grp", "dp", "mp"),
        P("dp", "mp"),
        P("mp"),
        P("mp"),
        P(),
    )
    out_specs = (P("grp", "dp", "mp"), P("mp"))
    return jax.shard_map(
        per_device, mesh=mesh, in_specs=in_specs, out_specs=out_specs, check_vma=False
    )
```

profile of v0, /device:TPU:1, one launch (start us, length us, event | category | flops | bytes accessed | tf_op | source)
XLA Modules:
  0.0 401.8 jit_solution(5204446621175504910)
XLA Ops:
  7.2 0.0 copy-start
  7.2 0.0 copy-start.3
  7.2 1.2 broadcast_in_dim.41
  8.4 49.7 %all_to_all.27 = bf16[16,3,64,256]{3,2,1,0:T(8,128)(2,1)} all-to-all(bf16[16,3,64,256]{3,2,1,0:T(8,128)(2,1)S(1)} %broadcast_in_dim.41), channel_id=1, replica_groups=mesh['grp'=2,'dp'=16,'mp'=16] {'mp'}, dimensions={0} | all-to-all | bytes 3145728 | tf_op jit(solution)/shard_map/all_to_all | solution.py:17
  58.1 0.0 copy-done.3
  58.1 1.1 broadcast_in_dim.40
  59.2 9.5 %all-to-all-start = ((bf16[16,64,512]{2,1,0:T(8,128)(2,1)}), bf16[16,64,512]{2,1,0:T(8,128)(2,1)S(1)}, u32[]{:S(2)}, u32[]{:S(2)}) async-start(bf16[16,64,512]{2,1,0:T(8,128)(2,1)} %broadcast_in_dim.40), calls=%async_computation | async-start | bytes 2097152 | tf_op jit(solution)/shard_map/all_to_all | solution.py:17
  68.7 0.0 all-reduce.2.cloned.1.call-start
  68.8 0.0 copy-start.2
  68.8 1.6 fusion.21
  70.4 0.0 copy-done.2
  70.4 0.4 fusion.11
  70.8 0.4 fusion.9
  71.3 1.8 add_add_fusion
  73.1 0.0 all-reduce.2.cloned.1.call-update
  73.1 0.0 copy-start.4
  73.1 0.0 copy-start.5
  73.1 26.0 %all-to-all-done = bf16[16,64,512]{2,1,0:T(8,128)(2,1)S(1)} async-done(((bf16[16,64,512]{2,1,0:T(8,128)(2,1)}), bf16[16,64,512]{2,1,0:T(8,128)(2,1)S(1)}, u32[]{:S(2)}, u32[]{:S(2)}) %all-to-all-start) | async-done | bytes 1048608 | tf_op jit(solution)/shard_map/all_to_all | solution.py:17
  99.1 0.3 multiply_reduce_fusion
  99.3 0.1 reduce_sum.76
  99.4 134.8 %all-reduce.2.cloned.1.call-done = f32[1024,512]{1,0:T(8,128)} async-done(((f32[1024,512]{1,0:T(8,128)}), f32[1024,512]{1,0:T(8,128)}) %all-reduce.2.cloned.1.call-update) | async-done | bytes 2097168 | tf_op jit(solution)/shard_map/psum | solution.py:82
  234.2 1.8 multiply_reduce_fusion.1
  236.0 0.7 broadcast_in_dim.42
  236.8 11.5 %all-to-all-start.2 = ((f32[16,1,2048]{2,1,0:T(1,128)}), f32[16,1,2048]{2,1,0:T(1,128)S(1)}, u32[]{:S(2)}, u32[]{:S(2)}) async-start(f32[16,1,2048]{2,1,0:T(1,128)} %broadcast_in_dim.42), calls=%async_computation.2 | async-start | bytes 262144 | tf_op jit(solution)/shard_map/all_to_all | solution.py:17
  248.3 0.0 reduce-scatter.2.cloned.1.call-start
  248.4 8.8 %all-to-all-done.2 = f32[16,1,2048]{2,1,0:T(1,128)S(1)} async-done(((f32[16,1,2048]{2,1,0:T(1,128)}), f32[16,1,2048]{2,1,0:T(1,128)S(1)}, u32[]{:S(2)}, u32[]{:S(2)}) %all-to-all-start.2) | async-done | bytes 131104 | tf_op jit(solution)/shard_map/all_to_all | solution.py:17
  257.2 0.1 reduce_sum.77
  257.3 0.0 copy-done.4
  257.3 0.0 copy-done.5
  257.3 2.1 fusion.3
  259.4 0.0 copy-done
  259.4 3.2 fusion.4
  262.7 0.0 copy-start.6
  262.7 0.0 reduce-scatter.2.cloned.1.call-update
  262.7 0.0 copy-start.1
  262.7 56.1 %reduce-scatter.2.cloned.1.call-done = f32[64,1000]{1,0:T(8,128)} async-done(((f32[1024,1000]{1,0:T(8,128)}), f32[64,1000]{1,0:T(8,128)}) %reduce-scatter.2.cloned.1.call-update) | async-done | bytes 256016 | tf_op jit(solution)/shard_map/reduce_scatter | solution.py:93
  318.8 1.1 reduce_max.9
  319.9 1.2 exponential_reduce_fusion
  321.1 0.7 reshape.80
  321.8 7.1 %all-to-all-start.3 = ((f32[16,1,128]{2,1,0:T(1,128)}), f32[16,1,128]{2,1,0:T(1,128)S(1)}, u32[]{:S(2)}, u32[]{:S(2)}) async-start(f32[16,1,128]{2,1,0:T(1,128)} %reshape.80), calls=%async_computation.4 | async-start | bytes 16384 | tf_op jit(solution)/shard_map/all_to_all | solution.py:17
  329.0 0.0 all-gather.2.cloned.1.call-start
  329.0 7.2 %all-to-all-done.3 = f32[16,1,128]{2,1,0:T(1,128)S(1)} async-done(((f32[16,1,128]{2,1,0:T(1,128)}), f32[16,1,128]{2,1,0:T(1,128)S(1)}, u32[]{:S(2)}, u32[]{:S(2)}) %all-to-all-start.3) | async-done | bytes 8224 | tf_op jit(solution)/shard_map/all_to_all | solution.py:17
  336.2 0.5 broadcast.109
  336.7 0.7 reduce.3
  337.4 0.1 reshape.81
  337.8 1.8 subtract_select_fusion.1
  339.6 4.3 %collective-permute-start = (f32[64,1000]{1,0:T(8,128)}, f32[64,1000]{1,0:T(8,128)S(1)}, u32[]{:S(2)}, u32[]{:S(2)}) collective-permute-start(f32[64,1000]{1,0:T(8,128)} %subtract_select_fusion.1), channel_id=1, source_target_pairs={{0,256},{256,0},{1,257},{257,1},{2,258},{258,2},{3,259},{259,3},{4... | collective-permute-start | bytes 768008 | tf_op jit(solution)/shard_map/ppermute | solution.py:68
  343.9 0.0 copy-done.6
  343.9 0.1 select_reduce_fusion
  344.0 0.6 reduce_sum.80
  345.3 3.1 collective-permute-done
  348.4 1.9 multiply_reduce_fusion.2
  350.4 0.0 all-gather.2.cloned.1.call-update
  350.4 0.6 broadcast_in_dim.47
  351.0 3.4 all-to-all-start.4
  354.4 7.1 %all-to-all-done.4 = f32[16,1,64]{2,1,0:T(1,128)S(1)} async-done(((f32[16,1,64]{2,1,0:T(1,128)}), f32[16,1,64]{2,1,0:T(1,128)S(1)}, u32[]{:S(2)}, u32[]{:S(2)}) %all-to-all-start.4) | async-done | bytes 4128 | tf_op jit(solution)/shard_map/all_to_all | solution.py:17
  361.6 0.5 negate_multiply_fusion
  362.1 29.3 %all-gather.2.cloned.1.call-done = bf16[1024,1000]{1,0:T(8,128)(2,1)} async-done(((bf16[64,1000]{1,0:T(8,128)(2,1)}), bf16[1024,1000]{1,0:T(8,128)(2,1)}) %all-gather.2.cloned.1.call-update) | async-done | bytes 2048016 | tf_op jit(solution)/shard_map/all_gather | solution.py:130
  391.4 0.0 copy-done.1
  391.4 3.9 fusion.2
  (25 shorter events, 0.4 us)
Async XLA Ops:
  7.2 252.3 %copy-start = (bf16[1,1000,512]{2,1,0:T(8,128)(2,1)S(1)}, bf16[1,1000,512]{2,1,0:T(8,128)(2,1)}, u32[]{:S(2)}) copy-start(bf16[1,1000,512]{2,1,0:T(8,128)(2,1)} %param.9) | copy-start | bytes 3072004
  7.2 50.9 %copy-start.3 = (bf16[64,512]{1,0:T(8,128)(2,1)S(1)}, bf16[64,512]{1,0:T(8,128)(2,1)}, u32[]{:S(2)}) copy-start(bf16[64,512]{1,0:T(8,128)(2,1)} %param.10) | copy-start | bytes 196612
  59.2 39.9 %all-to-all-start = ((bf16[16,64,512]{2,1,0:T(8,128)(2,1)}), bf16[16,64,512]{2,1,0:T(8,128)(2,1)S(1)}, u32[]{:S(2)}, u32[]{:S(2)}) async-start(bf16[16,64,512]{2,1,0:T(8,128)(2,1)} %broadcast_in_dim.40), calls=%async_computation | async-start | bytes 2097152 | tf_op jit(solution)/shard_map/all_to_all | solution.py:17
  68.7 165.5 %all-reduce.2.cloned.1.call-start = ((), (), s32[]{:S(2)}) async-start(), calls=%async_computation.6 | async-start | bytes 4194304 | tf_op jit(solution)/shard_map/psum | solution.py:82
  68.8 1.6 copy-start.2
  73.1 184.2 %copy-start.4 = (f32[512]{0:T(512)S(1)}, f32[512]{0:T(512)}, u32[]{:S(2)}) copy-start(f32[512]{0:T(512)} %param.11) | copy-start | bytes 6148
  73.1 184.2 %copy-start.5 = (f32[512]{0:T(512)S(1)}, f32[512]{0:T(512)}, u32[]{:S(2)}) copy-start(f32[512]{0:T(512)} %param.12) | copy-start | bytes 6148
  236.8 20.4 %all-to-all-start.2 = ((f32[16,1,2048]{2,1,0:T(1,128)}), f32[16,1,2048]{2,1,0:T(1,128)S(1)}, u32[]{:S(2)}, u32[]{:S(2)}) async-start(f32[16,1,2048]{2,1,0:T(1,128)} %broadcast_in_dim.42), calls=%async_computation.2 | async-start | bytes 262144 | tf_op jit(solution)/shard_map/all_to_all | solution.py:17
  248.3 70.5 %reduce-scatter.2.cloned.1.call-start = ((), (), s32[]{:S(2)}) async-start(), calls=%async_computation.7 | async-start | bytes 4456448 | tf_op jit(solution)/shard_map/reduce_scatter | solution.py:93
  262.7 81.2 %copy-start.6 = (s32[16]{0:T(128)S(1)}, s32[16]{0:T(128)}, u32[]{:S(2)}) copy-start(s32[16]{0:T(128)} %param.13) | copy-start | bytes 196
  262.7 128.7 %copy-start.1 = (f32[1024,512]{1,0:T(8,128)S(1)}, f32[1024,512]{1,0:T(8,128)}, u32[]{:S(2)}) copy-start(f32[1024,512]{1,0:T(8,128)} %all-reduce.2.cloned.1.call-done) | copy-start | bytes 6291460
  321.8 14.4 %all-to-all-start.3 = ((f32[16,1,128]{2,1,0:T(1,128)}), f32[16,1,128]{2,1,0:T(1,128)S(1)}, u32[]{:S(2)}, u32[]{:S(2)}) async-start(f32[16,1,128]{2,1,0:T(1,128)} %reshape.80), calls=%async_computation.4 | async-start | bytes 16384 | tf_op jit(solution)/shard_map/all_to_all | solution.py:17
  329.0 62.4 %all-gather.2.cloned.1.call-start = ((), (), s32[]{:S(2)}) async-start(), calls=%async_computation.8 | async-start | bytes 2228224 | tf_op jit(solution)/shard_map/all_gather | solution.py:130
  339.6 8.8 %collective-permute-start = (f32[64,1000]{1,0:T(8,128)}, f32[64,1000]{1,0:T(8,128)S(1)}, u32[]{:S(2)}, u32[]{:S(2)}) collective-permute-start(f32[64,1000]{1,0:T(8,128)} %subtract_select_fusion.1), channel_id=1, source_target_pairs={{0,256},{256,0},{1,257},{257,1},{2,258},{258,2},{3,259},{259,3},{4... | collective-permute-start | bytes 768008 | tf_op jit(solution)/shard_map/ppermute | solution.py:68
  351.0 10.6 %all-to-all-start.4 = ((f32[16,1,64]{2,1,0:T(1,128)}), f32[16,1,64]{2,1,0:T(1,128)S(1)}, u32[]{:S(2)}, u32[]{:S(2)}) async-start(f32[16,1,64]{2,1,0:T(1,128)} %broadcast_in_dim.47), calls=%async_computation.5 | async-start | bytes 16384 | tf_op jit(solution)/shard_map/all_to_all | solution.py:17
Sparse Core Ops, SparseCore 0:
  73.2 160.9 all-reduce.1
  262.8 55.9 reduce-scatter.1
  350.5 40.8 all-gather.1
where the time goes:
time: 402 us
  waiting for transfers between devices  272 us (68%)
  blocking collectives  49.7 us (12%)
  starting transfers between devices  36 us (9%)
  between operations  14.7 us (4%)
  other arithmetic  12.3 us (3%)
  matrix products  9.76 us (2%)
  local copies, waits for them, and re-layouts  6.83 us (2%)
    psum x1, waiting for transfers between devices, per_device(): united = lax.psum(running, ('grp', 'dp'))  135 us
    reduce_scatter x1, waiting for transfers between devices, per_device(): lax.psum_scatter(jnp.einsum('td,vd->tv', own_rows, head_rows, preferred_e...  56.1 us
    all_to_all x1, blocking collectives, copy_for_each(): return lax.all_to_all(copies, axis, split_axis=0, concat_axis=0, tiled=True)  49.7 us
    all_to_all x4, waiting for transfers between devices, copy_for_each(): return lax.all_to_all(copies, axis, split_axis=0, concat_axis=0, tiled=True)  49.1 us
    all_to_all x4, starting transfers between devices, copy_for_each(): return lax.all_to_all(copies, axis, split_axis=0, concat_axis=0, tiled=True)  31.6 us
    all_gather x1, waiting for transfers between devices, per_device(): lax.all_gather(weighted, 'mp', axis=0, tiled=True)  29.3 us
  transfers between devices with their start and end apart: 8, of which 8 were waited for; matrix products, arithmetic and copies ran while one was open for 2% of the time, Pallas kernels for 0%

commit v1 on v0

v1 whole, which is shorter than its diff:
```python
import jax
import jax.numpy as jnp
from jax import lax
from jax.sharding import Mesh, PartitionSpec as P

EPSILON = 1e-05
SLABS = ("xl", "z")
BLOCKS = ("grp", "xl", "z")
COLUMNS = ("y", "core")


def exchanged(tiles, axes):
    return lax.all_to_all(tiles, axes, split_axis=0, concat_axis=0, tiled=True)


def copied(shard, axes):
    return exchanged(jnp.broadcast_to(shard, (lax.axis_size(axes), *shard.shape)), axes)


def from_other_core(shard):
    return lax.ppermute(shard, "core", [(0, 1), (1, 0)])


def from_other_group(shard):
    return lax.ppermute(shard, "grp", [(0, 1), (1, 0)])


def per_device(captured, unite_weight, heads, final_hidden, target_gain, draft_gain, lengths):
    f32, bf16, half = jnp.float32, jnp.bfloat16, jnp.float16
    columns = final_hidden.shape[1]
    model_width = columns * lax.axis_size(COLUMNS)
    layers, slab, features = captured.shape
    n_y = lax.axis_size("y")
    n_slabs = lax.axis_size(SLABS)
    part = slab // 2
    group = lax.axis_index("grp")
    core = lax.axis_index("core")
    is_target = group == 0
    is_first = core == 0
    vocab = heads.shape[1]

    own_heads = heads[0]
    other_heads = from_other_group(own_heads)
    both_heads = jnp.stack(
        [
            jnp.where(is_target, own_heads, other_heads),
            jnp.where(is_target, other_heads, own_heads),
        ]
    )
    core_heads = from_other_core(both_heads)

    hidden_part = jnp.where(is_target, final_hidden[:part], final_hidden[part:])
    hidden_rows = copied(hidden_part, SLABS).astype(f32)

    block = captured.transpose(1, 0, 2).reshape(slab, layers * features)
    mine = copied(block, "y")
    other = from_other_core(mine)
    tokens = jnp.stack(
        [jnp.where(is_first, mine, other), jnp.where(is_first, other, mine)], axis=1
    ).reshape(-1, layers * features)
    partial = jnp.dot(
        tokens, unite_weight.reshape(layers * features, columns), preferred_element_type=f32
    )
    pieces = partial.astype(half).reshape(n_slabs, 2, part, columns).transpose(1, 0, 2, 3)
    received = exchanged(pieces.reshape(-1, part, columns), BLOCKS)
    united = jnp.sum(received.astype(f32), axis=0)

    squares = jnp.concatenate(
        [
            jnp.sum(united * united, axis=1),
            jnp.sum(hidden_rows * hidden_rows, axis=2).reshape(-1),
        ]
    )
    square_sums = jnp.sum(copied(squares, COLUMNS), axis=0)
    scales = lax.rsqrt(square_sums / model_width + EPSILON)
    draft_part = (united * scales[:part, None] * draft_gain[None, :]).astype(bf16)
    draft_rows = copied(draft_part, SLABS)
    hidden_scale = scales[part:].reshape(n_slabs, part, 1)
    target_rows = (hidden_rows * hidden_scale * target_gain[None, None, :]).astype(bf16)

    def logits_of(rows, which):
        by_core = rows.reshape(n_y, 2, part, columns)
        kept = jnp.where(is_first, by_core[:, 0], by_core[:, 1])
        given = jnp.where(is_first, by_core[:, 1], by_core[:, 0])
        taken = from_other_core(given)
        sums = jnp.einsum(
            "ytd,vd->ytv", kept, both_heads[which], preferred_element_type=f32
        ) + jnp.einsum("ytd,vd->ytv", taken, core_heads[which], preferred_element_type=f32)
        return jnp.sum(exchanged(sums.astype(half), "y").astype(f32), axis=0)

    def row_stats(logits):
        top = jnp.max(logits, axis=1)
        return top, jnp.sum(jnp.exp(logits - top[:, None]), axis=1)

    def combined(tops, totals):
        top = jnp.max(tops, axis=0)
        return top, jnp.sum(totals * jnp.exp(tops - top[None]), axis=0)

    target_logits = logits_of(target_rows, 0)
    target_stats = copied(jnp.stack(row_stats(target_logits)), SLABS)
    target_top, target_total = combined(target_stats[:, 0], target_stats[:, 1])
    target_probs = jnp.exp(target_logits - target_top[:, None]) / target_total[:, None]

    draft_logits = logits_of(draft_rows, 1)
    top, total = row_stats(draft_logits)
    crossed = jnp.sum(target_probs * (draft_logits - top[:, None]), axis=1)
    mass = jnp.sum(target_probs, axis=1)
    stats = copied(jnp.stack([top, total, crossed, mass]), SLABS)
    draft_top, draft_total = combined(stats[:, 0], stats[:, 1])
    draft_probs = jnp.exp(draft_logits - draft_top[:, None]) / draft_total[:, None]
    shift = stats[:, 0] - draft_top[None] - jnp.log(draft_total)[None]
    cross_term = jnp.sum(stats[:, 2] + stats[:, 3] * shift, axis=0)

    slab_index = lax.axis_index("y") * 2 + core
    position = group * part + lax.iota(jnp.int32, part)
    valid_len = jnp.sum(
        jnp.where(lax.iota(jnp.int32, lengths.shape[0]) == slab_index, lengths, 0)
    )
    valid_mask = (position < valid_len).astype(f32)
    valid_total = jnp.sum(lengths).astype(f32)
    own_loss = -valid_mask * cross_term
    other_loss = from_other_group(own_loss)
    token_loss = jnp.concatenate(
        [jnp.where(is_target, own_loss, other_loss), jnp.where(is_target, other_loss, own_loss)]
    )

    weights = (valid_mask / valid_total)[:, None]
    weighted = (target_probs * weights).astype(bf16)
    delta = ((draft_probs - target_probs) * weights).astype(bf16)
    outgoing = jnp.concatenate(
        [
            jnp.broadcast_to(weighted, (n_y, part, vocab)),
            jnp.broadcast_to(delta, (n_y, part, vocab)),
        ]
    )
    gathered = exchanged(outgoing, ("grp", "y"))
    core_gathered = from_other_core(gathered)

    other_rows = from_other_group(draft_rows)
    all_rows = jnp.stack(
        [
            jnp.where(is_target, draft_rows, other_rows),
            jnp.where(is_target, other_rows, draft_rows),
        ]
    ).reshape(2, n_y, 2, part, columns)
    own_side = jnp.where(is_first, all_rows[:, :, 0], all_rows[:, :, 1])
    core_side = jnp.where(is_first, all_rows[:, :, 1], all_rows[:, :, 0])

    def gradient(weights_by_token, rows_by_token):
        return jnp.einsum(
            "tv,td->vd",
            weights_by_token.reshape(-1, vocab),
            rows_by_token.reshape(-1, columns),
            preferred_element_type=f32,
        )

    summed = gradient(gathered, own_side) + gradient(core_gathered, core_side)
    sign_factor = jnp.where(is_target, -1.0, 1.0).astype(f32)
    grad_terms = (sign_factor * summed).astype(bf16)[None]
    return (grad_terms, token_loss)


def solution(mesh):
    sizes = mesh.shape
    grid = mesh.devices.reshape(sizes["grp"], 2, sizes["dp"] // 2, sizes["mp"] // 2, 2)
    fine = Mesh(grid, ("grp", "xl", "z", "y", "core"))
    in_specs = (
        P(None, COLUMNS, BLOCKS),
        P(None, BLOCKS, COLUMNS),
        P("grp", SLABS, COLUMNS),
        P(SLABS, COLUMNS),
        P(COLUMNS),
        P(COLUMNS),
        P(),
    )
    out_specs = (P("grp", SLABS, COLUMNS), P(COLUMNS))
    return jax.shard_map(
        per_device, mesh=fine, in_specs=in_specs, out_specs=out_specs, check_vma=False
    )
```

time: 402 us -> 264 us (0.66)
  waiting for transfers between devices: 272 us -> 103 us
  starting transfers between devices: 36 us -> 77.9 us
  between operations: 14.7 us -> 1.88 us
    psum x1 -> x0, waiting for transfers between devices: 135 us -> none  [per_device(): united = lax.psum(running, ('grp', 'dp'))]
    reduce_scatter x1 -> x0, waiting for transfers between devices: 56.1 us -> none  [per_device(): lax.psum_scatter(jnp.einsum('td,vd->tv', own_rows, head_rows, preferred_e...]
    ppermute x1 -> x8, waiting for transfers between devices: 3.11 us -> 58.8 us  [the longest x3 57.7 us: from_other_group(): return lax.ppermute(shard, 'grp', [(0, 1), (1, 0)])]
    all_gather x1 -> x0, waiting for transfers between devices: 29.3 us -> none  [per_device(): lax.all_gather(weighted, 'mp', axis=0, tiled=True)]
    ppermute x1 -> x8, starting transfers between devices: 4.26 us -> 31.1 us  [the longest x5 19.1 us: from_other_core(): return lax.ppermute(shard, 'core', [(0, 1), (1, 0)])]
    all_to_all x4 -> x7, starting transfers between devices: 31.6 us -> 46.8 us  [exchanged(): return lax.all_to_all(tiles, axes, split_axis=0, concat_axis=0, tiled=True)]
    all_to_all x4 -> x7, waiting for transfers between devices: 49.1 us -> 44.5 us  [exchanged(): return lax.all_to_all(tiles, axes, split_axis=0, concat_axis=0, tiled=True)]
    all_to_all x1 -> x3, blocking collectives: 49.7 us -> 50.3 us  [exchanged(): return lax.all_to_all(tiles, axes, split_axis=0, concat_axis=0, tiled=True)]
  transfers between devices with their start and end apart: 8 -> 15, of which waited for: 8 -> 9; matrix products, arithmetic and copies ran while one was open for 2% -> 9% of each run, Pallas kernels for 0% -> 0%
where the time goes in v1:
time: 264 us; the launch traced here: 263 us
  waiting for transfers between devices  103 us (39%)
  starting transfers between devices  77.9 us (30%)
  blocking collectives  50.3 us (19%)
  other arithmetic  14.3 us (5%)
  matrix products  9.54 us (4%)
  local copies, waits for them, and re-layouts  5.72 us (2%)
    ppermute x3, waiting for transfers between devices, from_other_group(): return lax.ppermute(shard, 'grp', [(0, 1), (1, 0)])  57.7 us
    all_to_all x3, blocking collectives, exchanged(): return lax.all_to_all(tiles, axes, split_axis=0, concat_axis=0, tiled=True)  50.3 us
    all_to_all x7, starting transfers between devices, exchanged(): return lax.all_to_all(tiles, axes, split_axis=0, concat_axis=0, tiled=True)  46.8 us
    all_to_all x7, waiting for transfers between devices, exchanged(): return lax.all_to_all(tiles, axes, split_axis=0, concat_axis=0, tiled=True)  44.5 us
    ppermute x5, starting transfers between devices, from_other_core(): return lax.ppermute(shard, 'core', [(0, 1), (1, 0)])  19.1 us
    ppermute x3, starting transfers between devices, from_other_group(): return lax.ppermute(shard, 'grp', [(0, 1), (1, 0)])  12 us
  transfers between devices with their start and end apart: 15, of which 9 were waited for; matrix products, arithmetic and copies ran while one was open for 9% of the time, Pallas kernels for 0%

profile of v1, /device:TPU:1, one launch (start us, length us, event | category | flops | bytes accessed | tf_op | source)
XLA Modules:
  0.0 263.0 jit_solution(4229570920894827251)
XLA Ops:
  0.7 1.0 copy.52
  1.7 27.9 %all_to_all.51 = bf16[8,64,768]{2,1,0:T(8,128)(2,1)S(1)} all-to-all(bf16[8,64,768]{2,1,0:T(8,128)(2,1)S(1)} %broadcast_in_dim.23), channel_id=1, replica_groups=mesh['grp'=2,'xl'=2,'z'=8,'y'=8,'core'=2] {'y'}, dimensions={0} | all-to-all | bytes 1572864 | tf_op jit(solution)/shard_map/all_to_all | solution.py:13
  29.6 5.5 %collective-permute-start = (bf16[8,64,768]{2,1,0:T(8,128)(2,1)S(1)}, bf16[8,64,768]{2,1,0:T(8,128)(2,1)S(1)}, u32[]{:S(2)}, u32[]{:S(2)}) collective-permute-start(bf16[8,64,768]{2,1,0:T(8,128)(2,1)S(1)} %all_to_all.51), channel_id=1, source_target_pairs={{0,1},{1,0},{2,3},{3,2},{4,5},{5,4},{6,7},{7,6},{8,9},{9,8},{10,11... | collective-permute-start | bytes 2359304 | tf_op jit(solution)/shard_map/ppermute | solution.py:21
  35.2 0.8 broadcast_in_dim.22
  36.0 11.1 %all-to-all-start = ((bf16[16,32,512]{2,1,0:T(8,128)(2,1)}), bf16[16,32,512]{2,1,0:T(8,128)(2,1)S(1)}, u32[]{:S(2)}, u32[]{:S(2)}) async-start(bf16[16,32,512]{2,1,0:T(8,128)(2,1)} %broadcast_in_dim.22), calls=%async_computation | async-start | bytes 1048576 | tf_op jit(solution)/shard_map/all_to_all | solution.py:13
  47.1 0.1 select_bitcast_fusion.1
  47.2 0.1 pad_maximum_fusion.1
  47.4 1.0 convolution_convert_fusion
  48.4 1.2 copy.33
  49.6 11.9 %all-to-all-done = bf16[16,32,512]{2,1,0:T(8,128)(2,1)S(1)} async-done(((bf16[16,32,512]{2,1,0:T(8,128)(2,1)}), bf16[16,32,512]{2,1,0:T(8,128)(2,1)S(1)}, u32[]{:S(2)}, u32[]{:S(2)}) %all-to-all-start) | async-done | bytes 524320 | tf_op jit(solution)/shard_map/all_to_all | solution.py:13
  61.5 7.7 %all-to-all-start.2 = ((f16[32,32,512]{2,1,0:T(8,128)(2,1)}), f16[32,32,512]{2,1,0:T(8,128)(2,1)}, u32[]{:S(2)}, u32[]{:S(2)}) async-start(f16[32,32,512]{2,1,0:T(8,128)(2,1)} %bitcast.8), calls=%async_computation.2 | async-start | bytes 2097152 | tf_op jit(solution)/shard_map/all_to_all | solution.py:13
  69.2 4.6 %collective-permute-start.1 = (bf16[1000,512]{1,0:T(8,128)(2,1)S(1)}, bf16[1000,512]{1,0:T(8,128)(2,1)S(1)}, u32[]{:S(2)}, u32[]{:S(2)}) collective-permute-start(bf16[1000,512]{1,0:T(8,128)(2,1)S(1)} %bitcast.121), channel_id=1, source_target_pairs={{0,256},{256,0},{1,257},{257,1},{2,258},{258,2},{3,259},{259,3},{4... | collective-permute-start | bytes 3072008 | tf_op jit(solution)/shard_map/ppermute | solution.py:25
  73.8 33.0 %collective-permute-done.1 = bf16[1000,512]{1,0:T(8,128)(2,1)S(1)} collective-permute-done((bf16[1000,512]{1,0:T(8,128)(2,1)S(1)}, bf16[1000,512]{1,0:T(8,128)(2,1)S(1)}, u32[]{:S(2)}, u32[]{:S(2)}) %collective-permute-start.1) | collective-permute-done | bytes 1024032 | tf_op jit(solution)/shard_map/ppermute | solution.py:25
  106.8 0.1 fusion.11
  106.9 1.5 pad_maximum_fusion
  108.4 2.7 %collective-permute-start.3 = (bf16[2,1000,512]{2,1,0:T(8,128)(2,1)}, bf16[2,1000,512]{2,1,0:T(8,128)(2,1)}, u32[]{:S(2)}, u32[]{:S(2)}) collective-permute-start(bf16[2,1000,512]{2,1,0:T(8,128)(2,1)} %pad_maximum_fusion), channel_id=1, source_target_pairs={{0,1},{1,0},{2,3},{3,2},{4,5},{5,4},{6,7},{7,6},{8,9},{9,8},{10,11... | collective-permute-start | bytes 6144008 | tf_op jit(solution)/shard_map/ppermute | solution.py:21
  111.1 0.2 fusion.3
  111.4 1.4 convert_reduce_fusion
  112.8 0.1 multiply_reduce_fusion.1
  113.0 9.9 %all_to_all.52 = f32[16,1,544]{2,1,0:T(1,128)S(1)} all-to-all(f32[16,1,544]{2,1,0:T(1,128)S(1)} %broadcast_in_dim.24), channel_id=1, replica_groups=mesh['grp'=2,'xl'=2,'z'=8,'y'=8,'core'=2] {'y','core'}, dimensions={0} | all-to-all | bytes 69632 | tf_op jit(solution)/shard_map/all_to_all | solution.py:13
  123.2 0.8 broadcast_in_dim.52
  124.1 6.9 %all-to-all-start.6 = ((bf16[16,32,512]{2,1,0:T(8,128)(2,1)}), bf16[16,32,512]{2,1,0:T(8,128)(2,1)S(1)}, u32[]{:S(2)}, u32[]{:S(2)}) async-start(bf16[16,32,512]{2,1,0:T(8,128)(2,1)} %broadcast_in_dim.52), calls=%async_computation.6 | async-start | bytes 1048576 | tf_op jit(solution)/shard_map/all_to_all | solution.py:13
  130.9 1.2 fusion.5
  132.2 2.6 collective-permute-start.2
  134.8 1.1 collective-permute-done.2
  136.0 1.7 fusion.7
  137.6 1.4 fusion.1
  139.0 5.6 %all-to-all-done.6 = bf16[16,32,512]{2,1,0:T(8,128)(2,1)S(1)} async-done(((bf16[16,32,512]{2,1,0:T(8,128)(2,1)}), bf16[16,32,512]{2,1,0:T(8,128)(2,1)S(1)}, u32[]{:S(2)}, u32[]{:S(2)}) %all-to-all-start.6) | async-done | bytes 524320 | tf_op jit(solution)/shard_map/all_to_all | solution.py:13
  144.6 4.1 %all-to-all-start.4 = ((f16[8,32,1000]{2,1,0:T(8,128)(2,1)}), f16[8,32,1000]{2,1,0:T(8,128)(2,1)}, u32[]{:S(2)}, u32[]{:S(2)}) async-start(f16[8,32,1000]{2,1,0:T(8,128)(2,1)} %fusion.1), calls=%async_computation.4 | async-start | bytes 1048576 | tf_op jit(solution)/shard_map/all_to_all | solution.py:13
  148.7 0.7 select_bitcast_fusion.2
  149.5 4.7 %collective-permute-start.4 = (bf16[8,32,512]{2,1,0:T(8,128)(2,1)}, bf16[8,32,512]{2,1,0:T(8,128)(2,1)}, u32[]{:S(2)}, u32[]{:S(2)}) collective-permute-start(bf16[8,32,512]{2,1,0:T(8,128)(2,1)} %select_bitcast_fusion.2), channel_id=1, source_target_pairs={{0,1},{1,0},{2,3},{3,2},{4,5},{5,4},{6,7},{7,6},{8,9},{9,8},{10,11... | collective-permute-start | bytes 786440 | tf_op jit(solution)/shard_map/ppermute | solution.py:21
  154.1 9.3 %all-to-all-done.4 = f16[8,32,1000]{2,1,0:T(8,128)(2,1)} async-done(((f16[8,32,1000]{2,1,0:T(8,128)(2,1)}), f16[8,32,1000]{2,1,0:T(8,128)(2,1)}, u32[]{:S(2)}, u32[]{:S(2)}) %all-to-all-start.4) | async-done | bytes 512032 | tf_op jit(solution)/shard_map/all_to_all | solution.py:13
  163.5 1.1 convert_reduce_fusion.2
  164.6 0.1 reduce_max.36
  164.7 0.2 exponential_reduce_fusion.1
  165.0 0.6 broadcast_in_dim.25
  165.6 9.9 %all-to-all-start.5 = ((f32[16,2,32]{2,1,0:T(2,128)}), f32[16,2,32]{2,1,0:T(2,128)S(1)}, u32[]{:S(2)}, u32[]{:S(2)}) async-start(f32[16,2,32]{2,1,0:T(2,128)} %broadcast_in_dim.25), calls=%async_computation.5 | async-start | bytes 32768 | tf_op jit(solution)/shard_map/all_to_all | solution.py:13
  175.4 1.8 fusion.6
  177.2 1.3 fusion.2
  178.6 4.2 %all-to-all-done.5 = f32[16,2,32]{2,1,0:T(2,128)S(1)} async-done(((f32[16,2,32]{2,1,0:T(2,128)}), f32[16,2,32]{2,1,0:T(2,128)S(1)}, u32[]{:S(2)}, u32[]{:S(2)}) %all-to-all-start.5) | async-done | bytes 4128 | tf_op jit(solution)/shard_map/all_to_all | solution.py:13
  182.8 3.5 %all-to-all-start.7 = ((f16[8,32,1000]{2,1,0:T(8,128)(2,1)}), f16[8,32,1000]{2,1,0:T(8,128)(2,1)S(1)}, u32[]{:S(2)}, u32[]{:S(2)}) async-start(f16[8,32,1000]{2,1,0:T(8,128)(2,1)} %fusion.2), calls=%async_computation.7 | async-start | bytes 1048576 | tf_op jit(solution)/shard_map/all_to_all | solution.py:13
  186.3 0.7 fusion.21
  187.7 0.7 compare_select_fusion.1
  188.5 0.1 multiply_convert_fusion.2
  188.6 13.5 %all-to-all-done.7 = f16[8,32,1000]{2,1,0:T(8,128)(2,1)S(1)} async-done(((f16[8,32,1000]{2,1,0:T(8,128)(2,1)}), f16[8,32,1000]{2,1,0:T(8,128)(2,1)S(1)}, u32[]{:S(2)}, u32[]{:S(2)}) %all-to-all-start.7) | async-done | bytes 512032 | tf_op jit(solution)/shard_map/all_to_all | solution.py:13
  202.2 0.1 reduce_max.38
  202.3 0.2 exponential_reduce_fusion
  202.7 12.5 %all_to_all.53 = f32[16,1,128]{2,1,0:T(1,128)S(1)} all-to-all(f32[16,1,128]{2,1,0:T(1,128)S(1)} %reshape.118), channel_id=1, replica_groups=mesh['grp'=2,'xl'=2,'z'=8,'y'=8,'core'=2] {'xl','z'}, dimensions={0} | all-to-all | bytes 16384 | tf_op jit(solution)/shard_map/all_to_all | solution.py:13
  215.2 0.5 broadcast.64
  215.7 0.7 reduce.3
  216.6 0.1 multiply_convert_fusion.1
  216.8 1.1 pad_maximum_fusion.2
  217.9 3.7 %all-to-all-start.9 = ((bf16[16,32,1000]{2,1,0:T(8,128)(2,1)}), bf16[16,32,1000]{2,1,0:T(8,128)(2,1)S(1)}, u32[]{:S(2)}, u32[]{:S(2)}) async-start(bf16[16,32,1000]{2,1,0:T(8,128)(2,1)} %pad_maximum_fusion.2), calls=%async_computation.9 | async-start | bytes 2097152 | tf_op jit(solution)/shard_map/all_to_all | solution.py:13
  221.6 4.7 %collective-permute-start.5 = (bf16[16,32,512]{2,1,0:T(8,128)(2,1)S(1)}, bf16[16,32,512]{2,1,0:T(8,128)(2,1)}, u32[]{:S(2)}, u32[]{:S(2)}) collective-permute-start(bf16[16,32,512]{2,1,0:T(8,128)(2,1)S(1)} %all-to-all-done.6), channel_id=1, source_target_pairs={{0,256},{256,0},{1,257},{257,1},{2,258},{258,2},{3,259},{259,3},{4... | collective-permute-start | bytes 1572872 | tf_op jit(solution)/shard_map/ppermute | solution.py:25
  226.3 21.7 %collective-permute-done.5 = bf16[16,32,512]{2,1,0:T(8,128)(2,1)} collective-permute-done((bf16[16,32,512]{2,1,0:T(8,128)(2,1)S(1)}, bf16[16,32,512]{2,1,0:T(8,128)(2,1)}, u32[]{:S(2)}, u32[]{:S(2)}) %collective-permute-start.5) | collective-permute-done | bytes 524320 | tf_op jit(solution)/shard_map/ppermute | solution.py:25
  248.0 1.1 broadcast_select_fusion.3
  249.1 3.6 %collective-permute-start.6 = (bf16[16,32,1000]{2,1,0:T(8,128)(2,1)S(1)}, bf16[16,32,1000]{2,1,0:T(8,128)(2,1)S(1)}, u32[]{:S(2)}, u32[]{:S(2)}) collective-permute-start(bf16[16,32,1000]{2,1,0:T(8,128)(2,1)S(1)} %all-to-all-done.9), channel_id=1, source_target_pairs={{0,1},{1,0},{2,3},{3,2},{4,5},{5,4},{6,7},{7,6},{8,9},{9,8},{10,11... | collective-permute-start | bytes 3072008 | tf_op jit(solution)/shard_map/ppermute | solution.py:21
  252.8 0.7 fusion.20
  253.5 2.8 %collective-permute-start.7 = (f32[32]{0:T(128)S(1)}, f32[32]{0:T(128)S(1)}, u32[]{:S(2)}, u32[]{:S(2)}) collective-permute-start(f32[32]{0:T(128)S(1)} %fusion.20), channel_id=1, source_target_pairs={{0,256},{256,0},{1,257},{257,1},{2,258},{258,2},{3,259},{259,3},{4... | collective-permute-start | bytes 392 | tf_op jit(solution)/shard_map/ppermute | solution.py:25
  256.3 2.9 %collective-permute-done.7 = f32[32]{0:T(128)S(1)} collective-permute-done((f32[32]{0:T(128)S(1)}, f32[32]{0:T(128)S(1)}, u32[]{:S(2)}, u32[]{:S(2)}) %collective-permute-start.7) | collective-permute-done | bytes 160 | tf_op jit(solution)/shard_map/ppermute | solution.py:25
  259.3 0.7 broadcast_select_fusion.9
  259.9 0.6 pad_maximum_fusion.7
  260.5 0.7 fusion.26
  261.3 1.7 fusion
  (49 shorter events, 1.3 us)
Async XLA Ops:
  0.6 46.7 %copy-start = (bf16[3,256,512]{2,1,0:T(8,128)(2,1)S(1)}, bf16[3,256,512]{2,1,0:T(8,128)(2,1)}, u32[]{:S(2)}) copy-start(bf16[3,256,512]{2,1,0:T(8,128)(2,1)} %param.8) | copy-start | bytes 2359300
  0.6 34.5 %copy-start.3 = (bf16[64,512]{1,0:T(8,128)(2,1)S(1)}, bf16[64,512]{1,0:T(8,128)(2,1)}, u32[]{:S(2)}) copy-start(bf16[64,512]{1,0:T(8,128)(2,1)} %param.10) | copy-start | bytes 196612
  29.6 17.4 %collective-permute-start = (bf16[8,64,768]{2,1,0:T(8,128)(2,1)S(1)}, bf16[8,64,768]{2,1,0:T(8,128)(2,1)S(1)}, u32[]{:S(2)}, u32[]{:S(2)}) collective-permute-start(bf16[8,64,768]{2,1,0:T(8,128)(2,1)S(1)} %all_to_all.51), channel_id=1, source_target_pairs={{0,1},{1,0},{2,3},{3,2},{4,5},{5,4},{6,7},{7,6},{8,9},{9,8},{10,11... | collective-permute-start | bytes 2359304 | tf_op jit(solution)/shard_map/ppermute | solution.py:21
  36.0 25.5 %all-to-all-start = ((bf16[16,32,512]{2,1,0:T(8,128)(2,1)}), bf16[16,32,512]{2,1,0:T(8,128)(2,1)S(1)}, u32[]{:S(2)}, u32[]{:S(2)}) async-start(bf16[16,32,512]{2,1,0:T(8,128)(2,1)} %broadcast_in_dim.22), calls=%async_computation | async-start | bytes 1048576 | tf_op jit(solution)/shard_map/all_to_all | solution.py:13
  48.3 20.8 %copy-start.1 = (bf16[1,1000,512]{2,1,0:T(8,128)(2,1)S(1)}, bf16[1,1000,512]{2,1,0:T(8,128)(2,1)}, u32[]{:S(2)}) copy-start(bf16[1,1000,512]{2,1,0:T(8,128)(2,1)} %param.9) | copy-start | bytes 3072004
  61.5 49.6 %copy-start.2 = (bf16[16,32,512]{2,1,0:T(8,128)(2,1)}, bf16[16,32,512]{2,1,0:T(8,128)(2,1)S(1)}, u32[]{:S(2)}) copy-start(bf16[16,32,512]{2,1,0:T(8,128)(2,1)S(1)} %all-to-all-done) | copy-start | bytes 1572868
  61.5 49.9 %all-to-all-start.2 = ((f16[32,32,512]{2,1,0:T(8,128)(2,1)}), f16[32,32,512]{2,1,0:T(8,128)(2,1)}, u32[]{:S(2)}, u32[]{:S(2)}) async-start(f16[32,32,512]{2,1,0:T(8,128)(2,1)} %bitcast.8), calls=%async_computation.2 | async-start | bytes 2097152 | tf_op jit(solution)/shard_map/all_to_all | solution.py:13
  69.2 37.6 %collective-permute-start.1 = (bf16[1000,512]{1,0:T(8,128)(2,1)S(1)}, bf16[1000,512]{1,0:T(8,128)(2,1)S(1)}, u32[]{:S(2)}, u32[]{:S(2)}) collective-permute-start(bf16[1000,512]{1,0:T(8,128)(2,1)S(1)} %bitcast.121), channel_id=1, source_target_pairs={{0,256},{256,0},{1,257},{257,1},{2,258},{258,2},{3,259},{259,3},{4... | collective-permute-start | bytes 3072008 | tf_op jit(solution)/shard_map/ppermute | solution.py:25
  106.9 16.2 %copy-start.5 = (f32[512]{0:T(512)S(1)}, f32[512]{0:T(512)}, u32[]{:S(2)}) copy-start(f32[512]{0:T(512)} %param.12) | copy-start | bytes 6148
  108.4 22.5 %copy-start.4 = (f32[512]{0:T(512)S(1)}, f32[512]{0:T(512)}, u32[]{:S(2)}) copy-start(f32[512]{0:T(512)} %param.11) | copy-start | bytes 6148
  108.4 26.4 %collective-permute-start.3 = (bf16[2,1000,512]{2,1,0:T(8,128)(2,1)}, bf16[2,1000,512]{2,1,0:T(8,128)(2,1)}, u32[]{:S(2)}, u32[]{:S(2)}) collective-permute-start(bf16[2,1000,512]{2,1,0:T(8,128)(2,1)} %pad_maximum_fusion), channel_id=1, source_target_pairs={{0,1},{1,0},{2,3},{3,2},{4,5},{5,4},{6,7},{7,6},{8,9},{9,8},{10,11... | collective-permute-start | bytes 6144008 | tf_op jit(solution)/shard_map/ppermute | solution.py:21
  124.1 20.5 %all-to-all-start.6 = ((bf16[16,32,512]{2,1,0:T(8,128)(2,1)}), bf16[16,32,512]{2,1,0:T(8,128)(2,1)S(1)}, u32[]{:S(2)}, u32[]{:S(2)}) async-start(bf16[16,32,512]{2,1,0:T(8,128)(2,1)} %broadcast_in_dim.52), calls=%async_computation.6 | async-start | bytes 1048576 | tf_op jit(solution)/shard_map/all_to_all | solution.py:13
  132.2 3.7 %collective-permute-start.2 = (bf16[8,32,512]{2,1,0:T(8,128)(2,1)S(1)}, bf16[8,32,512]{2,1,0:T(8,128)(2,1)S(1)}, u32[]{:S(2)}, u32[]{:S(2)}) collective-permute-start(bf16[8,32,512]{2,1,0:T(8,128)(2,1)S(1)} %select_bitcast_fusion.3), channel_id=1, source_target_pairs={{0,1},{1,0},{2,3},{3,2},{4,5},{5,4},{6,7},{7,6},{8,9},{9,8},{10,11... | collective-permute-start | bytes 786440 | tf_op jit(solution)/shard_map/ppermute | solution.py:21
  144.6 18.9 %all-to-all-start.4 = ((f16[8,32,1000]{2,1,0:T(8,128)(2,1)}), f16[8,32,1000]{2,1,0:T(8,128)(2,1)}, u32[]{:S(2)}, u32[]{:S(2)}) async-start(f16[8,32,1000]{2,1,0:T(8,128)(2,1)} %fusion.1), calls=%async_computation.4 | async-start | bytes 1048576 | tf_op jit(solution)/shard_map/all_to_all | solution.py:13
  149.5 26.0 %collective-permute-start.4 = (bf16[8,32,512]{2,1,0:T(8,128)(2,1)}, bf16[8,32,512]{2,1,0:T(8,128)(2,1)}, u32[]{:S(2)}, u32[]{:S(2)}) collective-permute-start(bf16[8,32,512]{2,1,0:T(8,128)(2,1)} %select_bitcast_fusion.2), channel_id=1, source_target_pairs={{0,1},{1,0},{2,3},{3,2},{4,5},{5,4},{6,7},{7,6},{8,9},{9,8},{10,11... | collective-permute-start | bytes 786440 | tf_op jit(solution)/shard_map/ppermute | solution.py:21
  165.6 17.2 %all-to-all-start.5 = ((f32[16,2,32]{2,1,0:T(2,128)}), f32[16,2,32]{2,1,0:T(2,128)S(1)}, u32[]{:S(2)}, u32[]{:S(2)}) async-start(f32[16,2,32]{2,1,0:T(2,128)} %broadcast_in_dim.25), calls=%async_computation.5 | async-start | bytes 32768 | tf_op jit(solution)/shard_map/all_to_all | solution.py:13
  177.2 9.1 %copy-start.6 = (s32[16]{0:T(128)S(1)}, s32[16]{0:T(128)}, u32[]{:S(2)}) copy-start(s32[16]{0:T(128)} %param.13) | copy-start | bytes 196
  182.8 19.4 %all-to-all-start.7 = ((f16[8,32,1000]{2,1,0:T(8,128)(2,1)}), f16[8,32,1000]{2,1,0:T(8,128)(2,1)S(1)}, u32[]{:S(2)}, u32[]{:S(2)}) async-start(f16[8,32,1000]{2,1,0:T(8,128)(2,1)} %fusion.2), calls=%async_computation.7 | async-start | bytes 1048576 | tf_op jit(solution)/shard_map/all_to_all | solution.py:13
  217.9 31.2 %all-to-all-start.9 = ((bf16[16,32,1000]{2,1,0:T(8,128)(2,1)}), bf16[16,32,1000]{2,1,0:T(8,128)(2,1)S(1)}, u32[]{:S(2)}, u32[]{:S(2)}) async-start(bf16[16,32,1000]{2,1,0:T(8,128)(2,1)} %pad_maximum_fusion.2), calls=%async_computation.9 | async-start | bytes 2097152 | tf_op jit(solution)/shard_map/all_to_all | solution.py:13
  221.6 26.4 %collective-permute-start.5 = (bf16[16,32,512]{2,1,0:T(8,128)(2,1)S(1)}, bf16[16,32,512]{2,1,0:T(8,128)(2,1)}, u32[]{:S(2)}, u32[]{:S(2)}) collective-permute-start(bf16[16,32,512]{2,1,0:T(8,128)(2,1)S(1)} %all-to-all-done.6), channel_id=1, source_target_pairs={{0,256},{256,0},{1,257},{257,1},{2,258},{258,2},{3,259},{259,3},{4... | collective-permute-start | bytes 1572872 | tf_op jit(solution)/shard_map/ppermute | solution.py:25
  249.1 12.1 %collective-permute-start.6 = (bf16[16,32,1000]{2,1,0:T(8,128)(2,1)S(1)}, bf16[16,32,1000]{2,1,0:T(8,128)(2,1)S(1)}, u32[]{:S(2)}, u32[]{:S(2)}) collective-permute-start(bf16[16,32,1000]{2,1,0:T(8,128)(2,1)S(1)} %all-to-all-done.9), channel_id=1, source_target_pairs={{0,1},{1,0},{2,3},{3,2},{4,5},{5,4},{6,7},{7,6},{8,9},{9,8},{10,11... | collective-permute-start | bytes 3072008 | tf_op jit(solution)/shard_map/ppermute | solution.py:21
  253.5 5.8 %collective-permute-start.7 = (f32[32]{0:T(128)S(1)}, f32[32]{0:T(128)S(1)}, u32[]{:S(2)}, u32[]{:S(2)}) collective-permute-start(f32[32]{0:T(128)S(1)} %fusion.20), channel_id=1, source_target_pairs={{0,256},{256,0},{1,257},{257,1},{2,258},{258,2},{3,259},{259,3},{4... | collective-permute-start | bytes 392 | tf_op jit(solution)/shard_map/ppermute | solution.py:25

commit v2 on v1

--- a/solution.py
+++ b/solution.py
@@ -49,8 +49,7 @@
     )
     core_heads = from_other_core(both_heads)
 
-    hidden_part = jnp.where(is_target, final_hidden[:part], final_hidden[part:])
-    hidden_rows = copied(hidden_part, SLABS).astype(f32)
+    hidden_part = jnp.where(is_target, final_hidden[:part], final_hidden[part:]).astype(f32)
 
     block = captured.transpose(1, 0, 2).reshape(slab, layers * features)
     mine = copied(block, "y")
@@ -65,68 +64,66 @@
     received = exchanged(pieces.reshape(-1, part, columns), BLOCKS)
     united = jnp.sum(received.astype(f32), axis=0)
 
-    squares = jnp.concatenate(
-        [
-            jnp.sum(united * united, axis=1),
-            jnp.sum(hidden_rows * hidden_rows, axis=2).reshape(-1),
-        ]
+    squares = jnp.stack(
+        [jnp.sum(hidden_part * hidden_part, axis=1), jnp.sum(united * united, axis=1)]
     )
     square_sums = jnp.sum(copied(squares, COLUMNS), axis=0)
     scales = lax.rsqrt(square_sums / model_width + EPSILON)
-    draft_part = (united * scales[:part, None] * draft_gain[None, :]).astype(bf16)
-    draft_rows = copied(draft_part, SLABS)
-    hidden_scale = scales[part:].reshape(n_slabs, part, 1)
-    target_rows = (hidden_rows * hidden_scale * target_gain[None, None, :]).astype(bf16)
+    target_part = (hidden_part * scales[0][:, None] * target_gain[None, :]).astype(bf16)
+    draft_part = (united * scales[1][:, None] * draft_gain[None, :]).astype(bf16)
+    both_rows = copied(jnp.stack([target_part, draft_part]), SLABS)
+    draft_rows = both_rows[:, 1]
+    other_rows = from_other_group(draft_rows)
 
-    def logits_of(rows, which):
-        by_core = rows.reshape(n_y, 2, part, columns)
-        kept = jnp.where(is_first, by_core[:, 0], by_core[:, 1])
-        given = jnp.where(is_first, by_core[:, 1], by_core[:, 0])
-        taken = from_other_core(given)
-        sums = jnp.einsum(
-            "ytd,vd->ytv", kept, both_heads[which], preferred_element_type=f32
-        ) + jnp.einsum("ytd,vd->ytv", taken, core_heads[which], preferred_element_type=f32)
-        return jnp.sum(exchanged(sums.astype(half), "y").astype(f32), axis=0)
+    by_core = both_rows.reshape(n_y, 2, 2, part, columns)
+    kept = jnp.where(is_first, by_core[:, 0], by_core[:, 1])
+    given = jnp.where(is_first, by_core[:, 1], by_core[:, 0])
+    taken = from_other_core(given)
 
-    def row_stats(logits):
-        top = jnp.max(logits, axis=1)
-        return top, jnp.sum(jnp.exp(logits - top[:, None]), axis=1)
+    def partial_logits(which):
+        return (
+            jnp.einsum(
+                "ytd,vd->ytv", kept[:, which], both_heads[which], preferred_element_type=f32
+            )
+            + jnp.einsum(
+                "ytd,vd->ytv", taken[:, which], core_heads[which], preferred_element_type=f32
+            )
+        ).astype(half)
 
-    def combined(tops, totals):
-        top = jnp.max(tops, axis=0)
-        return top, jnp.sum(totals * jnp.exp(tops - top[None]), axis=0)
+    partials = jnp.stack([partial_logits(0), partial_logits(1)], axis=1)
+    partials = exchanged(partials, "y")
+    logits = jnp.sum(partials.astype(f32), axis=0)
 
-    target_logits = logits_of(target_rows, 0)
-    target_stats = copied(jnp.stack(row_stats(target_logits)), SLABS)
-    target_top, target_total = combined(target_stats[:, 0], target_stats[:, 1])
-    target_probs = jnp.exp(target_logits - target_top[:, None]) / target_total[:, None]
-
-    draft_logits = logits_of(draft_rows, 1)
-    top, total = row_stats(draft_logits)
-    crossed = jnp.sum(target_probs * (draft_logits - top[:, None]), axis=1)
-    mass = jnp.sum(target_probs, axis=1)
-    stats = copied(jnp.stack([top, total, crossed, mass]), SLABS)
-    draft_top, draft_total = combined(stats[:, 0], stats[:, 1])
-    draft_probs = jnp.exp(draft_logits - draft_top[:, None]) / draft_total[:, None]
-    shift = stats[:, 0] - draft_top[None] - jnp.log(draft_total)[None]
-    cross_term = jnp.sum(stats[:, 2] + stats[:, 3] * shift, axis=0)
+    local_top = jnp.max(logits, axis=2)
+    shifted = logits - local_top[:, :, None]
+    raised = jnp.exp(shifted)
+    local_total = jnp.sum(raised, axis=2)
+    crossed = jnp.sum(raised[0] * shifted[1], axis=1)
+    stats = copied(jnp.concatenate([local_top, local_total, crossed[None]]), BLOCKS)
+    stats = stats.reshape(2, n_slabs, 5, part)
+    tops, totals, crosses = stats[:, :, 0:2], stats[:, :, 2:4], stats[:, :, 4]
+    top = jnp.max(tops, axis=1)
+    total = jnp.sum(totals * jnp.exp(tops - top[:, None]), axis=1)
+    block_factor = jnp.exp(tops[:, :, 0] - top[:, None, 0]) / total[:, None, 0]
+    draft_shift = tops[:, :, 1] - top[:, None, 1] - jnp.log(total)[:, None, 1]
+    cross_term = jnp.sum(
+        block_factor * (crosses + totals[:, :, 0] * draft_shift), axis=1
+    ).reshape(-1)
+    own_top = jnp.where(is_target, top[0], top[1])
+    own_total = jnp.where(is_target, total[0], total[1])
+    probs = jnp.exp(logits - own_top[:, :, None]) / own_total[:, :, None]
 
     slab_index = lax.axis_index("y") * 2 + core
-    position = group * part + lax.iota(jnp.int32, part)
     valid_len = jnp.sum(
         jnp.where(lax.iota(jnp.int32, lengths.shape[0]) == slab_index, lengths, 0)
     )
-    valid_mask = (position < valid_len).astype(f32)
+    valid_mask = (lax.iota(jnp.int32, slab) < valid_len).astype(f32)
     valid_total = jnp.sum(lengths).astype(f32)
-    own_loss = -valid_mask * cross_term
-    other_loss = from_other_group(own_loss)
-    token_loss = jnp.concatenate(
-        [jnp.where(is_target, own_loss, other_loss), jnp.where(is_target, other_loss, own_loss)]
-    )
+    token_loss = -valid_mask * cross_term
 
-    weights = (valid_mask / valid_total)[:, None]
-    weighted = (target_probs * weights).astype(bf16)
-    delta = ((draft_probs - target_probs) * weights).astype(bf16)
+    weights = jnp.where(is_target, valid_mask[:part], valid_mask[part:]) / valid_total
+    weighted = (probs[0] * weights[:, None]).astype(bf16)
+    delta = ((probs[1] - probs[0]) * weights[:, None]).astype(bf16)
     outgoing = jnp.concatenate(
         [
             jnp.broadcast_to(weighted, (n_y, part, vocab)),
@@ -136,7 +133,6 @@
     gathered = exchanged(outgoing, ("grp", "y"))
     core_gathered = from_other_core(gathered)
 
-    other_rows = from_other_group(draft_rows)
     all_rows = jnp.stack(
         [
             jnp.where(is_target, draft_rows, other_rows),

time: 264 us -> 236 us (0.89)
  blocking collectives: 50.3 us -> 27.9 us
  starting transfers between devices: 77.9 us -> 62.4 us
  waiting for transfers between devices: 103 us -> 115 us
  other arithmetic: 14.3 us -> 9.74 us
    all_to_all x3 -> x1, blocking collectives: 50.3 us -> 27.9 us  [exchanged(): return lax.all_to_all(tiles, axes, split_axis=0, concat_axis=0, tiled=True)]
    all_to_all x7 -> x6, waiting for transfers between devices: 44.5 us -> 65.9 us  [exchanged(): return lax.all_to_all(tiles, axes, split_axis=0, concat_axis=0, tiled=True)]
    ppermute x3 -> x2, waiting for transfers between devices: 57.7 us -> 44.6 us  [from_other_group(): return lax.ppermute(shard, 'grp', [(0, 1), (1, 0)])]
    all_to_all x7 -> x6, starting transfers between devices: 46.8 us -> 40.1 us  [exchanged(): return lax.all_to_all(tiles, axes, split_axis=0, concat_axis=0, tiled=True)]
    ppermute x3 -> x2, starting transfers between devices: 12 us -> 7.12 us  [from_other_group(): return lax.ppermute(shard, 'grp', [(0, 1), (1, 0)])]
    ppermute x5 -> x4, starting transfers between devices: 19.1 us -> 15.2 us  [from_other_core(): return lax.ppermute(shard, 'core', [(0, 1), (1, 0)])]
    ppermute x5 -> x4, waiting for transfers between devices: 1.14 us -> 4.68 us  [from_other_core(): return lax.ppermute(shard, 'core', [(0, 1), (1, 0)])]
  transfers between devices with their start and end apart: 15 -> 12, of which waited for: 9 -> 10; matrix products, arithmetic and copies ran while one was open for 9% -> 4% of each run, Pallas kernels for 0% -> 0%
where the time goes in v2:
time: 236 us; the launch traced here: 235 us
  waiting for transfers between devices  115 us (49%)
  starting transfers between devices  62.4 us (26%)
  blocking collectives  27.9 us (12%)
  matrix products  10.2 us (4%)
  other arithmetic  9.74 us (4%)
  local copies, waits for them, and re-layouts  7.88 us (3%)
    all_to_all x6, waiting for transfers between devices, exchanged(): return lax.all_to_all(tiles, axes, split_axis=0, concat_axis=0, tiled=True)  65.9 us
    ppermute x2, waiting for transfers between devices, from_other_group(): return lax.ppermute(shard, 'grp', [(0, 1), (1, 0)])  44.6 us
    all_to_all x6, starting transfers between devices, exchanged(): return lax.all_to_all(tiles, axes, split_axis=0, concat_axis=0, tiled=True)  40.1 us
    all_to_all x1, blocking collectives, exchanged(): return lax.all_to_all(tiles, axes, split_axis=0, concat_axis=0, tiled=True)  27.9 us
    ppermute x4, starting transfers between devices, from_other_core(): return lax.ppermute(shard, 'core', [(0, 1), (1, 0)])  15.2 us
    ppermute x2, starting transfers between devices, from_other_group(): return lax.ppermute(shard, 'grp', [(0, 1), (1, 0)])  7.12 us
  transfers between devices with their start and end apart: 12, of which 10 were waited for; matrix products, arithmetic and copies ran while one was open for 4% of the time, Pallas kernels for 0%

profile of v2, /device:TPU:1, one launch (start us, length us, event | category | flops | bytes accessed | tf_op | source)
XLA Modules:
  0.0 235.1 jit_solution(6369475115027605794)
XLA Ops:
  0.6 1.0 copy.64
  1.7 27.9 %all_to_all.35 = bf16[8,64,768]{2,1,0:T(8,128)(2,1)S(1)} all-to-all(bf16[8,64,768]{2,1,0:T(8,128)(2,1)S(1)} %broadcast_in_dim.36), channel_id=1, replica_groups=mesh['grp'=2,'xl'=2,'z'=8,'y'=8,'core'=2] {'y'}, dimensions={0} | all-to-all | bytes 1572864 | tf_op jit(solution)/shard_map/all_to_all | solution.py:13
  29.6 5.5 %collective-permute-start = (bf16[8,64,768]{2,1,0:T(8,128)(2,1)S(1)}, bf16[8,64,768]{2,1,0:T(8,128)(2,1)S(1)}, u32[]{:S(2)}, u32[]{:S(2)}) collective-permute-start(bf16[8,64,768]{2,1,0:T(8,128)(2,1)S(1)} %all_to_all.35), channel_id=1, source_target_pairs={{0,1},{1,0},{2,3},{3,2},{4,5},{5,4},{6,7},{7,6},{8,9},{9,8},{10,11... | collective-permute-start | bytes 2359304 | tf_op jit(solution)/shard_map/ppermute | solution.py:21
  35.1 1.9 collective-permute-done
  37.0 0.1 select_bitcast_fusion.1
  37.1 0.1 pad_maximum_fusion.1
  37.3 1.0 convolution_convert_fusion
  38.2 1.2 copy.43
  39.5 13.0 %all-to-all-start.1 = ((f16[32,32,512]{2,1,0:T(8,128)(2,1)}), f16[32,32,512]{2,1,0:T(8,128)(2,1)S(1)}, u32[]{:S(2)}, u32[]{:S(2)}) async-start(f16[32,32,512]{2,1,0:T(8,128)(2,1)} %bitcast.139), calls=%async_computation.1 | async-start | bytes 2097152 | tf_op jit(solution)/shard_map/all_to_all | solution.py:13
  52.5 0.1 fusion.16
  52.6 25.1 %all-to-all-done.1 = f16[32,32,512]{2,1,0:T(8,128)(2,1)S(1)} async-done(((f16[32,32,512]{2,1,0:T(8,128)(2,1)}), f16[32,32,512]{2,1,0:T(8,128)(2,1)S(1)}, u32[]{:S(2)}, u32[]{:S(2)}) %all-to-all-start.1) | async-done | bytes 1048608 | tf_op jit(solution)/shard_map/all_to_all | solution.py:13
  77.7 0.2 convert_reduce_fusion.1
  77.9 0.1 multiply_reduce_fusion
  78.0 0.6 broadcast_in_dim.37
  78.6 7.6 %all-to-all-start.2 = ((f32[16,2,32]{2,1,0:T(2,128)}), f32[16,2,32]{2,1,0:T(2,128)S(1)}, u32[]{:S(2)}, u32[]{:S(2)}) async-start(f32[16,2,32]{2,1,0:T(2,128)} %broadcast_in_dim.37), calls=%async_computation.2 | async-start | bytes 32768 | tf_op jit(solution)/shard_map/all_to_all | solution.py:13
  86.3 2.4 %collective-permute-start.1 = (bf16[1000,512]{1,0:T(8,128)(2,1)S(1)}, bf16[1000,512]{1,0:T(8,128)(2,1)}, u32[]{:S(2)}, u32[]{:S(2)}) collective-permute-start(bf16[1000,512]{1,0:T(8,128)(2,1)S(1)} %bitcast.137), channel_id=1, source_target_pairs={{0,256},{256,0},{1,257},{257,1},{2,258},{258,2},{3,259},{259,3},{4... | collective-permute-start | bytes 3072008 | tf_op jit(solution)/shard_map/ppermute | solution.py:25
  88.7 4.9 %all-to-all-done.2 = f32[16,2,32]{2,1,0:T(2,128)S(1)} async-done(((f32[16,2,32]{2,1,0:T(2,128)}), f32[16,2,32]{2,1,0:T(2,128)S(1)}, u32[]{:S(2)}, u32[]{:S(2)}) %all-to-all-start.2) | async-done | bytes 4128 | tf_op jit(solution)/shard_map/all_to_all | solution.py:13
  93.7 0.1 fusion.21
  93.8 0.1 fusion.20
  93.8 1.1 broadcast_in_dim.38
  94.9 3.7 %all-to-all-start.3 = ((bf16[16,2,32,512]{3,2,1,0:T(8,128)(2,1)}), bf16[16,2,32,512]{3,2,1,0:T(8,128)(2,1)S(1)}, u32[]{:S(2)}, u32[]{:S(2)}) async-start(bf16[16,2,32,512]{3,2,1,0:T(8,128)(2,1)} %broadcast_in_dim.38), calls=%async_computation.3 | async-start | bytes 2097152 | tf_op jit(solution)/shard_map/all_to_all | solution.py:13
  98.6 23.9 %collective-permute-done.1 = bf16[1000,512]{1,0:T(8,128)(2,1)} collective-permute-done((bf16[1000,512]{1,0:T(8,128)(2,1)S(1)}, bf16[1000,512]{1,0:T(8,128)(2,1)}, u32[]{:S(2)}, u32[]{:S(2)}) %collective-permute-start.1) | collective-permute-done | bytes 1024032 | tf_op jit(solution)/shard_map/ppermute | solution.py:25
  122.5 1.4 fusion.10
  123.9 1.5 pad_maximum_fusion
  125.4 4.0 %collective-permute-start.3 = (bf16[2,1000,512]{2,1,0:T(8,128)(2,1)}, bf16[2,1000,512]{2,1,0:T(8,128)(2,1)}, u32[]{:S(2)}, u32[]{:S(2)}) collective-permute-start(bf16[2,1000,512]{2,1,0:T(8,128)(2,1)} %pad_maximum_fusion), channel_id=1, source_target_pairs={{0,1},{1,0},{2,3},{3,2},{4,5},{5,4},{6,7},{7,6},{8,9},{9,8},{10,11... | collective-permute-start | bytes 6144008 | tf_op jit(solution)/shard_map/ppermute | solution.py:21
  129.4 0.1 fusion.31
  129.5 0.1 select_bitcast_fusion.3
  129.6 1.9 collective-permute-start.2
  131.5 1.9 collective-permute-done.3
  133.4 0.6 collective-permute-done.2
  134.0 1.7 fusion.5
  135.7 1.7 fusion.6
  137.4 1.7 fusion.3
  139.1 0.5 fusion.4
  139.6 0.3 pad_maximum_fusion.2
  140.0 1.3 copy.47
  141.3 7.3 %all-to-all-start.4 = ((f16[8,2,32,1000]{3,2,1,0:T(8,128)(2,1)}), f16[8,2,32,1000]{3,2,1,0:T(8,128)(2,1)S(1)}, u32[]{:S(2)}, u32[]{:S(2)}) async-start(f16[8,2,32,1000]{3,2,1,0:T(8,128)(2,1)} %copy.47), calls=%async_computation.4 | async-start | bytes 2097152 | tf_op jit(solution)/shard_map/all_to_all | solution.py:13
  148.6 0.7 fusion.30
  150.0 0.7 compare_convert_fusion
  150.7 27.2 %all-to-all-done.4 = f16[8,2,32,1000]{3,2,1,0:T(8,128)(2,1)S(1)} async-done(((f16[8,2,32,1000]{3,2,1,0:T(8,128)(2,1)}), f16[8,2,32,1000]{3,2,1,0:T(8,128)(2,1)S(1)}, u32[]{:S(2)}, u32[]{:S(2)}) %all-to-all-start.4) | async-done | bytes 1024032 | tf_op jit(solution)/shard_map/all_to_all | solution.py:13
  177.8 0.2 convert_reduce_fusion
  178.1 0.1 reduce_max.18
  178.2 0.2 exponential_reduce_fusion
  178.4 0.1 fusion.15
  178.6 0.7 reshape.153
  179.3 4.8 %all-to-all-start.5 = ((f32[32,1,160]{2,1,0:T(1,128)}), f32[32,1,160]{2,1,0:T(1,128)S(1)}, u32[]{:S(2)}, u32[]{:S(2)}) async-start(f32[32,1,160]{2,1,0:T(1,128)} %reshape.153), calls=%async_computation.5 | async-start | bytes 65536 | tf_op jit(solution)/shard_map/all_to_all | solution.py:13
  184.2 8.7 %all-to-all-done.5 = f32[32,1,160]{2,1,0:T(1,128)S(1)} async-done(((f32[32,1,160]{2,1,0:T(1,128)}), f32[32,1,160]{2,1,0:T(1,128)S(1)}, u32[]{:S(2)}, u32[]{:S(2)}) %all-to-all-start.5) | async-done | bytes 20512 | tf_op jit(solution)/shard_map/all_to_all | solution.py:13
  192.9 0.5 broadcast.66
  193.4 0.7 reduce.1
  194.1 0.1 reshape.154
  194.3 0.1 exponential_divide_fusion
  194.5 0.1 multiply_convert_fusion.1
  194.7 1.1 pad_maximum_fusion.3
  195.8 3.7 %all-to-all-start.6 = ((bf16[16,32,1000]{2,1,0:T(8,128)(2,1)}), bf16[16,32,1000]{2,1,0:T(8,128)(2,1)S(1)}, u32[]{:S(2)}, u32[]{:S(2)}) async-start(bf16[16,32,1000]{2,1,0:T(8,128)(2,1)} %pad_maximum_fusion.3), calls=%async_computation.6 | async-start | bytes 2097152 | tf_op jit(solution)/shard_map/all_to_all | solution.py:13
  199.4 0.8 slice_bitcast_fusion.4
  200.3 4.7 %collective-permute-start.4 = (bf16[16,32,512]{2,1,0:T(8,128)(2,1)}, bf16[16,32,512]{2,1,0:T(8,128)(2,1)S(1)}, u32[]{:S(2)}, u32[]{:S(2)}) collective-permute-start(bf16[16,32,512]{2,1,0:T(8,128)(2,1)} %slice_bitcast_fusion.4), channel_id=1, source_target_pairs={{0,256},{256,0},{1,257},{257,1},{2,258},{258,2},{3,259},{259,3},{4... | collective-permute-start | bytes 1572872 | tf_op jit(solution)/shard_map/ppermute | solution.py:25
  205.0 20.7 %collective-permute-done.4 = bf16[16,32,512]{2,1,0:T(8,128)(2,1)S(1)} collective-permute-done((bf16[16,32,512]{2,1,0:T(8,128)(2,1)}, bf16[16,32,512]{2,1,0:T(8,128)(2,1)S(1)}, u32[]{:S(2)}, u32[]{:S(2)}) %collective-permute-start.4) | collective-permute-done | bytes 524320 | tf_op jit(solution)/shard_map/ppermute | solution.py:25
  225.8 0.1 broadcast_select_fusion.4
  225.9 3.8 %collective-permute-start.5 = (bf16[16,32,1000]{2,1,0:T(8,128)(2,1)S(1)}, bf16[16,32,1000]{2,1,0:T(8,128)(2,1)}, u32[]{:S(2)}, u32[]{:S(2)}) collective-permute-start(bf16[16,32,1000]{2,1,0:T(8,128)(2,1)S(1)} %all-to-all-done.6), channel_id=1, source_target_pairs={{0,1},{1,0},{2,3},{3,2},{4,5},{5,4},{6,7},{7,6},{8,9},{9,8},{10,11... | collective-permute-start | bytes 3072008 | tf_op jit(solution)/shard_map/ppermute | solution.py:21
  229.8 0.1 reshape.148
  229.9 1.2 negate_multiply_fusion
  231.1 0.7 fusion.35
  231.9 0.3 collective-permute-done.5
  232.1 2.9 %fusion = bf16[1,1000,512]{2,1,0:T(8,128)(2,1)} fusion(f32[1000,512]{1,0:T(8,128)S(1)} %fusion.35, bf16[512,1000]{1,0:T(8,128)(2,1)} %bitcast.44, bf16[512,512]{1,0:T(8,128)(2,1)S(1)} %bitcast.140, f32[]{:T(128)S(6)} %select_n.124), kind=kOutput, calls=%fused_computation.8 | convolution fusion | flops 525824000 | bytes 4620292 | tf_op jit(solution)/shard_map/tv,td->vd/dot_general | solution.py:146
  (34 shorter events, 0.6 us)
Async XLA Ops:
  0.6 36.6 %copy-start = (bf16[3,256,512]{2,1,0:T(8,128)(2,1)S(1)}, bf16[3,256,512]{2,1,0:T(8,128)(2,1)}, u32[]{:S(2)}) copy-start(bf16[3,256,512]{2,1,0:T(8,128)(2,1)} %param.8) | copy-start | bytes 2359300
  29.6 7.4 %collective-permute-start = (bf16[8,64,768]{2,1,0:T(8,128)(2,1)S(1)}, bf16[8,64,768]{2,1,0:T(8,128)(2,1)S(1)}, u32[]{:S(2)}, u32[]{:S(2)}) collective-permute-start(bf16[8,64,768]{2,1,0:T(8,128)(2,1)S(1)} %all_to_all.35), channel_id=1, source_target_pairs={{0,1},{1,0},{2,3},{3,2},{4,5},{5,4},{6,7},{7,6},{8,9},{9,8},{10,11... | collective-permute-start | bytes 2359304 | tf_op jit(solution)/shard_map/ppermute | solution.py:21
  38.2 14.3 %copy-start.2 = (bf16[64,512]{1,0:T(8,128)(2,1)S(1)}, bf16[64,512]{1,0:T(8,128)(2,1)}, u32[]{:S(2)}) copy-start(bf16[64,512]{1,0:T(8,128)(2,1)} %param.10) | copy-start | bytes 196612
  39.5 46.8 %copy-start.1 = (bf16[1,1000,512]{2,1,0:T(8,128)(2,1)S(1)}, bf16[1,1000,512]{2,1,0:T(8,128)(2,1)}, u32[]{:S(2)}) copy-start(bf16[1,1000,512]{2,1,0:T(8,128)(2,1)} %param.9) | copy-start | bytes 3072004
  39.5 54.2 %copy-start.3 = (f32[512]{0:T(512)S(1)}, f32[512]{0:T(512)}, u32[]{:S(2)}) copy-start(f32[512]{0:T(512)} %param.11) | copy-start | bytes 6148
  39.5 54.3 %copy-start.4 = (f32[512]{0:T(512)S(1)}, f32[512]{0:T(512)}, u32[]{:S(2)}) copy-start(f32[512]{0:T(512)} %param.12) | copy-start | bytes 6148
  39.5 38.3 %all-to-all-start.1 = ((f16[32,32,512]{2,1,0:T(8,128)(2,1)}), f16[32,32,512]{2,1,0:T(8,128)(2,1)S(1)}, u32[]{:S(2)}, u32[]{:S(2)}) async-start(f16[32,32,512]{2,1,0:T(8,128)(2,1)} %bitcast.139), calls=%async_computation.1 | async-start | bytes 2097152 | tf_op jit(solution)/shard_map/all_to_all | solution.py:13
  78.6 15.0 %all-to-all-start.2 = ((f32[16,2,32]{2,1,0:T(2,128)}), f32[16,2,32]{2,1,0:T(2,128)S(1)}, u32[]{:S(2)}, u32[]{:S(2)}) async-start(f32[16,2,32]{2,1,0:T(2,128)} %broadcast_in_dim.37), calls=%async_computation.2 | async-start | bytes 32768 | tf_op jit(solution)/shard_map/all_to_all | solution.py:13
  86.3 36.2 %collective-permute-start.1 = (bf16[1000,512]{1,0:T(8,128)(2,1)S(1)}, bf16[1000,512]{1,0:T(8,128)(2,1)}, u32[]{:S(2)}, u32[]{:S(2)}) collective-permute-start(bf16[1000,512]{1,0:T(8,128)(2,1)S(1)} %bitcast.137), channel_id=1, source_target_pairs={{0,256},{256,0},{1,257},{257,1},{2,258},{258,2},{3,259},{259,3},{4... | collective-permute-start | bytes 3072008 | tf_op jit(solution)/shard_map/ppermute | solution.py:25
  94.9 34.4 %all-to-all-start.3 = ((bf16[16,2,32,512]{3,2,1,0:T(8,128)(2,1)}), bf16[16,2,32,512]{3,2,1,0:T(8,128)(2,1)S(1)}, u32[]{:S(2)}, u32[]{:S(2)}) async-start(bf16[16,2,32,512]{3,2,1,0:T(8,128)(2,1)} %broadcast_in_dim.38), calls=%async_computation.3 | async-start | bytes 2097152 | tf_op jit(solution)/shard_map/all_to_all | solution.py:13
  125.4 8.1 %collective-permute-start.3 = (bf16[2,1000,512]{2,1,0:T(8,128)(2,1)}, bf16[2,1000,512]{2,1,0:T(8,128)(2,1)}, u32[]{:S(2)}, u32[]{:S(2)}) collective-permute-start(bf16[2,1000,512]{2,1,0:T(8,128)(2,1)} %pad_maximum_fusion), channel_id=1, source_target_pairs={{0,1},{1,0},{2,3},{3,2},{4,5},{5,4},{6,7},{7,6},{8,9},{9,8},{10,11... | collective-permute-start | bytes 6144008 | tf_op jit(solution)/shard_map/ppermute | solution.py:21
  129.6 4.5 %collective-permute-start.2 = (bf16[8,2,32,512]{3,2,0,1:T(8,128)(2,1)S(1)}, bf16[8,2,32,512]{3,2,0,1:T(8,128)(2,1)S(1)}, u32[]{:S(2)}, u32[]{:S(2)}) collective-permute-start(bf16[8,2,32,512]{3,2,0,1:T(8,128)(2,1)S(1)} %get-tuple-element.15), channel_id=1, source_target_pairs={{0,1},{1,0},{2,3},{3,2},{4,5},{5,4},{6,7},{7,6},{8,9},{9,8},{10,11... | collective-permute-start | bytes 1572872 | tf_op jit(solution)/shard_map/ppermute | solution.py:21
  139.9 8.7 %copy-start.5 = (s32[16]{0:T(128)S(1)}, s32[16]{0:T(128)}, u32[]{:S(2)}) copy-start(s32[16]{0:T(128)} %param.13) | copy-start | bytes 196
  141.3 36.6 %all-to-all-start.4 = ((f16[8,2,32,1000]{3,2,1,0:T(8,128)(2,1)}), f16[8,2,32,1000]{3,2,1,0:T(8,128)(2,1)S(1)}, u32[]{:S(2)}, u32[]{:S(2)}) async-start(f16[8,2,32,1000]{3,2,1,0:T(8,128)(2,1)} %copy.47), calls=%async_computation.4 | async-start | bytes 2097152 | tf_op jit(solution)/shard_map/all_to_all | solution.py:13
  179.3 13.6 %all-to-all-start.5 = ((f32[32,1,160]{2,1,0:T(1,128)}), f32[32,1,160]{2,1,0:T(1,128)S(1)}, u32[]{:S(2)}, u32[]{:S(2)}) async-start(f32[32,1,160]{2,1,0:T(1,128)} %reshape.153), calls=%async_computation.5 | async-start | bytes 65536 | tf_op jit(solution)/shard_map/all_to_all | solution.py:13
  195.8 30.2 %all-to-all-start.6 = ((bf16[16,32,1000]{2,1,0:T(8,128)(2,1)}), bf16[16,32,1000]{2,1,0:T(8,128)(2,1)S(1)}, u32[]{:S(2)}, u32[]{:S(2)}) async-start(bf16[16,32,1000]{2,1,0:T(8,128)(2,1)} %pad_maximum_fusion.3), calls=%async_computation.6 | async-start | bytes 2097152 | tf_op jit(solution)/shard_map/all_to_all | solution.py:13
  200.3 25.5 %collective-permute-start.4 = (bf16[16,32,512]{2,1,0:T(8,128)(2,1)}, bf16[16,32,512]{2,1,0:T(8,128)(2,1)S(1)}, u32[]{:S(2)}, u32[]{:S(2)}) collective-permute-start(bf16[16,32,512]{2,1,0:T(8,128)(2,1)} %slice_bitcast_fusion.4), channel_id=1, source_target_pairs={{0,256},{256,0},{1,257},{257,1},{2,258},{258,2},{3,259},{259,3},{4... | collective-permute-start | bytes 1572872 | tf_op jit(solution)/shard_map/ppermute | solution.py:25
  225.9 6.2 %collective-permute-start.5 = (bf16[16,32,1000]{2,1,0:T(8,128)(2,1)S(1)}, bf16[16,32,1000]{2,1,0:T(8,128)(2,1)}, u32[]{:S(2)}, u32[]{:S(2)}) collective-permute-start(bf16[16,32,1000]{2,1,0:T(8,128)(2,1)S(1)} %all-to-all-done.6), channel_id=1, source_target_pairs={{0,1},{1,0},{2,3},{3,2},{4,5},{5,4},{6,7},{7,6},{8,9},{9,8},{10,11... | collective-permute-start | bytes 3072008 | tf_op jit(solution)/shard_map/ppermute | solution.py:21

commit v3 on v2

--- a/solution.py
+++ b/solution.py
@@ -25,6 +25,11 @@
     return lax.ppermute(shard, "grp", [(0, 1), (1, 0)])
 
 
+def along_x(shard, step):
+    n = lax.axis_size(("grp", "xl"))
+    return lax.ppermute(shard, ("grp", "xl"), [(i, (i + step) % n) for i in range(n)])
+
+
 def per_device(captured, unite_weight, heads, final_hidden, target_gain, draft_gain, lengths):
     f32, bf16, half = jnp.float32, jnp.bfloat16, jnp.float16
     columns = final_hidden.shape[1]
@@ -40,7 +45,12 @@
     vocab = heads.shape[1]
 
     own_heads = heads[0]
-    other_heads = from_other_group(own_heads)
+    first_half, second_half = own_heads[: vocab // 2], own_heads[vocab // 2 :]
+    first_half = along_x(first_half, 1)
+    second_half = along_x(second_half, -1)
+    first_half = along_x(first_half, 1)
+    second_half = along_x(second_half, -1)
+    other_heads = jnp.concatenate([first_half, second_half])
     both_heads = jnp.stack(
         [
             jnp.where(is_target, own_heads, other_heads),
@@ -80,17 +90,17 @@
     given = jnp.where(is_first, by_core[:, 1], by_core[:, 0])
     taken = from_other_core(given)
 
-    def partial_logits(which):
-        return (
-            jnp.einsum(
-                "ytd,vd->ytv", kept[:, which], both_heads[which], preferred_element_type=f32
-            )
-            + jnp.einsum(
-                "ytd,vd->ytv", taken[:, which], core_heads[which], preferred_element_type=f32
-            )
-        ).astype(half)
+    def share_of(rows, head):
+        return jnp.einsum("ytd,vd->ytv", rows, head, preferred_element_type=f32)
 
-    partials = jnp.stack([partial_logits(0), partial_logits(1)], axis=1)
+    own_share = [share_of(kept[:, w], both_heads[w]) for w in range(2)]
+    partials = jnp.stack(
+        [
+            (own_share[w] + share_of(taken[:, w], core_heads[w])).astype(half)
+            for w in range(2)
+        ],
+        axis=1,
+    )
     partials = exchanged(partials, "y")
     logits = jnp.sum(partials.astype(f32), axis=0)
 
@@ -99,19 +109,21 @@
     raised = jnp.exp(shifted)
     local_total = jnp.sum(raised, axis=2)
     crossed = jnp.sum(raised[0] * shifted[1], axis=1)
-    stats = copied(jnp.concatenate([local_top, local_total, crossed[None]]), BLOCKS)
-    stats = stats.reshape(2, n_slabs, 5, part)
-    tops, totals, crosses = stats[:, :, 0:2], stats[:, :, 2:4], stats[:, :, 4]
-    top = jnp.max(tops, axis=1)
-    total = jnp.sum(totals * jnp.exp(tops - top[:, None]), axis=1)
-    block_factor = jnp.exp(tops[:, :, 0] - top[:, None, 0]) / total[:, None, 0]
-    draft_shift = tops[:, :, 1] - top[:, None, 1] - jnp.log(total)[:, None, 1]
-    cross_term = jnp.sum(
-        block_factor * (crosses + totals[:, :, 0] * draft_shift), axis=1
-    ).reshape(-1)
-    own_top = jnp.where(is_target, top[0], top[1])
-    own_total = jnp.where(is_target, total[0], total[1])
-    probs = jnp.exp(logits - own_top[:, :, None]) / own_total[:, :, None]
+    stats = copied(jnp.concatenate([local_top, local_total, crossed[None]]), SLABS)
+    tops, totals, crosses = stats[:, 0:2], stats[:, 2:4], stats[:, 4]
+    top = jnp.max(tops, axis=0)
+    total = jnp.sum(totals * jnp.exp(tops - top[None]), axis=0)
+    probs = jnp.exp(logits - top[:, :, None]) / total[:, :, None]
+    block_factor = jnp.exp(tops[:, 0] - top[None, 0]) / total[None, 0]
+    draft_shift = tops[:, 1] - top[None, 1] - jnp.log(total)[None, 1]
+    cross_term = jnp.sum(block_factor * (crosses + totals[:, 0] * draft_shift), axis=0)
+    other_term = from_other_group(cross_term)
+    cross_term = jnp.concatenate(
+        [
+            jnp.where(is_target, cross_term, other_term),
+            jnp.where(is_target, other_term, cross_term),
+        ]
+    )
 
     slab_index = lax.axis_index("y") * 2 + core
     valid_len = jnp.sum(
@@ -150,7 +162,8 @@
             preferred_element_type=f32,
         )
 
-    summed = gradient(gathered, own_side) + gradient(core_gathered, core_side)
+    own_sums = gradient(gathered, own_side)
+    summed = own_sums + gradient(core_gathered, core_side)
     sign_factor = jnp.where(is_target, -1.0, 1.0).astype(f32)
     grad_terms = (sign_factor * summed).astype(bf16)[None]
     return (grad_terms, token_loss)

time: 236 us -> 240 us (1.017)
  starting transfers between devices: 62.4 us -> 75.2 us
  waiting for transfers between devices: 115 us -> 107 us
  other arithmetic: 9.74 us -> 12.8 us
  matrix products: 10.2 us -> 7.69 us
    ppermute x2, waiting for transfers between devices: 44.6 us -> 23.3 us  [from_other_group(): return lax.ppermute(shard, 'grp', [(0, 1), (1, 0)])]
    ppermute x0 -> x4, waiting for transfers between devices: none -> 19.6 us  [along_x(): lax.ppermute(shard, ('grp', 'xl'), [(i, (i + step) % n) for i in range(n)])]
    ppermute x0 -> x4, starting transfers between devices: none -> 13 us  [along_x(): lax.ppermute(shard, ('grp', 'xl'), [(i, (i + step) % n) for i in range(n)])]
    all_to_all x6, waiting for transfers between devices: 65.9 us -> 60.5 us  [exchanged(): return lax.all_to_all(tiles, axes, split_axis=0, concat_axis=0, tiled=True)]
  transfers between devices with their start and end apart: 12 -> 16, of which waited for: 10 -> 12; matrix products, arithmetic and copies ran while one was open for 4% -> 5% of each run, Pallas kernels for 0% -> 0%
where the time goes in v3:
time: 240 us; the launch traced here: 239 us
  waiting for transfers between devices  107 us (45%)
  starting transfers between devices  75.2 us (31%)
  blocking collectives  27.9 us (12%)
  other arithmetic  12.8 us (5%)
  matrix products  7.69 us (3%)
  local copies, waits for them, and re-layouts  7.05 us (3%)
    all_to_all x6, waiting for transfers between devices, exchanged(): return lax.all_to_all(tiles, axes, split_axis=0, concat_axis=0, tiled=True)  60.5 us
    all_to_all x6, starting transfers between devices, exchanged(): return lax.all_to_all(tiles, axes, split_axis=0, concat_axis=0, tiled=True)  38.8 us
    all_to_all x1, blocking collectives, exchanged(): return lax.all_to_all(tiles, axes, split_axis=0, concat_axis=0, tiled=True)  27.9 us
    ppermute x2, waiting for transfers between devices, from_other_group(): return lax.ppermute(shard, 'grp', [(0, 1), (1, 0)])  23.3 us
    ppermute x4, waiting for transfers between devices, along_x(): lax.ppermute(shard, ('grp', 'xl'), [(i, (i + step) % n) for i in range(n)])  19.6 us
    ppermute x4, starting transfers between devices, from_other_core(): return lax.ppermute(shard, 'core', [(0, 1), (1, 0)])  15.8 us
    ppermute x4, starting transfers between devices, along_x(): lax.ppermute(shard, ('grp', 'xl'), [(i, (i + step) % n) for i in range(n)])  13 us
    ppermute x2, starting transfers between devices, from_other_group(): return lax.ppermute(shard, 'grp', [(0, 1), (1, 0)])  7.64 us
  transfers between devices with their start and end apart: 16, of which 12 were waited for; matrix products, arithmetic and copies ran while one was open for 5% of the time, Pallas kernels for 0%

profile of v3, /device:TPU:1, one launch (start us, length us, event | category | flops | bytes accessed | tf_op | source)
XLA Modules:
  0.0 239.1 jit_solution(9159154182247425817)
XLA Ops:
  0.6 1.0 copy.55
  1.7 27.9 %all_to_all.35 = bf16[8,64,768]{2,1,0:T(8,128)(2,1)S(1)} all-to-all(bf16[8,64,768]{2,1,0:T(8,128)(2,1)S(1)} %broadcast_in_dim.36), channel_id=1, replica_groups=mesh['grp'=2,'xl'=2,'z'=8,'y'=8,'core'=2] {'y'}, dimensions={0} | all-to-all | bytes 1572864 | tf_op jit(solution)/shard_map/all_to_all | solution.py:13
  29.6 5.5 %collective-permute-start = (bf16[8,64,768]{2,1,0:T(8,128)(2,1)S(1)}, bf16[8,64,768]{2,1,0:T(8,128)(2,1)S(1)}, u32[]{:S(2)}, u32[]{:S(2)}) collective-permute-start(bf16[8,64,768]{2,1,0:T(8,128)(2,1)S(1)} %all_to_all.35), channel_id=1, source_target_pairs={{0,1},{1,0},{2,3},{3,2},{4,5},{5,4},{6,7},{7,6},{8,9},{9,8},{10,11... | collective-permute-start | bytes 2359304 | tf_op jit(solution)/shard_map/ppermute | solution.py:21
  35.1 1.9 collective-permute-done
  37.0 0.1 select_bitcast_fusion.1
  37.1 0.1 pad_maximum_fusion.1
  37.3 1.0 convolution_convert_fusion
  38.2 1.2 copy.37
  39.5 13.0 %all-to-all-start.1 = ((f16[32,32,512]{2,1,0:T(8,128)(2,1)}), f16[32,32,512]{2,1,0:T(8,128)(2,1)S(1)}, u32[]{:S(2)}, u32[]{:S(2)}) async-start(f16[32,32,512]{2,1,0:T(8,128)(2,1)} %bitcast.9), calls=%async_computation.1 | async-start | bytes 2097152 | tf_op jit(solution)/shard_map/all_to_all | solution.py:13
  52.5 0.1 fusion.14
  52.6 25.1 %all-to-all-done.1 = f16[32,32,512]{2,1,0:T(8,128)(2,1)S(1)} async-done(((f16[32,32,512]{2,1,0:T(8,128)(2,1)}), f16[32,32,512]{2,1,0:T(8,128)(2,1)S(1)}, u32[]{:S(2)}, u32[]{:S(2)}) %all-to-all-start.1) | async-done | bytes 1048608 | tf_op jit(solution)/shard_map/all_to_all | solution.py:13
  77.7 0.2 convert_reduce_fusion.1
  77.9 0.1 multiply_reduce_fusion
  78.0 0.6 broadcast_in_dim.37
  78.6 7.6 %all-to-all-start.2 = ((f32[16,2,32]{2,1,0:T(2,128)}), f32[16,2,32]{2,1,0:T(2,128)S(1)}, u32[]{:S(2)}, u32[]{:S(2)}) async-start(f32[16,2,32]{2,1,0:T(2,128)} %broadcast_in_dim.37), calls=%async_computation.2 | async-start | bytes 32768 | tf_op jit(solution)/shard_map/all_to_all | solution.py:13
  86.2 0.1 slice_bitcast_fusion.6
  86.4 1.9 collective-permute-start.1
  88.3 4.6 %collective-permute-start.3 = (bf16[500,512]{1,0:T(8,128)(2,1)S(1)}, bf16[500,512]{1,0:T(8,128)(2,1)}, u32[]{:S(2)}, u32[]{:S(2)}) collective-permute-start(bf16[500,512]{1,0:T(8,128)(2,1)S(1)} %get-tuple-element.19), channel_id=1, source_target_pairs={{0,384},{128,0},{256,128},{384,256},{1,385},{129,1},{257,129},{385... | collective-permute-start | bytes 1536008 | tf_op jit(solution)/shard_map/ppermute | solution.py:30
  92.9 0.7 all-to-all-done.2
  93.8 1.1 broadcast_in_dim.38
  94.9 3.7 %all-to-all-start.3 = ((bf16[16,2,32,512]{3,2,1,0:T(8,128)(2,1)}), bf16[16,2,32,512]{3,2,1,0:T(8,128)(2,1)S(1)}, u32[]{:S(2)}, u32[]{:S(2)}) async-start(bf16[16,2,32,512]{3,2,1,0:T(8,128)(2,1)} %broadcast_in_dim.38), calls=%async_computation.3 | async-start | bytes 2097152 | tf_op jit(solution)/shard_map/all_to_all | solution.py:13
  98.6 4.1 %collective-permute-done.1 = bf16[500,512]{1,0:T(8,128)(2,1)} collective-permute-done((bf16[500,512]{1,0:T(8,128)(2,1)S(1)}, bf16[500,512]{1,0:T(8,128)(2,1)}, u32[]{:S(2)}, u32[]{:S(2)}) %collective-permute-start.1) | collective-permute-done | bytes 512032 | tf_op jit(solution)/shard_map/ppermute | solution.py:30
  102.7 1.9 collective-permute-start.2
  104.6 4.6 %collective-permute-start.4 = (bf16[500,512]{1,0:T(8,128)(2,1)}, bf16[500,512]{1,0:T(8,128)(2,1)S(1)}, u32[]{:S(2)}, u32[]{:S(2)}) collective-permute-start(bf16[500,512]{1,0:T(8,128)(2,1)} %collective-permute-done.3), channel_id=1, source_target_pairs={{0,384},{128,0},{256,128},{384,256},{1,385},{129,1},{257,129},{385... | collective-permute-start | bytes 1536008 | tf_op jit(solution)/shard_map/ppermute | solution.py:30
  109.2 13.7 %collective-permute-done.2 = bf16[500,512]{1,0:T(8,128)(2,1)S(1)} collective-permute-done((bf16[500,512]{1,0:T(8,128)(2,1)}, bf16[500,512]{1,0:T(8,128)(2,1)S(1)}, u32[]{:S(2)}, u32[]{:S(2)}) %collective-permute-start.2) | collective-permute-done | bytes 512032 | tf_op jit(solution)/shard_map/ppermute | solution.py:30
  122.9 1.8 collective-permute-done.4
  124.7 1.6 broadcast_select_fusion.1
  126.4 1.7 pad_maximum_fusion
  128.0 4.6 %collective-permute-start.6 = (bf16[2,1000,512]{2,1,0:T(8,128)(2,1)}, bf16[2,1000,512]{2,1,0:T(8,128)(2,1)}, u32[]{:S(2)}, u32[]{:S(2)}) collective-permute-start(bf16[2,1000,512]{2,1,0:T(8,128)(2,1)} %pad_maximum_fusion), channel_id=1, source_target_pairs={{0,1},{1,0},{2,3},{3,2},{4,5},{5,4},{6,7},{7,6},{8,9},{9,8},{10,11... | collective-permute-start | bytes 6144008 | tf_op jit(solution)/shard_map/ppermute | solution.py:21
  132.7 0.1 fusion.24
  132.9 2.1 collective-permute-start.5
  134.9 0.5 fusion.5
  135.4 0.5 fusion.7
  135.9 0.8 collective-permute-done.6
  136.7 0.6 collective-permute-done.5
  137.3 1.7 fusion.3
  139.0 1.7 fusion.4
  140.7 0.3 pad_maximum_fusion.2
  141.0 1.3 copy.41
  142.3 6.3 %all-to-all-start.4 = ((f16[8,2,32,1000]{3,2,1,0:T(8,128)(2,1)}), f16[8,2,32,1000]{3,2,1,0:T(8,128)(2,1)S(1)}, u32[]{:S(2)}, u32[]{:S(2)}) async-start(f16[8,2,32,1000]{3,2,1,0:T(8,128)(2,1)} %copy.41), calls=%async_computation.4 | async-start | bytes 2097152 | tf_op jit(solution)/shard_map/all_to_all | solution.py:13
  148.6 0.6 fusion.23
  149.9 0.5 compare_convert_fusion
  150.4 27.4 %all-to-all-done.4 = f16[8,2,32,1000]{3,2,1,0:T(8,128)(2,1)S(1)} async-done(((f16[8,2,32,1000]{3,2,1,0:T(8,128)(2,1)}), f16[8,2,32,1000]{3,2,1,0:T(8,128)(2,1)S(1)}, u32[]{:S(2)}, u32[]{:S(2)}) %all-to-all-start.4) | async-done | bytes 1024032 | tf_op jit(solution)/shard_map/all_to_all | solution.py:13
  177.8 0.2 convert_reduce_fusion
  178.2 0.2 exponential_reduce_fusion
  178.4 0.1 fusion.13
  178.6 0.7 reshape.137
  179.3 4.6 %all-to-all-start.5 = ((f32[16,1,160]{2,1,0:T(1,128)}), f32[16,1,160]{2,1,0:T(1,128)S(1)}, u32[]{:S(2)}, u32[]{:S(2)}) async-start(f32[16,1,160]{2,1,0:T(1,128)} %reshape.137), calls=%async_computation.5 | async-start | bytes 32768 | tf_op jit(solution)/shard_map/all_to_all | solution.py:13
  183.9 7.3 %all-to-all-done.5 = f32[16,1,160]{2,1,0:T(1,128)S(1)} async-done(((f32[16,1,160]{2,1,0:T(1,128)}), f32[16,1,160]{2,1,0:T(1,128)S(1)}, u32[]{:S(2)}, u32[]{:S(2)}) %all-to-all-start.5) | async-done | bytes 10272 | tf_op jit(solution)/shard_map/all_to_all | solution.py:13
  191.2 0.5 broadcast.61
  191.7 0.7 reduce.1
  192.5 0.1 exponential_divide_fusion
  192.9 1.1 pad_maximum_fusion.3
  194.0 3.7 %all-to-all-start.6 = ((bf16[16,32,1000]{2,1,0:T(8,128)(2,1)}), bf16[16,32,1000]{2,1,0:T(8,128)(2,1)S(1)}, u32[]{:S(2)}, u32[]{:S(2)}) async-start(bf16[16,32,1000]{2,1,0:T(8,128)(2,1)} %pad_maximum_fusion.3), calls=%async_computation.6 | async-start | bytes 2097152 | tf_op jit(solution)/shard_map/all_to_all | solution.py:13
  197.7 4.7 %collective-permute-start.7 = (bf16[16,32,512]{2,1,0:T(8,128)(2,1)S(1)}, bf16[16,32,512]{2,1,0:T(8,128)(2,1)}, u32[]{:S(2)}, u32[]{:S(2)}) collective-permute-start(bf16[16,32,512]{2,1,0:T(8,128)(2,1)S(1)} %slice_bitcast_fusion.4), channel_id=1, source_target_pairs={{0,256},{256,0},{1,257},{257,1},{2,258},{258,2},{3,259},{259,3},{4... | collective-permute-start | bytes 1572872 | tf_op jit(solution)/shard_map/ppermute | solution.py:25
  202.4 21.7 %collective-permute-done.7 = bf16[16,32,512]{2,1,0:T(8,128)(2,1)} collective-permute-done((bf16[16,32,512]{2,1,0:T(8,128)(2,1)S(1)}, bf16[16,32,512]{2,1,0:T(8,128)(2,1)}, u32[]{:S(2)}, u32[]{:S(2)}) %collective-permute-start.7) | collective-permute-done | bytes 524320 | tf_op jit(solution)/shard_map/ppermute | solution.py:25
  224.1 1.9 broadcast_select_fusion.3
  226.0 3.6 %collective-permute-start.8 = (bf16[16,32,1000]{2,1,0:T(8,128)(2,1)S(1)}, bf16[16,32,1000]{2,1,0:T(8,128)(2,1)S(1)}, u32[]{:S(2)}, u32[]{:S(2)}) collective-permute-start(bf16[16,32,1000]{2,1,0:T(8,128)(2,1)S(1)} %all-to-all-done.6), channel_id=1, source_target_pairs={{0,1},{1,0},{2,3},{3,2},{4,5},{5,4},{6,7},{7,6},{8,9},{9,8},{10,11... | collective-permute-start | bytes 3072008 | tf_op jit(solution)/shard_map/ppermute | solution.py:21
  229.7 2.9 %collective-permute-start.9 = (f32[32]{0:T(128)S(1)}, f32[32]{0:T(128)S(1)}, u32[]{:S(2)}, u32[]{:S(2)}) collective-permute-start(f32[32]{0:T(128)S(1)} %multiply_reduce_fusion.1), channel_id=1, source_target_pairs={{0,256},{256,0},{1,257},{257,1},{2,258},{258,2},{3,259},{259,3},{4... | collective-permute-start | bytes 392 | tf_op jit(solution)/shard_map/ppermute | solution.py:25
  232.6 1.2 broadcast_select_fusion.4
  233.9 1.6 collective-permute-done.9
  235.5 1.1 maximum_multiply_fusion
  236.6 0.7 fusion.26
  237.4 1.7 fusion
  (47 shorter events, 1.1 us)
Async XLA Ops:
  0.6 36.6 %copy-start = (bf16[3,256,512]{2,1,0:T(8,128)(2,1)S(1)}, bf16[3,256,512]{2,1,0:T(8,128)(2,1)}, u32[]{:S(2)}) copy-start(bf16[3,256,512]{2,1,0:T(8,128)(2,1)} %param.8) | copy-start | bytes 2359300
  29.6 7.4 %collective-permute-start = (bf16[8,64,768]{2,1,0:T(8,128)(2,1)S(1)}, bf16[8,64,768]{2,1,0:T(8,128)(2,1)S(1)}, u32[]{:S(2)}, u32[]{:S(2)}) collective-permute-start(bf16[8,64,768]{2,1,0:T(8,128)(2,1)S(1)} %all_to_all.35), channel_id=1, source_target_pairs={{0,1},{1,0},{2,3},{3,2},{4,5},{5,4},{6,7},{7,6},{8,9},{9,8},{10,11... | collective-permute-start | bytes 2359304 | tf_op jit(solution)/shard_map/ppermute | solution.py:21
  38.2 14.3 %copy-start.4 = (bf16[64,512]{1,0:T(8,128)(2,1)S(1)}, bf16[64,512]{1,0:T(8,128)(2,1)}, u32[]{:S(2)}) copy-start(bf16[64,512]{1,0:T(8,128)(2,1)} %param.10) | copy-start | bytes 196612
  39.5 46.8 %copy-start.3 = (bf16[1,1000,512]{2,1,0:T(8,128)(2,1)S(1)}, bf16[1,1000,512]{2,1,0:T(8,128)(2,1)}, u32[]{:S(2)}) copy-start(bf16[1,1000,512]{2,1,0:T(8,128)(2,1)} %param.9) | copy-start | bytes 3072004
  39.5 38.3 %all-to-all-start.1 = ((f16[32,32,512]{2,1,0:T(8,128)(2,1)}), f16[32,32,512]{2,1,0:T(8,128)(2,1)S(1)}, u32[]{:S(2)}, u32[]{:S(2)}) async-start(f16[32,32,512]{2,1,0:T(8,128)(2,1)} %bitcast.9), calls=%async_computation.1 | async-start | bytes 2097152 | tf_op jit(solution)/shard_map/all_to_all | solution.py:13
  52.5 41.2 %copy-start.5 = (f32[512]{0:T(512)S(1)}, f32[512]{0:T(512)}, u32[]{:S(2)}) copy-start(f32[512]{0:T(512)} %param.11) | copy-start | bytes 6148
  52.5 41.2 %copy-start.6 = (f32[512]{0:T(512)S(1)}, f32[512]{0:T(512)}, u32[]{:S(2)}) copy-start(f32[512]{0:T(512)} %param.12) | copy-start | bytes 6148
  78.6 15.0 %all-to-all-start.2 = ((f32[16,2,32]{2,1,0:T(2,128)}), f32[16,2,32]{2,1,0:T(2,128)S(1)}, u32[]{:S(2)}, u32[]{:S(2)}) async-start(f32[16,2,32]{2,1,0:T(2,128)} %broadcast_in_dim.37), calls=%async_computation.2 | async-start | bytes 32768 | tf_op jit(solution)/shard_map/all_to_all | solution.py:13
  86.4 16.3 %collective-permute-start.1 = (bf16[500,512]{1,0:T(8,128)(2,1)S(1)}, bf16[500,512]{1,0:T(8,128)(2,1)}, u32[]{:S(2)}, u32[]{:S(2)}) collective-permute-start(bf16[500,512]{1,0:T(8,128)(2,1)S(1)} %get-tuple-element.18), channel_id=1, source_target_pairs={{0,128},{128,256},{256,384},{384,0},{1,129},{129,257},{257,385},{3... | collective-permute-start | bytes 1536008 | tf_op jit(solution)/shard_map/ppermute | solution.py:30
  88.3 16.3 %collective-permute-start.3 = (bf16[500,512]{1,0:T(8,128)(2,1)S(1)}, bf16[500,512]{1,0:T(8,128)(2,1)}, u32[]{:S(2)}, u32[]{:S(2)}) collective-permute-start(bf16[500,512]{1,0:T(8,128)(2,1)S(1)} %get-tuple-element.19), channel_id=1, source_target_pairs={{0,384},{128,0},{256,128},{384,256},{1,385},{129,1},{257,129},{385... | collective-permute-start | bytes 1536008 | tf_op jit(solution)/shard_map/ppermute | solution.py:30
  94.9 37.7 %all-to-all-start.3 = ((bf16[16,2,32,512]{3,2,1,0:T(8,128)(2,1)}), bf16[16,2,32,512]{3,2,1,0:T(8,128)(2,1)S(1)}, u32[]{:S(2)}, u32[]{:S(2)}) async-start(bf16[16,2,32,512]{3,2,1,0:T(8,128)(2,1)} %broadcast_in_dim.38), calls=%async_computation.3 | async-start | bytes 2097152 | tf_op jit(solution)/shard_map/all_to_all | solution.py:13
  102.7 20.2 %collective-permute-start.2 = (bf16[500,512]{1,0:T(8,128)(2,1)}, bf16[500,512]{1,0:T(8,128)(2,1)S(1)}, u32[]{:S(2)}, u32[]{:S(2)}) collective-permute-start(bf16[500,512]{1,0:T(8,128)(2,1)} %collective-permute-done.1), channel_id=1, source_target_pairs={{0,128},{128,256},{256,384},{384,0},{1,129},{129,257},{257,385},{3... | collective-permute-start | bytes 1536008 | tf_op jit(solution)/shard_map/ppermute | solution.py:30
  104.6 20.2 %collective-permute-start.4 = (bf16[500,512]{1,0:T(8,128)(2,1)}, bf16[500,512]{1,0:T(8,128)(2,1)S(1)}, u32[]{:S(2)}, u32[]{:S(2)}) collective-permute-start(bf16[500,512]{1,0:T(8,128)(2,1)} %collective-permute-done.3), channel_id=1, source_target_pairs={{0,384},{128,0},{256,128},{384,256},{1,385},{129,1},{257,129},{385... | collective-permute-start | bytes 1536008 | tf_op jit(solution)/shard_map/ppermute | solution.py:30
  126.4 1.7 copy-start.1
  128.0 8.6 %collective-permute-start.6 = (bf16[2,1000,512]{2,1,0:T(8,128)(2,1)}, bf16[2,1000,512]{2,1,0:T(8,128)(2,1)}, u32[]{:S(2)}, u32[]{:S(2)}) collective-permute-start(bf16[2,1000,512]{2,1,0:T(8,128)(2,1)} %pad_maximum_fusion), channel_id=1, source_target_pairs={{0,1},{1,0},{2,3},{3,2},{4,5},{5,4},{6,7},{7,6},{8,9},{9,8},{10,11... | collective-permute-start | bytes 6144008 | tf_op jit(solution)/shard_map/ppermute | solution.py:21
  132.7 2.3 copy-start.2
  132.9 4.4 %collective-permute-start.5 = (bf16[8,2,32,512]{3,2,0,1:T(8,128)(2,1)S(1)}, bf16[8,2,32,512]{3,2,0,1:T(8,128)(2,1)S(1)}, u32[]{:S(2)}, u32[]{:S(2)}) collective-permute-start(bf16[8,2,32,512]{3,2,0,1:T(8,128)(2,1)S(1)} %get-tuple-element.14), channel_id=1, source_target_pairs={{0,1},{1,0},{2,3},{3,2},{4,5},{5,4},{6,7},{7,6},{8,9},{9,8},{10,11... | collective-permute-start | bytes 1572872 | tf_op jit(solution)/shard_map/ppermute | solution.py:21
  141.0 7.6 %copy-start.7 = (s32[16]{0:T(128)S(1)}, s32[16]{0:T(128)}, u32[]{:S(2)}) copy-start(s32[16]{0:T(128)} %param.13) | copy-start | bytes 196
  142.3 35.5 %all-to-all-start.4 = ((f16[8,2,32,1000]{3,2,1,0:T(8,128)(2,1)}), f16[8,2,32,1000]{3,2,1,0:T(8,128)(2,1)S(1)}, u32[]{:S(2)}, u32[]{:S(2)}) async-start(f16[8,2,32,1000]{3,2,1,0:T(8,128)(2,1)} %copy.41), calls=%async_computation.4 | async-start | bytes 2097152 | tf_op jit(solution)/shard_map/all_to_all | solution.py:13
  179.3 11.9 %all-to-all-start.5 = ((f32[16,1,160]{2,1,0:T(1,128)}), f32[16,1,160]{2,1,0:T(1,128)S(1)}, u32[]{:S(2)}, u32[]{:S(2)}) async-start(f32[16,1,160]{2,1,0:T(1,128)} %reshape.137), calls=%async_computation.5 | async-start | bytes 32768 | tf_op jit(solution)/shard_map/all_to_all | solution.py:13
  194.0 32.1 %all-to-all-start.6 = ((bf16[16,32,1000]{2,1,0:T(8,128)(2,1)}), bf16[16,32,1000]{2,1,0:T(8,128)(2,1)S(1)}, u32[]{:S(2)}, u32[]{:S(2)}) async-start(bf16[16,32,1000]{2,1,0:T(8,128)(2,1)} %pad_maximum_fusion.3), calls=%async_computation.6 | async-start | bytes 2097152 | tf_op jit(solution)/shard_map/all_to_all | solution.py:13
  197.7 26.4 %collective-permute-start.7 = (bf16[16,32,512]{2,1,0:T(8,128)(2,1)S(1)}, bf16[16,32,512]{2,1,0:T(8,128)(2,1)}, u32[]{:S(2)}, u32[]{:S(2)}) collective-permute-start(bf16[16,32,512]{2,1,0:T(8,128)(2,1)S(1)} %slice_bitcast_fusion.4), channel_id=1, source_target_pairs={{0,256},{256,0},{1,257},{257,1},{2,258},{258,2},{3,259},{259,3},{4... | collective-permute-start | bytes 1572872 | tf_op jit(solution)/shard_map/ppermute | solution.py:25
  226.0 11.4 %collective-permute-start.8 = (bf16[16,32,1000]{2,1,0:T(8,128)(2,1)S(1)}, bf16[16,32,1000]{2,1,0:T(8,128)(2,1)S(1)}, u32[]{:S(2)}, u32[]{:S(2)}) collective-permute-start(bf16[16,32,1000]{2,1,0:T(8,128)(2,1)S(1)} %all-to-all-done.6), channel_id=1, source_target_pairs={{0,1},{1,0},{2,3},{3,2},{4,5},{5,4},{6,7},{7,6},{8,9},{9,8},{10,11... | collective-permute-start | bytes 3072008 | tf_op jit(solution)/shard_map/ppermute | solution.py:21
  229.7 5.8 %collective-permute-start.9 = (f32[32]{0:T(128)S(1)}, f32[32]{0:T(128)S(1)}, u32[]{:S(2)}, u32[]{:S(2)}) collective-permute-start(f32[32]{0:T(128)S(1)} %multiply_reduce_fusion.1), channel_id=1, source_target_pairs={{0,256},{256,0},{1,257},{257,1},{2,258},{258,2},{3,259},{259,3},{4... | collective-permute-start | bytes 392 | tf_op jit(solution)/shard_map/ppermute | solution.py:25

commit v4 on v3

--- a/solution.py
+++ b/solution.py
@@ -28,6 +28,22 @@
 def along_x(shard, step):
     n = lax.axis_size(("grp", "xl"))
     return lax.ppermute(shard, ("grp", "xl"), [(i, (i + step) % n) for i in range(n)])
+
+
+def doubled(shard):
+    pieces, stride = shard[None], lax.axis_size("z") // 2
+    place = lax.axis_index("z")
+    while stride:
+        pairs = [(i, i ^ stride) for i in range(lax.axis_size("z"))]
+        other = lax.ppermute(pieces, "z", pairs)
+        low = (place & stride) == 0
+        pieces = jnp.stack(
+            [jnp.where(low, pieces, other), jnp.where(low, other, pieces)], axis=1
+        ).reshape(-1, *shard.shape)
+        stride //= 2
+    other = lax.ppermute(pieces, "xl", [(0, 1), (1, 0)])
+    low = lax.axis_index("xl") == 0
+    return jnp.concatenate([jnp.where(low, pieces, other), jnp.where(low, other, pieces)])
 
 
 def per_device(captured, unite_weight, heads, final_hidden, target_gain, draft_gain, lengths):
@@ -59,7 +75,8 @@
     )
     core_heads = from_other_core(both_heads)
 
-    hidden_part = jnp.where(is_target, final_hidden[:part], final_hidden[part:]).astype(f32)
+    hidden_part = jnp.where(is_target, final_hidden[:part], final_hidden[part:])
+    hidden_rows = doubled(hidden_part).astype(f32)
 
     block = captured.transpose(1, 0, 2).reshape(slab, layers * features)
     mine = copied(block, "y")
@@ -74,35 +91,36 @@
     received = exchanged(pieces.reshape(-1, part, columns), BLOCKS)
     united = jnp.sum(received.astype(f32), axis=0)
 
-    squares = jnp.stack(
-        [jnp.sum(hidden_part * hidden_part, axis=1), jnp.sum(united * united, axis=1)]
-    )
-    square_sums = jnp.sum(copied(squares, COLUMNS), axis=0)
-    scales = lax.rsqrt(square_sums / model_width + EPSILON)
-    target_part = (hidden_part * scales[0][:, None] * target_gain[None, :]).astype(bf16)
-    draft_part = (united * scales[1][:, None] * draft_gain[None, :]).astype(bf16)
-    both_rows = copied(jnp.stack([target_part, draft_part]), SLABS)
-    draft_rows = both_rows[:, 1]
+    squares = jnp.concatenate(
+        [jnp.sum(hidden_rows * hidden_rows, axis=2), jnp.sum(united * united, axis=1)[None]]
+    )
+    squares = copied(squares, COLUMNS)
+    scales = lax.rsqrt(jnp.sum(squares, axis=0) / model_width + EPSILON)
+    draft_part = (united * scales[-1][:, None] * draft_gain[None, :]).astype(bf16)
+    draft_rows = copied(draft_part, SLABS)
     other_rows = from_other_group(draft_rows)
-
-    by_core = both_rows.reshape(n_y, 2, 2, part, columns)
-    kept = jnp.where(is_first, by_core[:, 0], by_core[:, 1])
-    given = jnp.where(is_first, by_core[:, 1], by_core[:, 0])
-    taken = from_other_core(given)
+    target_rows = (hidden_rows * scales[:-1][:, :, None] * target_gain).astype(bf16)
+
+    def split_by_core(rows):
+        by_core = rows.reshape(n_y, 2, part, columns)
+        return (
+            jnp.where(is_first, by_core[:, 0], by_core[:, 1]),
+            jnp.where(is_first, by_core[:, 1], by_core[:, 0]),
+        )
 
     def share_of(rows, head):
         return jnp.einsum("ytd,vd->ytv", rows, head, preferred_element_type=f32)
 
-    own_share = [share_of(kept[:, w], both_heads[w]) for w in range(2)]
-    partials = jnp.stack(
-        [
-            (own_share[w] + share_of(taken[:, w], core_heads[w])).astype(half)
-            for w in range(2)
-        ],
-        axis=1,
-    )
+    kept, given = split_by_core(target_rows)
+    taken = from_other_core(given)
+    target_partial = (share_of(kept, both_heads[0]) + share_of(taken, core_heads[0])).astype(half)
+    kept, given = split_by_core(draft_rows)
+    taken = from_other_core(given)
+    own_share = share_of(kept, both_heads[1])
+    draft_partial = (own_share + share_of(taken, core_heads[1])).astype(half)
+    partials = jnp.concatenate([target_partial, draft_partial], axis=1)
     partials = exchanged(partials, "y")
-    logits = jnp.sum(partials.astype(f32), axis=0)
+    logits = jnp.sum(partials.astype(f32), axis=0).reshape(2, part, vocab)
 
     local_top = jnp.max(logits, axis=2)
     shifted = logits - local_top[:, :, None]
@@ -146,10 +164,7 @@
     core_gathered = from_other_core(gathered)
 
     all_rows = jnp.stack(
-        [
-            jnp.where(is_target, draft_rows, other_rows),
-            jnp.where(is_target, other_rows, draft_rows),
-        ]
+        [jnp.where(is_target, draft_rows, other_rows), jnp.where(is_target, other_rows, draft_rows)]
     ).reshape(2, n_y, 2, part, columns)
     own_side = jnp.where(is_first, all_rows[:, :, 0], all_rows[:, :, 1])
     core_side = jnp.where(is_first, all_rows[:, :, 1], all_rows[:, :, 0])

time: 240 us -> 249 us (1.038)
  starting transfers between devices: 75.2 us -> 92.4 us
  waiting for transfers between devices: 107 us -> 93.7 us
  other arithmetic: 12.8 us -> 16.8 us
    ppermute x0 -> x4, waiting for transfers between devices: none -> 19.2 us  [the longest x3 19.2 us: doubled(): other = lax.ppermute(pieces, 'z', pairs)]
    ppermute x4, waiting for transfers between devices: 19.6 us -> 0.79 us  [along_x(): lax.ppermute(shard, ('grp', 'xl'), [(i, (i + step) % n) for i in range(n)])]
    ppermute x0 -> x4, starting transfers between devices: none -> 18.8 us  [the longest x3 16.9 us: doubled(): other = lax.ppermute(pieces, 'z', pairs)]
    all_to_all x6, waiting for transfers between devices: 60.5 us -> 47.6 us  [exchanged(): return lax.all_to_all(tiles, axes, split_axis=0, concat_axis=0, tiled=True)]
    all_to_all x6, starting transfers between devices: 38.8 us -> 29.2 us  [exchanged(): return lax.all_to_all(tiles, axes, split_axis=0, concat_axis=0, tiled=True)]
    ppermute x4 -> x5, starting transfers between devices: 15.8 us -> 24 us  [from_other_core(): return lax.ppermute(shard, 'core', [(0, 1), (1, 0)])]
  transfers between devices with their start and end apart: 16 -> 21, of which waited for: 12 -> 11; matrix products, arithmetic and copies ran while one was open for 5% -> 8% of each run, Pallas kernels for 0% -> 0%
where the time goes in v4:
time: 249 us; the launch traced here: 248 us
  waiting for transfers between devices  93.7 us (38%)
  starting transfers between devices  92.4 us (37%)
  blocking collectives  27.9 us (11%)
  other arithmetic  16.8 us (7%)
  matrix products  7.7 us (3%)
  local copies, waits for them, and re-layouts  7.08 us (3%)
    all_to_all x6, waiting for transfers between devices, exchanged(): return lax.all_to_all(tiles, axes, split_axis=0, concat_axis=0, tiled=True)  47.6 us
    all_to_all x6, starting transfers between devices, exchanged(): return lax.all_to_all(tiles, axes, split_axis=0, concat_axis=0, tiled=True)  29.2 us
    all_to_all x1, blocking collectives, exchanged(): return lax.all_to_all(tiles, axes, split_axis=0, concat_axis=0, tiled=True)  27.9 us
    ppermute x2, waiting for transfers between devices, from_other_group(): return lax.ppermute(shard, 'grp', [(0, 1), (1, 0)])  24.7 us
    ppermute x5, starting transfers between devices, from_other_core(): return lax.ppermute(shard, 'core', [(0, 1), (1, 0)])  24 us
    ppermute x3, waiting for transfers between devices, doubled(): other = lax.ppermute(pieces, 'z', pairs)  19.2 us
    ppermute x3, starting transfers between devices, doubled(): other = lax.ppermute(pieces, 'z', pairs)  16.9 us
    ppermute x4, starting transfers between devices, along_x(): lax.ppermute(shard, ('grp', 'xl'), [(i, (i + step) % n) for i in range(n)])  13 us
  transfers between devices with their start and end apart: 21, of which 11 were waited for; matrix products, arithmetic and copies ran while one was open for 8% of the time, Pallas kernels for 0%

profile of v4, /device:TPU:1, one launch (start us, length us, event | category | flops | bytes accessed | tf_op | source)
XLA Modules:
  0.0 247.6 jit_solution(11347843931158324998)
XLA Ops:
  0.7 1.0 copy.69
  1.7 27.9 %all_to_all.35 = bf16[8,64,768]{2,1,0:T(8,128)(2,1)S(1)} all-to-all(bf16[8,64,768]{2,1,0:T(8,128)(2,1)S(1)} %broadcast_in_dim.44), channel_id=1, replica_groups=mesh['grp'=2,'xl'=2,'z'=8,'y'=8,'core'=2] {'y'}, dimensions={0} | all-to-all | bytes 1572864 | tf_op jit(solution)/shard_map/all_to_all | solution.py:13
  29.6 5.5 %collective-permute-start.4 = (bf16[8,64,768]{2,1,0:T(8,128)(2,1)S(1)}, bf16[8,64,768]{2,1,0:T(8,128)(2,1)S(1)}, u32[]{:S(2)}, u32[]{:S(2)}) collective-permute-start(bf16[8,64,768]{2,1,0:T(8,128)(2,1)S(1)} %all_to_all.35), channel_id=1, source_target_pairs={{0,1},{1,0},{2,3},{3,2},{4,5},{5,4},{6,7},{7,6},{8,9},{9,8},{10,11... | collective-permute-start | bytes 2359304 | tf_op jit(solution)/shard_map/ppermute | solution.py:21
  35.1 10.6 %collective-permute-start = (bf16[1,32,512]{2,1,0:T(8,128)(2,1)S(1)}, bf16[1,32,512]{2,1,0:T(8,128)(2,1)S(1)}, u32[]{:S(2)}, u32[]{:S(2)}) collective-permute-start(bf16[1,32,512]{2,1,0:T(8,128)(2,1)S(1)} %select_bitcast_fusion.10), channel_id=1, source_target_pairs={{0,64},{16,80},{32,96},{48,112},{64,0},{80,16},{96,32},{112,48},{1... | collective-permute-start | bytes 98312 | tf_op jit(solution)/shard_map/ppermute | solution.py:38
  46.1 1.0 convolution_convert_fusion
  47.1 1.3 copy.50
  48.3 7.3 %all-to-all-start.1 = ((f16[32,32,512]{2,1,0:T(8,128)(2,1)}), f16[32,32,512]{2,1,0:T(8,128)(2,1)}, u32[]{:S(2)}, u32[]{:S(2)}) async-start(f16[32,32,512]{2,1,0:T(8,128)(2,1)} %bitcast.20), calls=%async_computation.1 | async-start | bytes 2097152 | tf_op jit(solution)/shard_map/all_to_all | solution.py:13
  55.8 3.1 %collective-permute-start.5 = (bf16[500,512]{1,0:T(8,128)(2,1)S(1)}, bf16[500,512]{1,0:T(8,128)(2,1)S(1)}, u32[]{:S(2)}, u32[]{:S(2)}) collective-permute-start(bf16[500,512]{1,0:T(8,128)(2,1)S(1)} %get-tuple-element.12), channel_id=1, source_target_pairs={{0,128},{128,256},{256,384},{384,0},{1,129},{129,257},{257,385},{3... | collective-permute-start | bytes 1536008 | tf_op jit(solution)/shard_map/ppermute | solution.py:30
  58.8 3.4 %collective-permute-start.7 = (bf16[500,512]{1,0:T(8,128)(2,1)S(1)}, bf16[500,512]{1,0:T(8,128)(2,1)}, u32[]{:S(2)}, u32[]{:S(2)}) collective-permute-start(bf16[500,512]{1,0:T(8,128)(2,1)S(1)} %get-tuple-element.13), channel_id=1, source_target_pairs={{0,384},{128,0},{256,128},{384,256},{1,385},{129,1},{257,129},{385... | collective-permute-start | bytes 1536008 | tf_op jit(solution)/shard_map/ppermute | solution.py:30
  62.3 4.0 %collective-permute-start.1 = (bf16[2,32,512]{2,1,0:T(8,128)(2,1)S(1)}, bf16[2,32,512]{2,1,0:T(8,128)(2,1)S(1)}, u32[]{:S(2)}, u32[]{:S(2)}) collective-permute-start(bf16[2,32,512]{2,1,0:T(8,128)(2,1)S(1)} %maximum_bitcast_fusion), channel_id=1, source_target_pairs={{0,32},{16,48},{32,0},{48,16},{64,96},{80,112},{96,64},{112,80},{1... | collective-permute-start | bytes 196616 | tf_op jit(solution)/shard_map/ppermute | solution.py:38
  66.3 15.5 %collective-permute-done.1 = bf16[2,32,512]{2,1,0:T(8,128)(2,1)S(1)} collective-permute-done((bf16[2,32,512]{2,1,0:T(8,128)(2,1)S(1)}, bf16[2,32,512]{2,1,0:T(8,128)(2,1)S(1)}, u32[]{:S(2)}, u32[]{:S(2)}) %collective-permute-start.1) | collective-permute-done | bytes 65568 | tf_op jit(solution)/shard_map/ppermute | solution.py:38
  81.8 3.1 %collective-permute-start.6 = (bf16[500,512]{1,0:T(8,128)(2,1)S(1)}, bf16[500,512]{1,0:T(8,128)(2,1)S(1)}, u32[]{:S(2)}, u32[]{:S(2)}) collective-permute-start(bf16[500,512]{1,0:T(8,128)(2,1)S(1)} %collective-permute-done.5), channel_id=1, source_target_pairs={{0,128},{128,256},{256,384},{384,0},{1,129},{129,257},{257,385},{3... | collective-permute-start | bytes 1536008 | tf_op jit(solution)/shard_map/ppermute | solution.py:30
  85.0 3.4 %collective-permute-start.8 = (bf16[500,512]{1,0:T(8,128)(2,1)}, bf16[500,512]{1,0:T(8,128)(2,1)S(1)}, u32[]{:S(2)}, u32[]{:S(2)}) collective-permute-start(bf16[500,512]{1,0:T(8,128)(2,1)} %collective-permute-done.7), channel_id=1, source_target_pairs={{0,384},{128,0},{256,128},{384,256},{1,385},{129,1},{257,129},{385... | collective-permute-start | bytes 1536008 | tf_op jit(solution)/shard_map/ppermute | solution.py:30
  88.4 2.3 collective-permute-start.2
  90.7 3.7 %collective-permute-done.2 = bf16[4,32,512]{2,1,0:T(8,128)(2,1)S(1)} collective-permute-done((bf16[4,32,512]{2,1,0:T(8,128)(2,1)S(1)}, bf16[4,32,512]{2,1,0:T(8,128)(2,1)S(1)}, u32[]{:S(2)}, u32[]{:S(2)}) %collective-permute-start.2) | collective-permute-done | bytes 131104 | tf_op jit(solution)/shard_map/ppermute | solution.py:38
  94.5 1.9 collective-permute-start.3
  96.4 0.8 collective-permute-done.8
  97.2 0.8 copy-done.5
  98.0 1.9 broadcast_select_fusion.1
  99.9 1.5 pad_maximum_fusion
  101.4 7.7 %collective-permute-start.10 = (bf16[2,1000,512]{2,1,0:T(8,128)(2,1)}, bf16[2,1000,512]{2,1,0:T(8,128)(2,1)}, u32[]{:S(2)}, u32[]{:S(2)}) collective-permute-start(bf16[2,1000,512]{2,1,0:T(8,128)(2,1)} %pad_maximum_fusion), channel_id=1, source_target_pairs={{0,1},{1,0},{2,3},{3,2},{4,5},{5,4},{6,7},{7,6},{8,9},{9,8},{10,11... | collective-permute-start | bytes 6144008 | tf_op jit(solution)/shard_map/ppermute | solution.py:21
  109.2 0.2 multiply_reduce_fusion
  109.4 1.4 convert_reduce_fusion.1
  110.9 0.5 copy-done.2
  111.4 0.8 reshape.109
  112.2 3.5 %all-to-all-start.2 = ((f32[16,1,544]{2,1,0:T(1,128)}), f32[16,1,544]{2,1,0:T(1,128)S(1)}, u32[]{:S(2)}, u32[]{:S(2)}) async-start(f32[16,1,544]{2,1,0:T(1,128)} %reshape.109), calls=%async_computation.2 | async-start | bytes 81920 | tf_op jit(solution)/shard_map/all_to_all | solution.py:13
  115.7 1.0 maximum_convert_fusion
  116.7 6.4 %all-to-all-done.2 = f32[16,1,544]{2,1,0:T(1,128)S(1)} async-done(((f32[16,1,544]{2,1,0:T(1,128)}), f32[16,1,544]{2,1,0:T(1,128)S(1)}, u32[]{:S(2)}, u32[]{:S(2)}) %all-to-all-start.2) | async-done | bytes 34848 | tf_op jit(solution)/shard_map/all_to_all | solution.py:13
  123.1 0.5 broadcast.25
  123.6 0.7 reduce.3
  124.6 0.8 broadcast_in_dim.47
  125.5 6.5 %all-to-all-start.3 = ((bf16[16,32,512]{2,1,0:T(8,128)(2,1)}), bf16[16,32,512]{2,1,0:T(8,128)(2,1)S(1)}, u32[]{:S(2)}, u32[]{:S(2)}) async-start(bf16[16,32,512]{2,1,0:T(8,128)(2,1)} %broadcast_in_dim.47), calls=%async_computation.3 | async-start | bytes 1048576 | tf_op jit(solution)/shard_map/all_to_all | solution.py:13
  131.9 1.4 fusion.4
  133.4 2.6 %collective-permute-start.9 = (bf16[8,32,512]{2,1,0:T(8,128)(2,1)S(1)}, bf16[8,32,512]{2,1,0:T(8,128)(2,1)S(1)}, u32[]{:S(2)}, u32[]{:S(2)}) collective-permute-start(bf16[8,32,512]{2,1,0:T(8,128)(2,1)S(1)} %select_bitcast_fusion.3), channel_id=1, source_target_pairs={{0,1},{1,0},{2,3},{3,2},{4,5},{5,4},{6,7},{7,6},{8,9},{9,8},{10,11... | collective-permute-start | bytes 786440 | tf_op jit(solution)/shard_map/ppermute | solution.py:21
  136.0 0.5 fusion.7
  136.4 0.7 collective-permute-done.9
  137.1 1.7 fusion.1
  138.8 6.8 %all-to-all-done.3 = bf16[16,32,512]{2,1,0:T(8,128)(2,1)S(1)} async-done(((bf16[16,32,512]{2,1,0:T(8,128)(2,1)}), bf16[16,32,512]{2,1,0:T(8,128)(2,1)S(1)}, u32[]{:S(2)}, u32[]{:S(2)}) %all-to-all-start.3) | async-done | bytes 524320 | tf_op jit(solution)/shard_map/all_to_all | solution.py:13
  145.6 4.7 %collective-permute-start.11 = (bf16[8,32,512]{2,1,0:T(8,128)(2,1)S(1)}, bf16[8,32,512]{2,1,0:T(8,128)(2,1)S(1)}, u32[]{:S(2)}, u32[]{:S(2)}) collective-permute-start(bf16[8,32,512]{2,1,0:T(8,128)(2,1)S(1)} %select_bitcast_fusion.2), channel_id=1, source_target_pairs={{0,1},{1,0},{2,3},{3,2},{4,5},{5,4},{6,7},{7,6},{8,9},{9,8},{10,11... | collective-permute-start | bytes 786440 | tf_op jit(solution)/shard_map/ppermute | solution.py:21
  150.3 0.5 fusion.5
  150.8 0.7 collective-permute-done.11
  151.4 1.7 fusion.2
  153.1 1.3 pad_maximum_fusion.2
  154.4 3.6 %all-to-all-start.4 = ((f16[8,64,1000]{2,1,0:T(8,128)(2,1)}), f16[8,64,1000]{2,1,0:T(8,128)(2,1)S(1)}, u32[]{:S(2)}, u32[]{:S(2)}) async-start(f16[8,64,1000]{2,1,0:T(8,128)(2,1)} %pad_maximum_fusion.2), calls=%async_computation.4 | async-start | bytes 2097152 | tf_op jit(solution)/shard_map/all_to_all | solution.py:13
  158.0 0.7 fusion.25
  159.3 0.6 compare_convert_fusion
  159.9 27.2 %all-to-all-done.4 = f16[8,64,1000]{2,1,0:T(8,128)(2,1)S(1)} async-done(((f16[8,64,1000]{2,1,0:T(8,128)(2,1)}), f16[8,64,1000]{2,1,0:T(8,128)(2,1)S(1)}, u32[]{:S(2)}, u32[]{:S(2)}) %all-to-all-start.4) | async-done | bytes 1024032 | tf_op jit(solution)/shard_map/all_to_all | solution.py:13
  187.2 0.2 convert_reduce_fusion
  187.5 0.2 exponential_reduce_fusion
  188.2 0.7 reshape.111
  188.9 4.5 %all-to-all-start.5 = ((f32[16,1,160]{2,1,0:T(1,128)}), f32[16,1,160]{2,1,0:T(1,128)S(1)}, u32[]{:S(2)}, u32[]{:S(2)}) async-start(f32[16,1,160]{2,1,0:T(1,128)} %reshape.111), calls=%async_computation.5 | async-start | bytes 32768 | tf_op jit(solution)/shard_map/all_to_all | solution.py:13
  193.5 7.3 %all-to-all-done.5 = f32[16,1,160]{2,1,0:T(1,128)S(1)} async-done(((f32[16,1,160]{2,1,0:T(1,128)}), f32[16,1,160]{2,1,0:T(1,128)S(1)}, u32[]{:S(2)}, u32[]{:S(2)}) %all-to-all-start.5) | async-done | bytes 10272 | tf_op jit(solution)/shard_map/all_to_all | solution.py:13
  200.7 0.7 reduce.4
  201.9 1.1 pad_maximum_fusion.3
  203.0 3.9 %all-to-all-start.6 = ((bf16[16,32,1000]{2,1,0:T(8,128)(2,1)}), bf16[16,32,1000]{2,1,0:T(8,128)(2,1)S(1)}, u32[]{:S(2)}, u32[]{:S(2)}) async-start(bf16[16,32,1000]{2,1,0:T(8,128)(2,1)} %pad_maximum_fusion.3), calls=%async_computation.6 | async-start | bytes 2097152 | tf_op jit(solution)/shard_map/all_to_all | solution.py:13
  206.9 4.8 %collective-permute-start.12 = (bf16[16,32,512]{2,1,0:T(8,128)(2,1)S(1)}, bf16[16,32,512]{2,1,0:T(8,128)(2,1)}, u32[]{:S(2)}, u32[]{:S(2)}) collective-permute-start(bf16[16,32,512]{2,1,0:T(8,128)(2,1)S(1)} %all-to-all-done.3), channel_id=1, source_target_pairs={{0,256},{256,0},{1,257},{257,1},{2,258},{258,2},{3,259},{259,3},{4... | collective-permute-start | bytes 1572872 | tf_op jit(solution)/shard_map/ppermute | solution.py:25
  211.6 21.6 %collective-permute-done.12 = bf16[16,32,512]{2,1,0:T(8,128)(2,1)} collective-permute-done((bf16[16,32,512]{2,1,0:T(8,128)(2,1)S(1)}, bf16[16,32,512]{2,1,0:T(8,128)(2,1)}, u32[]{:S(2)}, u32[]{:S(2)}) %collective-permute-start.12) | collective-permute-done | bytes 524320 | tf_op jit(solution)/shard_map/ppermute | solution.py:25
  233.3 1.1 broadcast_select_fusion.3
  234.5 3.6 %collective-permute-start.13 = (bf16[16,32,1000]{2,1,0:T(8,128)(2,1)S(1)}, bf16[16,32,1000]{2,1,0:T(8,128)(2,1)S(1)}, u32[]{:S(2)}, u32[]{:S(2)}) collective-permute-start(bf16[16,32,1000]{2,1,0:T(8,128)(2,1)S(1)} %all-to-all-done.6), channel_id=1, source_target_pairs={{0,1},{1,0},{2,3},{3,2},{4,5},{5,4},{6,7},{7,6},{8,9},{9,8},{10,11... | collective-permute-start | bytes 3072008 | tf_op jit(solution)/shard_map/ppermute | solution.py:21
  238.1 2.7 %collective-permute-start.14 = (f32[32]{0:T(128)S(1)}, f32[32]{0:T(128)S(1)}, u32[]{:S(2)}, u32[]{:S(2)}) collective-permute-start(f32[32]{0:T(128)S(1)} %multiply_reduce_fusion.2), channel_id=1, source_target_pairs={{0,256},{256,0},{1,257},{257,1},{2,258},{258,2},{3,259},{259,3},{4... | collective-permute-start | bytes 392 | tf_op jit(solution)/shard_map/ppermute | solution.py:25
  240.8 3.0 %collective-permute-done.14 = f32[32]{0:T(128)S(1)} collective-permute-done((f32[32]{0:T(128)S(1)}, f32[32]{0:T(128)S(1)}, u32[]{:S(2)}, u32[]{:S(2)}) %collective-permute-start.14) | collective-permute-done | bytes 160 | tf_op jit(solution)/shard_map/ppermute | solution.py:25
  243.9 1.2 maximum_multiply_fusion
  245.1 0.7 fusion.27
  245.9 1.7 fusion
  (75 shorter events, 2.3 us)
Async XLA Ops:
  0.6 45.5 %copy-start = (bf16[3,256,512]{2,1,0:T(8,128)(2,1)S(1)}, bf16[3,256,512]{2,1,0:T(8,128)(2,1)}, u32[]{:S(2)}) copy-start(bf16[3,256,512]{2,1,0:T(8,128)(2,1)} %param.8) | copy-start | bytes 2359300
  0.6 34.5 %copy-start.6 = (bf16[64,512]{1,0:T(8,128)(2,1)S(1)}, bf16[64,512]{1,0:T(8,128)(2,1)}, u32[]{:S(2)}) copy-start(bf16[64,512]{1,0:T(8,128)(2,1)} %param.10) | copy-start | bytes 196612
  29.6 16.2 %collective-permute-start.4 = (bf16[8,64,768]{2,1,0:T(8,128)(2,1)S(1)}, bf16[8,64,768]{2,1,0:T(8,128)(2,1)S(1)}, u32[]{:S(2)}, u32[]{:S(2)}) collective-permute-start(bf16[8,64,768]{2,1,0:T(8,128)(2,1)S(1)} %all_to_all.35), channel_id=1, source_target_pairs={{0,1},{1,0},{2,3},{3,2},{4,5},{5,4},{6,7},{7,6},{8,9},{9,8},{10,11... | collective-permute-start | bytes 2359304 | tf_op jit(solution)/shard_map/ppermute | solution.py:21
  35.1 27.1 %collective-permute-start = (bf16[1,32,512]{2,1,0:T(8,128)(2,1)S(1)}, bf16[1,32,512]{2,1,0:T(8,128)(2,1)S(1)}, u32[]{:S(2)}, u32[]{:S(2)}) collective-permute-start(bf16[1,32,512]{2,1,0:T(8,128)(2,1)S(1)} %select_bitcast_fusion.10), channel_id=1, source_target_pairs={{0,64},{16,80},{32,96},{48,112},{64,0},{80,16},{96,32},{112,48},{1... | collective-permute-start | bytes 98312 | tf_op jit(solution)/shard_map/ppermute | solution.py:38
  47.1 8.5 %copy-start.1 = (bf16[1,1000,512]{2,1,0:T(8,128)(2,1)S(1)}, bf16[1,1000,512]{2,1,0:T(8,128)(2,1)}, u32[]{:S(2)}) copy-start(bf16[1,1000,512]{2,1,0:T(8,128)(2,1)} %param.9) | copy-start | bytes 3072004
  48.3 61.0 %all-to-all-start.1 = ((f16[32,32,512]{2,1,0:T(8,128)(2,1)}), f16[32,32,512]{2,1,0:T(8,128)(2,1)}, u32[]{:S(2)}, u32[]{:S(2)}) async-start(f16[32,32,512]{2,1,0:T(8,128)(2,1)} %bitcast.20), calls=%async_computation.1 | async-start | bytes 2097152 | tf_op jit(solution)/shard_map/all_to_all | solution.py:13
  55.8 26.1 %collective-permute-start.5 = (bf16[500,512]{1,0:T(8,128)(2,1)S(1)}, bf16[500,512]{1,0:T(8,128)(2,1)S(1)}, u32[]{:S(2)}, u32[]{:S(2)}) collective-permute-start(bf16[500,512]{1,0:T(8,128)(2,1)S(1)} %get-tuple-element.12), channel_id=1, source_target_pairs={{0,128},{128,256},{256,384},{384,0},{1,129},{129,257},{257,385},{3... | collective-permute-start | bytes 1536008 | tf_op jit(solution)/shard_map/ppermute | solution.py:30
  58.8 26.1 %collective-permute-start.7 = (bf16[500,512]{1,0:T(8,128)(2,1)S(1)}, bf16[500,512]{1,0:T(8,128)(2,1)}, u32[]{:S(2)}, u32[]{:S(2)}) collective-permute-start(bf16[500,512]{1,0:T(8,128)(2,1)S(1)} %get-tuple-element.13), channel_id=1, source_target_pairs={{0,384},{128,0},{256,128},{384,256},{1,385},{129,1},{257,129},{385... | collective-permute-start | bytes 1536008 | tf_op jit(solution)/shard_map/ppermute | solution.py:30
  62.3 19.5 %collective-permute-start.1 = (bf16[2,32,512]{2,1,0:T(8,128)(2,1)S(1)}, bf16[2,32,512]{2,1,0:T(8,128)(2,1)S(1)}, u32[]{:S(2)}, u32[]{:S(2)}) collective-permute-start(bf16[2,32,512]{2,1,0:T(8,128)(2,1)S(1)} %maximum_bitcast_fusion), channel_id=1, source_target_pairs={{0,32},{16,48},{32,0},{48,16},{64,96},{80,112},{96,64},{112,80},{1... | collective-permute-start | bytes 196616 | tf_op jit(solution)/shard_map/ppermute | solution.py:38
  81.8 14.6 %collective-permute-start.6 = (bf16[500,512]{1,0:T(8,128)(2,1)S(1)}, bf16[500,512]{1,0:T(8,128)(2,1)S(1)}, u32[]{:S(2)}, u32[]{:S(2)}) collective-permute-start(bf16[500,512]{1,0:T(8,128)(2,1)S(1)} %collective-permute-done.5), channel_id=1, source_target_pairs={{0,128},{128,256},{256,384},{384,0},{1,129},{129,257},{257,385},{3... | collective-permute-start | bytes 1536008 | tf_op jit(solution)/shard_map/ppermute | solution.py:30
  85.0 12.2 %collective-permute-start.8 = (bf16[500,512]{1,0:T(8,128)(2,1)}, bf16[500,512]{1,0:T(8,128)(2,1)S(1)}, u32[]{:S(2)}, u32[]{:S(2)}) collective-permute-start(bf16[500,512]{1,0:T(8,128)(2,1)} %collective-permute-done.7), channel_id=1, source_target_pairs={{0,384},{128,0},{256,128},{384,256},{1,385},{129,1},{257,129},{385... | collective-permute-start | bytes 1536008 | tf_op jit(solution)/shard_map/ppermute | solution.py:30
  88.4 6.0 %collective-permute-start.2 = (bf16[4,32,512]{2,1,0:T(8,128)(2,1)S(1)}, bf16[4,32,512]{2,1,0:T(8,128)(2,1)S(1)}, u32[]{:S(2)}, u32[]{:S(2)}) collective-permute-start(bf16[4,32,512]{2,1,0:T(8,128)(2,1)S(1)} %bitcast.162), channel_id=1, source_target_pairs={{0,16},{16,0},{32,48},{48,32},{64,80},{80,64},{96,112},{112,96},{1... | collective-permute-start | bytes 393224 | tf_op jit(solution)/shard_map/ppermute | solution.py:38
  94.5 14.6 %collective-permute-start.3 = (bf16[8,32,512]{2,1,0:T(8,128)(2,1)S(1)}, bf16[8,32,512]{2,1,0:T(8,128)(2,1)S(1)}, u32[]{:S(2)}, u32[]{:S(2)}) collective-permute-start(bf16[8,32,512]{2,1,0:T(8,128)(2,1)S(1)} %bitcast.161), channel_id=1, source_target_pairs={{0,128},{128,0},{1,129},{129,1},{2,130},{130,2},{3,131},{131,3},{4... | collective-permute-start | bytes 786440 | tf_op jit(solution)/shard_map/ppermute | solution.py:44
  96.4 0.8 copy-start.4
  97.2 0.8 copy-start.5
  101.4 35.0 %collective-permute-start.10 = (bf16[2,1000,512]{2,1,0:T(8,128)(2,1)}, bf16[2,1000,512]{2,1,0:T(8,128)(2,1)}, u32[]{:S(2)}, u32[]{:S(2)}) collective-permute-start(bf16[2,1000,512]{2,1,0:T(8,128)(2,1)} %pad_maximum_fusion), channel_id=1, source_target_pairs={{0,1},{1,0},{2,3},{3,2},{4,5},{5,4},{6,7},{7,6},{8,9},{9,8},{10,11... | collective-permute-start | bytes 6144008 | tf_op jit(solution)/shard_map/ppermute | solution.py:21
  110.7 0.6 copy-start.2
  112.1 12.4 %copy-start.3 = (f32[32,512]{1,0:T(8,128)S(1)}, f32[32,512]{1,0:T(8,128)}, u32[]{:S(2)}) copy-start(f32[32,512]{1,0:T(8,128)} %copy-done.2) | copy-start | bytes 196612
  112.2 12.4 %copy-start.8 = (f32[512]{0:T(512)S(1)}, f32[512]{0:T(512)}, u32[]{:S(2)}) copy-start(f32[512]{0:T(512)} %param.12) | copy-start | bytes 6148
  112.2 19.8 %copy-start.7 = (f32[512]{0:T(512)S(1)}, f32[512]{0:T(512)}, u32[]{:S(2)}) copy-start(f32[512]{0:T(512)} %param.11) | copy-start | bytes 6148
  112.2 10.9 %all-to-all-start.2 = ((f32[16,1,544]{2,1,0:T(1,128)}), f32[16,1,544]{2,1,0:T(1,128)S(1)}, u32[]{:S(2)}, u32[]{:S(2)}) async-start(f32[16,1,544]{2,1,0:T(1,128)} %reshape.109), calls=%async_computation.2 | async-start | bytes 81920 | tf_op jit(solution)/shard_map/all_to_all | solution.py:13
  125.5 20.1 %all-to-all-start.3 = ((bf16[16,32,512]{2,1,0:T(8,128)(2,1)}), bf16[16,32,512]{2,1,0:T(8,128)(2,1)S(1)}, u32[]{:S(2)}, u32[]{:S(2)}) async-start(bf16[16,32,512]{2,1,0:T(8,128)(2,1)} %broadcast_in_dim.47), calls=%async_computation.3 | async-start | bytes 1048576 | tf_op jit(solution)/shard_map/all_to_all | solution.py:13
  133.4 3.7 %collective-permute-start.9 = (bf16[8,32,512]{2,1,0:T(8,128)(2,1)S(1)}, bf16[8,32,512]{2,1,0:T(8,128)(2,1)S(1)}, u32[]{:S(2)}, u32[]{:S(2)}) collective-permute-start(bf16[8,32,512]{2,1,0:T(8,128)(2,1)S(1)} %select_bitcast_fusion.3), channel_id=1, source_target_pairs={{0,1},{1,0},{2,3},{3,2},{4,5},{5,4},{6,7},{7,6},{8,9},{9,8},{10,11... | collective-permute-start | bytes 786440 | tf_op jit(solution)/shard_map/ppermute | solution.py:21
  145.6 5.8 %collective-permute-start.11 = (bf16[8,32,512]{2,1,0:T(8,128)(2,1)S(1)}, bf16[8,32,512]{2,1,0:T(8,128)(2,1)S(1)}, u32[]{:S(2)}, u32[]{:S(2)}) collective-permute-start(bf16[8,32,512]{2,1,0:T(8,128)(2,1)S(1)} %select_bitcast_fusion.2), channel_id=1, source_target_pairs={{0,1},{1,0},{2,3},{3,2},{4,5},{5,4},{6,7},{7,6},{8,9},{9,8},{10,11... | collective-permute-start | bytes 786440 | tf_op jit(solution)/shard_map/ppermute | solution.py:21
  153.1 4.9 %copy-start.9 = (s32[16]{0:T(128)S(1)}, s32[16]{0:T(128)}, u32[]{:S(2)}) copy-start(s32[16]{0:T(128)} %param.13) | copy-start | bytes 196
  154.4 32.8 %all-to-all-start.4 = ((f16[8,64,1000]{2,1,0:T(8,128)(2,1)}), f16[8,64,1000]{2,1,0:T(8,128)(2,1)S(1)}, u32[]{:S(2)}, u32[]{:S(2)}) async-start(f16[8,64,1000]{2,1,0:T(8,128)(2,1)} %pad_maximum_fusion.2), calls=%async_computation.4 | async-start | bytes 2097152 | tf_op jit(solution)/shard_map/all_to_all | solution.py:13
  188.9 11.9 %all-to-all-start.5 = ((f32[16,1,160]{2,1,0:T(1,128)}), f32[16,1,160]{2,1,0:T(1,128)S(1)}, u32[]{:S(2)}, u32[]{:S(2)}) async-start(f32[16,1,160]{2,1,0:T(1,128)} %reshape.111), calls=%async_computation.5 | async-start | bytes 32768 | tf_op jit(solution)/shard_map/all_to_all | solution.py:13
  203.0 31.5 %all-to-all-start.6 = ((bf16[16,32,1000]{2,1,0:T(8,128)(2,1)}), bf16[16,32,1000]{2,1,0:T(8,128)(2,1)S(1)}, u32[]{:S(2)}, u32[]{:S(2)}) async-start(bf16[16,32,1000]{2,1,0:T(8,128)(2,1)} %pad_maximum_fusion.3), calls=%async_computation.6 | async-start | bytes 2097152 | tf_op jit(solution)/shard_map/all_to_all | solution.py:13
  206.9 26.4 %collective-permute-start.12 = (bf16[16,32,512]{2,1,0:T(8,128)(2,1)S(1)}, bf16[16,32,512]{2,1,0:T(8,128)(2,1)}, u32[]{:S(2)}, u32[]{:S(2)}) collective-permute-start(bf16[16,32,512]{2,1,0:T(8,128)(2,1)S(1)} %all-to-all-done.3), channel_id=1, source_target_pairs={{0,256},{256,0},{1,257},{257,1},{2,258},{258,2},{3,259},{259,3},{4... | collective-permute-start | bytes 1572872 | tf_op jit(solution)/shard_map/ppermute | solution.py:25
  234.5 11.4 %collective-permute-start.13 = (bf16[16,32,1000]{2,1,0:T(8,128)(2,1)S(1)}, bf16[16,32,1000]{2,1,0:T(8,128)(2,1)S(1)}, u32[]{:S(2)}, u32[]{:S(2)}) collective-permute-start(bf16[16,32,1000]{2,1,0:T(8,128)(2,1)S(1)} %all-to-all-done.6), channel_id=1, source_target_pairs={{0,1},{1,0},{2,3},{3,2},{4,5},{5,4},{6,7},{7,6},{8,9},{9,8},{10,11... | collective-permute-start | bytes 3072008 | tf_op jit(solution)/shard_map/ppermute | solution.py:21
  238.1 5.8 %collective-permute-start.14 = (f32[32]{0:T(128)S(1)}, f32[32]{0:T(128)S(1)}, u32[]{:S(2)}, u32[]{:S(2)}) collective-permute-start(f32[32]{0:T(128)S(1)} %multiply_reduce_fusion.2), channel_id=1, source_target_pairs={{0,256},{256,0},{1,257},{257,1},{2,258},{258,2},{3,259},{259,3},{4... | collective-permute-start | bytes 392 | tf_op jit(solution)/shard_map/ppermute | solution.py:25

commit v5 on v4

--- a/solution.py
+++ b/solution.py
@@ -52,7 +52,6 @@
     model_width = columns * lax.axis_size(COLUMNS)
     layers, slab, features = captured.shape
     n_y = lax.axis_size("y")
-    n_slabs = lax.axis_size(SLABS)
     part = slab // 2
     group = lax.axis_index("grp")
     core = lax.axis_index("core")
@@ -87,8 +86,8 @@
     partial = jnp.dot(
         tokens, unite_weight.reshape(layers * features, columns), preferred_element_type=f32
     )
-    pieces = partial.astype(half).reshape(n_slabs, 2, part, columns).transpose(1, 0, 2, 3)
-    received = exchanged(pieces.reshape(-1, part, columns), BLOCKS)
+    pieces = partial.astype(half).reshape(-1, part, columns)
+    received = exchanged(pieces, (*SLABS, "grp"))
     united = jnp.sum(received.astype(f32), axis=0)
 
     squares = jnp.concatenate(
@@ -113,7 +112,9 @@
 
     kept, given = split_by_core(target_rows)
     taken = from_other_core(given)
-    target_partial = (share_of(kept, both_heads[0]) + share_of(taken, core_heads[0])).astype(half)
+    target_partial = (
+        share_of(kept, both_heads[0]) + share_of(taken, core_heads[0])
+    ).astype(half)
     kept, given = split_by_core(draft_rows)
     taken = from_other_core(given)
     own_share = share_of(kept, both_heads[1])
@@ -154,17 +155,17 @@
     weights = jnp.where(is_target, valid_mask[:part], valid_mask[part:]) / valid_total
     weighted = (probs[0] * weights[:, None]).astype(bf16)
     delta = ((probs[1] - probs[0]) * weights[:, None]).astype(bf16)
-    outgoing = jnp.concatenate(
-        [
-            jnp.broadcast_to(weighted, (n_y, part, vocab)),
-            jnp.broadcast_to(delta, (n_y, part, vocab)),
-        ]
-    )
+    outgoing = jnp.broadcast_to(
+        jnp.stack([weighted, delta])[:, None], (2, n_y, part, vocab)
+    ).reshape(-1, part, vocab)
     gathered = exchanged(outgoing, ("grp", "y"))
     core_gathered = from_other_core(gathered)
 
     all_rows = jnp.stack(
-        [jnp.where(is_target, draft_rows, other_rows), jnp.where(is_target, other_rows, draft_rows)]
+        [
+            jnp.where(is_target, draft_rows, other_rows),
+            jnp.where(is_target, other_rows, draft_rows),
+        ]
     ).reshape(2, n_y, 2, part, columns)
     own_side = jnp.where(is_first, all_rows[:, :, 0], all_rows[:, :, 1])
     core_side = jnp.where(is_first, all_rows[:, :, 1], all_rows[:, :, 0])

time: 249 us -> 249 us (level)
  no operation moved by 1% of the time
where the time goes in v5:
time: 249 us; the launch traced here: 247 us
  starting transfers between devices  93.4 us (38%)
  waiting for transfers between devices  92.6 us (37%)
  blocking collectives  27.9 us (11%)
  other arithmetic  15.7 us (6%)
  matrix products  8.71 us (3%)
  local copies, waits for them, and re-layouts  6.89 us (3%)
    all_to_all x6, waiting for transfers between devices, exchanged(): return lax.all_to_all(tiles, axes, split_axis=0, concat_axis=0, tiled=True)  47.6 us
    all_to_all x6, starting transfers between devices, exchanged(): return lax.all_to_all(tiles, axes, split_axis=0, concat_axis=0, tiled=True)  30.6 us
    all_to_all x1, blocking collectives, exchanged(): return lax.all_to_all(tiles, axes, split_axis=0, concat_axis=0, tiled=True)  27.9 us
    ppermute x2, waiting for transfers between devices, from_other_group(): return lax.ppermute(shard, 'grp', [(0, 1), (1, 0)])  24.7 us
    ppermute x5, starting transfers between devices, from_other_core(): return lax.ppermute(shard, 'core', [(0, 1), (1, 0)])  23.4 us
    ppermute x3, waiting for transfers between devices, doubled(): other = lax.ppermute(pieces, 'z', pairs)  18.9 us
    ppermute x3, starting transfers between devices, doubled(): other = lax.ppermute(pieces, 'z', pairs)  17.1 us
    ppermute x4, starting transfers between devices, along_x(): lax.ppermute(shard, ('grp', 'xl'), [(i, (i + step) % n) for i in range(n)])  13 us
  transfers between devices with their start and end apart: 21, of which 11 were waited for; matrix products, arithmetic and copies ran while one was open for 8% of the time, Pallas kernels for 0%

profile of v5, /device:TPU:1, one launch (start us, length us, event | category | flops | bytes accessed | tf_op | source)
XLA Modules:
  0.0 247.4 jit_solution(683523383947821835)
XLA Ops:
  0.7 1.0 copy.65
  1.7 27.9 %all_to_all.35 = bf16[8,64,768]{2,1,0:T(8,128)(2,1)S(1)} all-to-all(bf16[8,64,768]{2,1,0:T(8,128)(2,1)S(1)} %broadcast_in_dim.44), channel_id=1, replica_groups=mesh['grp'=2,'xl'=2,'z'=8,'y'=8,'core'=2] {'y'}, dimensions={0} | all-to-all | bytes 1572864 | tf_op jit(solution)/shard_map/all_to_all | solution.py:13
  29.6 5.5 %collective-permute-start.4 = (bf16[8,64,768]{2,1,0:T(8,128)(2,1)S(1)}, bf16[8,64,768]{2,1,0:T(8,128)(2,1)S(1)}, u32[]{:S(2)}, u32[]{:S(2)}) collective-permute-start(bf16[8,64,768]{2,1,0:T(8,128)(2,1)S(1)} %all_to_all.35), channel_id=1, source_target_pairs={{0,1},{1,0},{2,3},{3,2},{4,5},{5,4},{6,7},{7,6},{8,9},{9,8},{10,11... | collective-permute-start | bytes 2359304 | tf_op jit(solution)/shard_map/ppermute | solution.py:21
  35.1 10.6 %collective-permute-start = (bf16[1,32,512]{2,1,0:T(8,128)(2,1)S(1)}, bf16[1,32,512]{2,1,0:T(8,128)(2,1)S(1)}, u32[]{:S(2)}, u32[]{:S(2)}) collective-permute-start(bf16[1,32,512]{2,1,0:T(8,128)(2,1)S(1)} %select_bitcast_fusion.10), channel_id=1, source_target_pairs={{0,64},{16,80},{32,96},{48,112},{64,0},{80,16},{96,32},{112,48},{1... | collective-permute-start | bytes 98312 | tf_op jit(solution)/shard_map/ppermute | solution.py:38
  45.9 0.1 pad_maximum_fusion.1
  46.1 2.0 convolution_convert_fusion
  48.1 7.4 %all-to-all-start.1 = ((f16[32,32,512]{2,1,0:T(8,128)(2,1)}), f16[32,32,512]{2,1,0:T(8,128)(2,1)}, u32[]{:S(2)}, u32[]{:S(2)}) async-start(f16[32,32,512]{2,1,0:T(8,128)(2,1)} %bitcast.18), calls=%async_computation.1 | async-start | bytes 2097152 | tf_op jit(solution)/shard_map/all_to_all | solution.py:13
  55.6 3.1 %collective-permute-start.5 = (bf16[500,512]{1,0:T(8,128)(2,1)S(1)}, bf16[500,512]{1,0:T(8,128)(2,1)S(1)}, u32[]{:S(2)}, u32[]{:S(2)}) collective-permute-start(bf16[500,512]{1,0:T(8,128)(2,1)S(1)} %get-tuple-element.12), channel_id=1, source_target_pairs={{0,128},{128,256},{256,384},{384,0},{1,129},{129,257},{257,385},{3... | collective-permute-start | bytes 1536008 | tf_op jit(solution)/shard_map/ppermute | solution.py:30
  58.7 3.4 %collective-permute-start.7 = (bf16[500,512]{1,0:T(8,128)(2,1)S(1)}, bf16[500,512]{1,0:T(8,128)(2,1)}, u32[]{:S(2)}, u32[]{:S(2)}) collective-permute-start(bf16[500,512]{1,0:T(8,128)(2,1)S(1)} %get-tuple-element.13), channel_id=1, source_target_pairs={{0,384},{128,0},{256,128},{384,256},{1,385},{129,1},{257,129},{385... | collective-permute-start | bytes 1536008 | tf_op jit(solution)/shard_map/ppermute | solution.py:30
  62.2 4.0 %collective-permute-start.1 = (bf16[2,32,512]{2,1,0:T(8,128)(2,1)S(1)}, bf16[2,32,512]{2,1,0:T(8,128)(2,1)S(1)}, u32[]{:S(2)}, u32[]{:S(2)}) collective-permute-start(bf16[2,32,512]{2,1,0:T(8,128)(2,1)S(1)} %maximum_bitcast_fusion), channel_id=1, source_target_pairs={{0,32},{16,48},{32,0},{48,16},{64,96},{80,112},{96,64},{112,80},{1... | collective-permute-start | bytes 196616 | tf_op jit(solution)/shard_map/ppermute | solution.py:38
  66.2 15.4 %collective-permute-done.1 = bf16[2,32,512]{2,1,0:T(8,128)(2,1)S(1)} collective-permute-done((bf16[2,32,512]{2,1,0:T(8,128)(2,1)S(1)}, bf16[2,32,512]{2,1,0:T(8,128)(2,1)S(1)}, u32[]{:S(2)}, u32[]{:S(2)}) %collective-permute-start.1) | collective-permute-done | bytes 65568 | tf_op jit(solution)/shard_map/ppermute | solution.py:38
  81.6 2.5 %collective-permute-start.6 = (bf16[500,512]{1,0:T(8,128)(2,1)S(1)}, bf16[500,512]{1,0:T(8,128)(2,1)S(1)}, u32[]{:S(2)}, u32[]{:S(2)}) collective-permute-start(bf16[500,512]{1,0:T(8,128)(2,1)S(1)} %collective-permute-done.5), channel_id=1, source_target_pairs={{0,128},{128,256},{256,384},{384,0},{1,129},{129,257},{257,385},{3... | collective-permute-start | bytes 1536008 | tf_op jit(solution)/shard_map/ppermute | solution.py:30
  84.1 4.0 %collective-permute-start.8 = (bf16[500,512]{1,0:T(8,128)(2,1)}, bf16[500,512]{1,0:T(8,128)(2,1)S(1)}, u32[]{:S(2)}, u32[]{:S(2)}) collective-permute-start(bf16[500,512]{1,0:T(8,128)(2,1)} %collective-permute-done.7), channel_id=1, source_target_pairs={{0,384},{128,0},{256,128},{384,256},{1,385},{129,1},{257,129},{385... | collective-permute-start | bytes 1536008 | tf_op jit(solution)/shard_map/ppermute | solution.py:30
  88.1 2.5 %collective-permute-start.2 = (bf16[4,32,512]{2,1,0:T(8,128)(2,1)S(1)}, bf16[4,32,512]{2,1,0:T(8,128)(2,1)S(1)}, u32[]{:S(2)}, u32[]{:S(2)}) collective-permute-start(bf16[4,32,512]{2,1,0:T(8,128)(2,1)S(1)} %bitcast.145), channel_id=1, source_target_pairs={{0,16},{16,0},{32,48},{48,32},{64,80},{80,64},{96,112},{112,96},{1... | collective-permute-start | bytes 393224 | tf_op jit(solution)/shard_map/ppermute | solution.py:38
  90.6 3.5 %collective-permute-done.2 = bf16[4,32,512]{2,1,0:T(8,128)(2,1)S(1)} collective-permute-done((bf16[4,32,512]{2,1,0:T(8,128)(2,1)S(1)}, bf16[4,32,512]{2,1,0:T(8,128)(2,1)S(1)}, u32[]{:S(2)}, u32[]{:S(2)}) %collective-permute-start.2) | collective-permute-done | bytes 131104 | tf_op jit(solution)/shard_map/ppermute | solution.py:38
  94.2 1.9 collective-permute-start.3
  96.2 0.7 copy-done.4
  96.9 0.2 copy-done.5
  97.1 1.9 broadcast_select_fusion.1
  99.0 1.5 pad_maximum_fusion
  100.5 7.1 %collective-permute-start.10 = (bf16[2,1000,512]{2,1,0:T(8,128)(2,1)}, bf16[2,1000,512]{2,1,0:T(8,128)(2,1)}, u32[]{:S(2)}, u32[]{:S(2)}) collective-permute-start(bf16[2,1000,512]{2,1,0:T(8,128)(2,1)} %pad_maximum_fusion), channel_id=1, source_target_pairs={{0,1},{1,0},{2,3},{3,2},{4,5},{5,4},{6,7},{7,6},{8,9},{9,8},{10,11... | collective-permute-start | bytes 6144008 | tf_op jit(solution)/shard_map/ppermute | solution.py:21
  107.7 0.2 multiply_reduce_fusion
  107.9 1.4 convert_reduce_fusion.1
  109.4 0.5 copy-done.2
  110.0 0.8 reshape.119
  110.7 3.5 %all-to-all-start.2 = ((f32[16,1,544]{2,1,0:T(1,128)}), f32[16,1,544]{2,1,0:T(1,128)S(1)}, u32[]{:S(2)}, u32[]{:S(2)}) async-start(f32[16,1,544]{2,1,0:T(1,128)} %reshape.119), calls=%async_computation.2 | async-start | bytes 81920 | tf_op jit(solution)/shard_map/all_to_all | solution.py:13
  114.2 1.0 maximum_convert_fusion
  115.3 6.4 %all-to-all-done.2 = f32[16,1,544]{2,1,0:T(1,128)S(1)} async-done(((f32[16,1,544]{2,1,0:T(1,128)}), f32[16,1,544]{2,1,0:T(1,128)S(1)}, u32[]{:S(2)}, u32[]{:S(2)}) %all-to-all-start.2) | async-done | bytes 34848 | tf_op jit(solution)/shard_map/all_to_all | solution.py:13
  121.6 0.5 broadcast.31
  122.2 0.7 reduce.3
  123.2 0.8 broadcast_in_dim.47
  124.0 7.8 %all-to-all-start.3 = ((bf16[16,32,512]{2,1,0:T(8,128)(2,1)}), bf16[16,32,512]{2,1,0:T(8,128)(2,1)S(1)}, u32[]{:S(2)}, u32[]{:S(2)}) async-start(bf16[16,32,512]{2,1,0:T(8,128)(2,1)} %broadcast_in_dim.47), calls=%async_computation.3 | async-start | bytes 1048576 | tf_op jit(solution)/shard_map/all_to_all | solution.py:13
  131.9 1.4 fusion.4
  133.3 2.6 %collective-permute-start.9 = (bf16[8,32,512]{2,1,0:T(8,128)(2,1)S(1)}, bf16[8,32,512]{2,1,0:T(8,128)(2,1)S(1)}, u32[]{:S(2)}, u32[]{:S(2)}) collective-permute-start(bf16[8,32,512]{2,1,0:T(8,128)(2,1)S(1)} %select_bitcast_fusion.3), channel_id=1, source_target_pairs={{0,1},{1,0},{2,3},{3,2},{4,5},{5,4},{6,7},{7,6},{8,9},{9,8},{10,11... | collective-permute-start | bytes 786440 | tf_op jit(solution)/shard_map/ppermute | solution.py:21
  135.9 0.5 fusion.7
  136.4 0.7 collective-permute-done.9
  137.0 1.7 fusion.1
  138.7 6.8 %all-to-all-done.3 = bf16[16,32,512]{2,1,0:T(8,128)(2,1)S(1)} async-done(((bf16[16,32,512]{2,1,0:T(8,128)(2,1)}), bf16[16,32,512]{2,1,0:T(8,128)(2,1)S(1)}, u32[]{:S(2)}, u32[]{:S(2)}) %all-to-all-start.3) | async-done | bytes 524320 | tf_op jit(solution)/shard_map/all_to_all | solution.py:13
  145.5 4.7 %collective-permute-start.11 = (bf16[8,32,512]{2,1,0:T(8,128)(2,1)S(1)}, bf16[8,32,512]{2,1,0:T(8,128)(2,1)S(1)}, u32[]{:S(2)}, u32[]{:S(2)}) collective-permute-start(bf16[8,32,512]{2,1,0:T(8,128)(2,1)S(1)} %select_bitcast_fusion.2), channel_id=1, source_target_pairs={{0,1},{1,0},{2,3},{3,2},{4,5},{5,4},{6,7},{7,6},{8,9},{9,8},{10,11... | collective-permute-start | bytes 786440 | tf_op jit(solution)/shard_map/ppermute | solution.py:21
  150.2 0.5 fusion.5
  150.7 0.7 collective-permute-done.11
  151.4 1.7 fusion.2
  153.1 1.3 pad_maximum_fusion.2
  154.3 3.6 %all-to-all-start.4 = ((f16[8,64,1000]{2,1,0:T(8,128)(2,1)}), f16[8,64,1000]{2,1,0:T(8,128)(2,1)S(1)}, u32[]{:S(2)}, u32[]{:S(2)}) async-start(f16[8,64,1000]{2,1,0:T(8,128)(2,1)} %pad_maximum_fusion.2), calls=%async_computation.4 | async-start | bytes 2097152 | tf_op jit(solution)/shard_map/all_to_all | solution.py:13
  157.9 0.7 fusion.24
  159.2 0.6 compare_convert_fusion
  159.9 27.2 %all-to-all-done.4 = f16[8,64,1000]{2,1,0:T(8,128)(2,1)S(1)} async-done(((f16[8,64,1000]{2,1,0:T(8,128)(2,1)}), f16[8,64,1000]{2,1,0:T(8,128)(2,1)S(1)}, u32[]{:S(2)}, u32[]{:S(2)}) %all-to-all-start.4) | async-done | bytes 1024032 | tf_op jit(solution)/shard_map/all_to_all | solution.py:13
  187.1 0.2 convert_reduce_fusion
  187.5 0.2 exponential_reduce_fusion
  188.1 0.7 reshape.121
  188.8 4.5 %all-to-all-start.5 = ((f32[16,1,160]{2,1,0:T(1,128)}), f32[16,1,160]{2,1,0:T(1,128)S(1)}, u32[]{:S(2)}, u32[]{:S(2)}) async-start(f32[16,1,160]{2,1,0:T(1,128)} %reshape.121), calls=%async_computation.5 | async-start | bytes 32768 | tf_op jit(solution)/shard_map/all_to_all | solution.py:13
  193.4 7.3 %all-to-all-done.5 = f32[16,1,160]{2,1,0:T(1,128)S(1)} async-done(((f32[16,1,160]{2,1,0:T(1,128)}), f32[16,1,160]{2,1,0:T(1,128)S(1)}, u32[]{:S(2)}, u32[]{:S(2)}) %all-to-all-start.5) | async-done | bytes 10272 | tf_op jit(solution)/shard_map/all_to_all | solution.py:13
  200.7 0.7 reduce.4
  201.8 1.1 broadcast_in_dim.51
  202.9 3.8 %all-to-all-start.6 = ((bf16[16,32,1000]{2,1,0:T(8,128)(2,1)}), bf16[16,32,1000]{2,1,0:T(8,128)(2,1)S(1)}, u32[]{:S(2)}, u32[]{:S(2)}) async-start(bf16[16,32,1000]{2,1,0:T(8,128)(2,1)} %bitcast.41), calls=%async_computation.6 | async-start | bytes 2097152 | tf_op jit(solution)/shard_map/all_to_all | solution.py:13
  206.6 4.8 %collective-permute-start.12 = (bf16[16,32,512]{2,1,0:T(8,128)(2,1)S(1)}, bf16[16,32,512]{2,1,0:T(8,128)(2,1)}, u32[]{:S(2)}, u32[]{:S(2)}) collective-permute-start(bf16[16,32,512]{2,1,0:T(8,128)(2,1)S(1)} %all-to-all-done.3), channel_id=1, source_target_pairs={{0,256},{256,0},{1,257},{257,1},{2,258},{258,2},{3,259},{259,3},{4... | collective-permute-start | bytes 1572872 | tf_op jit(solution)/shard_map/ppermute | solution.py:25
  211.4 21.6 %collective-permute-done.12 = bf16[16,32,512]{2,1,0:T(8,128)(2,1)} collective-permute-done((bf16[16,32,512]{2,1,0:T(8,128)(2,1)S(1)}, bf16[16,32,512]{2,1,0:T(8,128)(2,1)}, u32[]{:S(2)}, u32[]{:S(2)}) %collective-permute-start.12) | collective-permute-done | bytes 524320 | tf_op jit(solution)/shard_map/ppermute | solution.py:25
  233.1 1.1 broadcast_select_fusion.3
  234.2 3.6 %collective-permute-start.13 = (bf16[16,32,1000]{2,1,0:T(8,128)(2,1)S(1)}, bf16[16,32,1000]{2,1,0:T(8,128)(2,1)S(1)}, u32[]{:S(2)}, u32[]{:S(2)}) collective-permute-start(bf16[16,32,1000]{2,1,0:T(8,128)(2,1)S(1)} %all-to-all-done.6), channel_id=1, source_target_pairs={{0,1},{1,0},{2,3},{3,2},{4,5},{5,4},{6,7},{7,6},{8,9},{9,8},{10,11... | collective-permute-start | bytes 3072008 | tf_op jit(solution)/shard_map/ppermute | solution.py:21
  237.9 2.7 %collective-permute-start.14 = (f32[32]{0:T(128)S(1)}, f32[32]{0:T(128)S(1)}, u32[]{:S(2)}, u32[]{:S(2)}) collective-permute-start(f32[32]{0:T(128)S(1)} %multiply_reduce_fusion.2), channel_id=1, source_target_pairs={{0,256},{256,0},{1,257},{257,1},{2,258},{258,2},{3,259},{259,3},{4... | collective-permute-start | bytes 392 | tf_op jit(solution)/shard_map/ppermute | solution.py:25
  240.6 3.0 %collective-permute-done.14 = f32[32]{0:T(128)S(1)} collective-permute-done((f32[32]{0:T(128)S(1)}, f32[32]{0:T(128)S(1)}, u32[]{:S(2)}, u32[]{:S(2)}) %collective-permute-start.14) | collective-permute-done | bytes 160 | tf_op jit(solution)/shard_map/ppermute | solution.py:25
  243.7 1.2 maximum_multiply_fusion
  244.9 0.7 fusion.26
  245.6 1.7 fusion
  (73 shorter events, 2.2 us)
Async XLA Ops:
  0.6 45.5 %copy-start = (bf16[3,256,512]{2,1,0:T(8,128)(2,1)S(1)}, bf16[3,256,512]{2,1,0:T(8,128)(2,1)}, u32[]{:S(2)}) copy-start(bf16[3,256,512]{2,1,0:T(8,128)(2,1)} %param.8) | copy-start | bytes 2359300
  0.6 34.5 %copy-start.6 = (bf16[64,512]{1,0:T(8,128)(2,1)S(1)}, bf16[64,512]{1,0:T(8,128)(2,1)}, u32[]{:S(2)}) copy-start(bf16[64,512]{1,0:T(8,128)(2,1)} %param.10) | copy-start | bytes 196612
  29.6 16.2 %collective-permute-start.4 = (bf16[8,64,768]{2,1,0:T(8,128)(2,1)S(1)}, bf16[8,64,768]{2,1,0:T(8,128)(2,1)S(1)}, u32[]{:S(2)}, u32[]{:S(2)}) collective-permute-start(bf16[8,64,768]{2,1,0:T(8,128)(2,1)S(1)} %all_to_all.35), channel_id=1, source_target_pairs={{0,1},{1,0},{2,3},{3,2},{4,5},{5,4},{6,7},{7,6},{8,9},{9,8},{10,11... | collective-permute-start | bytes 2359304 | tf_op jit(solution)/shard_map/ppermute | solution.py:21
  35.1 27.0 %collective-permute-start = (bf16[1,32,512]{2,1,0:T(8,128)(2,1)S(1)}, bf16[1,32,512]{2,1,0:T(8,128)(2,1)S(1)}, u32[]{:S(2)}, u32[]{:S(2)}) collective-permute-start(bf16[1,32,512]{2,1,0:T(8,128)(2,1)S(1)} %select_bitcast_fusion.10), channel_id=1, source_target_pairs={{0,64},{16,80},{32,96},{48,112},{64,0},{80,16},{96,32},{112,48},{1... | collective-permute-start | bytes 98312 | tf_op jit(solution)/shard_map/ppermute | solution.py:38
  48.1 7.4 %copy-start.1 = (bf16[1,1000,512]{2,1,0:T(8,128)(2,1)S(1)}, bf16[1,1000,512]{2,1,0:T(8,128)(2,1)}, u32[]{:S(2)}) copy-start(bf16[1,1000,512]{2,1,0:T(8,128)(2,1)} %param.9) | copy-start | bytes 3072004
  48.1 59.8 %all-to-all-start.1 = ((f16[32,32,512]{2,1,0:T(8,128)(2,1)}), f16[32,32,512]{2,1,0:T(8,128)(2,1)}, u32[]{:S(2)}, u32[]{:S(2)}) async-start(f16[32,32,512]{2,1,0:T(8,128)(2,1)} %bitcast.18), calls=%async_computation.1 | async-start | bytes 2097152 | tf_op jit(solution)/shard_map/all_to_all | solution.py:13
  55.6 25.9 %collective-permute-start.5 = (bf16[500,512]{1,0:T(8,128)(2,1)S(1)}, bf16[500,512]{1,0:T(8,128)(2,1)S(1)}, u32[]{:S(2)}, u32[]{:S(2)}) collective-permute-start(bf16[500,512]{1,0:T(8,128)(2,1)S(1)} %get-tuple-element.12), channel_id=1, source_target_pairs={{0,128},{128,256},{256,384},{384,0},{1,129},{129,257},{257,385},{3... | collective-permute-start | bytes 1536008 | tf_op jit(solution)/shard_map/ppermute | solution.py:30
  58.7 25.4 %collective-permute-start.7 = (bf16[500,512]{1,0:T(8,128)(2,1)S(1)}, bf16[500,512]{1,0:T(8,128)(2,1)}, u32[]{:S(2)}, u32[]{:S(2)}) collective-permute-start(bf16[500,512]{1,0:T(8,128)(2,1)S(1)} %get-tuple-element.13), channel_id=1, source_target_pairs={{0,384},{128,0},{256,128},{384,256},{1,385},{129,1},{257,129},{385... | collective-permute-start | bytes 1536008 | tf_op jit(solution)/shard_map/ppermute | solution.py:30
  62.2 19.3 %collective-permute-start.1 = (bf16[2,32,512]{2,1,0:T(8,128)(2,1)S(1)}, bf16[2,32,512]{2,1,0:T(8,128)(2,1)S(1)}, u32[]{:S(2)}, u32[]{:S(2)}) collective-permute-start(bf16[2,32,512]{2,1,0:T(8,128)(2,1)S(1)} %maximum_bitcast_fusion), channel_id=1, source_target_pairs={{0,32},{16,48},{32,0},{48,16},{64,96},{80,112},{96,64},{112,80},{1... | collective-permute-start | bytes 196616 | tf_op jit(solution)/shard_map/ppermute | solution.py:38
  81.6 14.6 %collective-permute-start.6 = (bf16[500,512]{1,0:T(8,128)(2,1)S(1)}, bf16[500,512]{1,0:T(8,128)(2,1)S(1)}, u32[]{:S(2)}, u32[]{:S(2)}) collective-permute-start(bf16[500,512]{1,0:T(8,128)(2,1)S(1)} %collective-permute-done.5), channel_id=1, source_target_pairs={{0,128},{128,256},{256,384},{384,0},{1,129},{129,257},{257,385},{3... | collective-permute-start | bytes 1536008 | tf_op jit(solution)/shard_map/ppermute | solution.py:30
  84.1 12.1 %collective-permute-start.8 = (bf16[500,512]{1,0:T(8,128)(2,1)}, bf16[500,512]{1,0:T(8,128)(2,1)S(1)}, u32[]{:S(2)}, u32[]{:S(2)}) collective-permute-start(bf16[500,512]{1,0:T(8,128)(2,1)} %collective-permute-done.7), channel_id=1, source_target_pairs={{0,384},{128,0},{256,128},{384,256},{1,385},{129,1},{257,129},{385... | collective-permute-start | bytes 1536008 | tf_op jit(solution)/shard_map/ppermute | solution.py:30
  88.1 6.0 %collective-permute-start.2 = (bf16[4,32,512]{2,1,0:T(8,128)(2,1)S(1)}, bf16[4,32,512]{2,1,0:T(8,128)(2,1)S(1)}, u32[]{:S(2)}, u32[]{:S(2)}) collective-permute-start(bf16[4,32,512]{2,1,0:T(8,128)(2,1)S(1)} %bitcast.145), channel_id=1, source_target_pairs={{0,16},{16,0},{32,48},{48,32},{64,80},{80,64},{96,112},{112,96},{1... | collective-permute-start | bytes 393224 | tf_op jit(solution)/shard_map/ppermute | solution.py:38
  94.2 13.4 %collective-permute-start.3 = (bf16[8,32,512]{2,1,0:T(8,128)(2,1)S(1)}, bf16[8,32,512]{2,1,0:T(8,128)(2,1)S(1)}, u32[]{:S(2)}, u32[]{:S(2)}) collective-permute-start(bf16[8,32,512]{2,1,0:T(8,128)(2,1)S(1)} %bitcast.144), channel_id=1, source_target_pairs={{0,128},{128,0},{1,129},{129,1},{2,130},{130,2},{3,131},{131,3},{4... | collective-permute-start | bytes 786440 | tf_op jit(solution)/shard_map/ppermute | solution.py:44
  96.2 0.8 copy-start.4
  96.2 0.9 copy-start.5
  100.5 35.9 %collective-permute-start.10 = (bf16[2,1000,512]{2,1,0:T(8,128)(2,1)}, bf16[2,1000,512]{2,1,0:T(8,128)(2,1)}, u32[]{:S(2)}, u32[]{:S(2)}) collective-permute-start(bf16[2,1000,512]{2,1,0:T(8,128)(2,1)} %pad_maximum_fusion), channel_id=1, source_target_pairs={{0,1},{1,0},{2,3},{3,2},{4,5},{5,4},{6,7},{7,6},{8,9},{9,8},{10,11... | collective-permute-start | bytes 6144008 | tf_op jit(solution)/shard_map/ppermute | solution.py:21
  109.3 0.6 copy-start.2
  110.7 12.4 %copy-start.3 = (f32[32,512]{1,0:T(8,128)S(1)}, f32[32,512]{1,0:T(8,128)}, u32[]{:S(2)}) copy-start(f32[32,512]{1,0:T(8,128)} %copy-done.2) | copy-start | bytes 196612
  110.7 12.4 %copy-start.8 = (f32[512]{0:T(512)S(1)}, f32[512]{0:T(512)}, u32[]{:S(2)}) copy-start(f32[512]{0:T(512)} %param.12) | copy-start | bytes 6148
  110.7 21.2 %copy-start.7 = (f32[512]{0:T(512)S(1)}, f32[512]{0:T(512)}, u32[]{:S(2)}) copy-start(f32[512]{0:T(512)} %param.11) | copy-start | bytes 6148
  110.7 10.9 %all-to-all-start.2 = ((f32[16,1,544]{2,1,0:T(1,128)}), f32[16,1,544]{2,1,0:T(1,128)S(1)}, u32[]{:S(2)}, u32[]{:S(2)}) async-start(f32[16,1,544]{2,1,0:T(1,128)} %reshape.119), calls=%async_computation.2 | async-start | bytes 81920 | tf_op jit(solution)/shard_map/all_to_all | solution.py:13
  124.0 21.5 %all-to-all-start.3 = ((bf16[16,32,512]{2,1,0:T(8,128)(2,1)}), bf16[16,32,512]{2,1,0:T(8,128)(2,1)S(1)}, u32[]{:S(2)}, u32[]{:S(2)}) async-start(bf16[16,32,512]{2,1,0:T(8,128)(2,1)} %broadcast_in_dim.47), calls=%async_computation.3 | async-start | bytes 1048576 | tf_op jit(solution)/shard_map/all_to_all | solution.py:13
  133.3 3.7 %collective-permute-start.9 = (bf16[8,32,512]{2,1,0:T(8,128)(2,1)S(1)}, bf16[8,32,512]{2,1,0:T(8,128)(2,1)S(1)}, u32[]{:S(2)}, u32[]{:S(2)}) collective-permute-start(bf16[8,32,512]{2,1,0:T(8,128)(2,1)S(1)} %select_bitcast_fusion.3), channel_id=1, source_target_pairs={{0,1},{1,0},{2,3},{3,2},{4,5},{5,4},{6,7},{7,6},{8,9},{9,8},{10,11... | collective-permute-start | bytes 786440 | tf_op jit(solution)/shard_map/ppermute | solution.py:21
  145.5 5.8 %collective-permute-start.11 = (bf16[8,32,512]{2,1,0:T(8,128)(2,1)S(1)}, bf16[8,32,512]{2,1,0:T(8,128)(2,1)S(1)}, u32[]{:S(2)}, u32[]{:S(2)}) collective-permute-start(bf16[8,32,512]{2,1,0:T(8,128)(2,1)S(1)} %select_bitcast_fusion.2), channel_id=1, source_target_pairs={{0,1},{1,0},{2,3},{3,2},{4,5},{5,4},{6,7},{7,6},{8,9},{9,8},{10,11... | collective-permute-start | bytes 786440 | tf_op jit(solution)/shard_map/ppermute | solution.py:21
  153.1 4.9 %copy-start.9 = (s32[16]{0:T(128)S(1)}, s32[16]{0:T(128)}, u32[]{:S(2)}) copy-start(s32[16]{0:T(128)} %param.13) | copy-start | bytes 196
  154.3 32.8 %all-to-all-start.4 = ((f16[8,64,1000]{2,1,0:T(8,128)(2,1)}), f16[8,64,1000]{2,1,0:T(8,128)(2,1)S(1)}, u32[]{:S(2)}, u32[]{:S(2)}) async-start(f16[8,64,1000]{2,1,0:T(8,128)(2,1)} %pad_maximum_fusion.2), calls=%async_computation.4 | async-start | bytes 2097152 | tf_op jit(solution)/shard_map/all_to_all | solution.py:13
  188.8 11.9 %all-to-all-start.5 = ((f32[16,1,160]{2,1,0:T(1,128)}), f32[16,1,160]{2,1,0:T(1,128)S(1)}, u32[]{:S(2)}, u32[]{:S(2)}) async-start(f32[16,1,160]{2,1,0:T(1,128)} %reshape.121), calls=%async_computation.5 | async-start | bytes 32768 | tf_op jit(solution)/shard_map/all_to_all | solution.py:13
  202.9 31.4 %all-to-all-start.6 = ((bf16[16,32,1000]{2,1,0:T(8,128)(2,1)}), bf16[16,32,1000]{2,1,0:T(8,128)(2,1)S(1)}, u32[]{:S(2)}, u32[]{:S(2)}) async-start(bf16[16,32,1000]{2,1,0:T(8,128)(2,1)} %bitcast.41), calls=%async_computation.6 | async-start | bytes 2097152 | tf_op jit(solution)/shard_map/all_to_all | solution.py:13
  206.6 26.4 %collective-permute-start.12 = (bf16[16,32,512]{2,1,0:T(8,128)(2,1)S(1)}, bf16[16,32,512]{2,1,0:T(8,128)(2,1)}, u32[]{:S(2)}, u32[]{:S(2)}) collective-permute-start(bf16[16,32,512]{2,1,0:T(8,128)(2,1)S(1)} %all-to-all-done.3), channel_id=1, source_target_pairs={{0,256},{256,0},{1,257},{257,1},{2,258},{258,2},{3,259},{259,3},{4... | collective-permute-start | bytes 1572872 | tf_op jit(solution)/shard_map/ppermute | solution.py:25
  234.2 11.4 %collective-permute-start.13 = (bf16[16,32,1000]{2,1,0:T(8,128)(2,1)S(1)}, bf16[16,32,1000]{2,1,0:T(8,128)(2,1)S(1)}, u32[]{:S(2)}, u32[]{:S(2)}) collective-permute-start(bf16[16,32,1000]{2,1,0:T(8,128)(2,1)S(1)} %all-to-all-done.6), channel_id=1, source_target_pairs={{0,1},{1,0},{2,3},{3,2},{4,5},{5,4},{6,7},{7,6},{8,9},{9,8},{10,11... | collective-permute-start | bytes 3072008 | tf_op jit(solution)/shard_map/ppermute | solution.py:21
  237.9 5.8 %collective-permute-start.14 = (f32[32]{0:T(128)S(1)}, f32[32]{0:T(128)S(1)}, u32[]{:S(2)}, u32[]{:S(2)}) collective-permute-start(f32[32]{0:T(128)S(1)} %multiply_reduce_fusion.2), channel_id=1, source_target_pairs={{0,256},{256,0},{1,257},{257,1},{2,258},{258,2},{3,259},{259,3},{4... | collective-permute-start | bytes 392 | tf_op jit(solution)/shard_map/ppermute | solution.py:25

commit v6 on v5

--- a/solution.py
+++ b/solution.py
@@ -41,9 +41,13 @@
             [jnp.where(low, pieces, other), jnp.where(low, other, pieces)], axis=1
         ).reshape(-1, *shard.shape)
         stride //= 2
-    other = lax.ppermute(pieces, "xl", [(0, 1), (1, 0)])
-    low = lax.axis_index("xl") == 0
-    return jnp.concatenate([jnp.where(low, pieces, other), jnp.where(low, other, pieces)])
+    return pieces
+
+
+def copied_small(table, axes):
+    rows, lanes = table.shape
+    tile = jnp.pad(table, ((0, -rows % 8), (0, -lanes % 128)))
+    return copied(tile, axes)[:, :rows, :lanes]
 
 
 def per_device(captured, unite_weight, heads, final_hidden, target_gain, draft_gain, lengths):
@@ -93,12 +97,20 @@
     squares = jnp.concatenate(
         [jnp.sum(hidden_rows * hidden_rows, axis=2), jnp.sum(united * united, axis=1)[None]]
     )
-    squares = copied(squares, COLUMNS)
+    squares = copied_small(squares, COLUMNS)
     scales = lax.rsqrt(jnp.sum(squares, axis=0) / model_width + EPSILON)
     draft_part = (united * scales[-1][:, None] * draft_gain[None, :]).astype(bf16)
     draft_rows = copied(draft_part, SLABS)
     other_rows = from_other_group(draft_rows)
     target_rows = (hidden_rows * scales[:-1][:, :, None] * target_gain).astype(bf16)
+    other_target = lax.ppermute(target_rows, "xl", [(0, 1), (1, 0)])
+    is_low = lax.axis_index("xl") == 0
+    target_rows = jnp.concatenate(
+        [
+            jnp.where(is_low, target_rows, other_target),
+            jnp.where(is_low, other_target, target_rows),
+        ]
+    )
 
     def split_by_core(rows):
         by_core = rows.reshape(n_y, 2, part, columns)
@@ -128,7 +140,7 @@
     raised = jnp.exp(shifted)
     local_total = jnp.sum(raised, axis=2)
     crossed = jnp.sum(raised[0] * shifted[1], axis=1)
-    stats = copied(jnp.concatenate([local_top, local_total, crossed[None]]), SLABS)
+    stats = copied_small(jnp.concatenate([local_top, local_total, crossed[None]]), SLABS)
     tops, totals, crosses = stats[:, 0:2], stats[:, 2:4], stats[:, 4]
     top = jnp.max(tops, axis=0)
     total = jnp.sum(totals * jnp.exp(tops - top[None]), axis=0)

time: 249 us -> 248 us (level)
  waiting for transfers between devices: 92.6 us -> 97.3 us
  starting transfers between devices: 93.4 us -> 89.6 us
    all_to_all x6, starting transfers between devices: 30.6 us -> 37.5 us  [exchanged(): return lax.all_to_all(tiles, axes, split_axis=0, concat_axis=0, tiled=True)]
    ppermute x5, starting transfers between devices: 23.4 us -> 17 us  [from_other_core(): return lax.ppermute(shard, 'core', [(0, 1), (1, 0)])]
    ppermute x3, starting transfers between devices: 17.1 us -> 11.8 us  [doubled(): other = lax.ppermute(pieces, 'z', pairs)]
    ppermute x4, waiting for transfers between devices: 0.09 us -> 3.09 us  [along_x(): lax.ppermute(shard, ('grp', 'xl'), [(i, (i + step) % n) for i in range(n)])]
  transfers between devices with their start and end apart: 21 -> 21, of which waited for: 11 -> 14; matrix products, arithmetic and copies ran while one was open for 8% -> 6% of each run, Pallas kernels for 0% -> 0%
where the time goes in v6:
time: 248 us; the launch traced here: 246 us
  waiting for transfers between devices  97.3 us (39%)
  starting transfers between devices  89.6 us (36%)
  blocking collectives  27.9 us (11%)
  other arithmetic  15.4 us (6%)
  matrix products  8.7 us (4%)
  local copies, waits for them, and re-layouts  5.47 us (2%)
    all_to_all x6, waiting for transfers between devices, exchanged(): return lax.all_to_all(tiles, axes, split_axis=0, concat_axis=0, tiled=True)  47.8 us
    all_to_all x6, starting transfers between devices, exchanged(): return lax.all_to_all(tiles, axes, split_axis=0, concat_axis=0, tiled=True)  37.5 us
    all_to_all x1, blocking collectives, exchanged(): return lax.all_to_all(tiles, axes, split_axis=0, concat_axis=0, tiled=True)  27.9 us
    ppermute x2, waiting for transfers between devices, from_other_group(): return lax.ppermute(shard, 'grp', [(0, 1), (1, 0)])  24.7 us
    ppermute x3, waiting for transfers between devices, doubled(): other = lax.ppermute(pieces, 'z', pairs)  18.2 us
    ppermute x5, starting transfers between devices, from_other_core(): return lax.ppermute(shard, 'core', [(0, 1), (1, 0)])  17 us
    ppermute x4, starting transfers between devices, along_x(): lax.ppermute(shard, ('grp', 'xl'), [(i, (i + step) % n) for i in range(n)])  13 us
    ppermute x3, starting transfers between devices, doubled(): other = lax.ppermute(pieces, 'z', pairs)  11.8 us
  transfers between devices with their start and end apart: 21, of which 14 were waited for; matrix products, arithmetic and copies ran while one was open for 6% of the time, Pallas kernels for 0%

profile of v6, /device:TPU:1, one launch (start us, length us, event | category | flops | bytes accessed | tf_op | source)
XLA Modules:
  0.0 246.2 jit_solution(2408317917225727302)
XLA Ops:
  0.6 1.0 copy.91
  1.7 27.9 %all_to_all.35 = bf16[8,64,768]{2,1,0:T(8,128)(2,1)S(1)} all-to-all(bf16[8,64,768]{2,1,0:T(8,128)(2,1)S(1)} %broadcast_in_dim.44), channel_id=1, replica_groups=mesh['grp'=2,'xl'=2,'z'=8,'y'=8,'core'=2] {'y'}, dimensions={0} | all-to-all | bytes 1572864 | tf_op jit(solution)/shard_map/all_to_all | solution.py:13
  29.6 5.5 %collective-permute-start.3 = (bf16[8,64,768]{2,1,0:T(8,128)(2,1)S(1)}, bf16[8,64,768]{2,1,0:T(8,128)(2,1)S(1)}, u32[]{:S(2)}, u32[]{:S(2)}) collective-permute-start(bf16[8,64,768]{2,1,0:T(8,128)(2,1)S(1)} %all_to_all.35), channel_id=1, source_target_pairs={{0,1},{1,0},{2,3},{3,2},{4,5},{5,4},{6,7},{7,6},{8,9},{9,8},{10,11... | collective-permute-start | bytes 2359304 | tf_op jit(solution)/shard_map/ppermute | solution.py:21
  35.1 1.9 collective-permute-done.3
  37.1 0.1 pad_maximum_fusion.1
  37.3 2.0 convolution_convert_fusion
  39.2 13.1 %all-to-all-start.1 = ((f16[32,32,512]{2,1,0:T(8,128)(2,1)}), f16[32,32,512]{2,1,0:T(8,128)(2,1)}, u32[]{:S(2)}, u32[]{:S(2)}) async-start(f16[32,32,512]{2,1,0:T(8,128)(2,1)} %bitcast.18), calls=%async_computation.1 | async-start | bytes 2097152 | tf_op jit(solution)/shard_map/all_to_all | solution.py:13
  52.5 3.1 %collective-permute-start.5 = (bf16[500,512]{1,0:T(8,128)(2,1)S(1)}, bf16[500,512]{1,0:T(8,128)(2,1)S(1)}, u32[]{:S(2)}, u32[]{:S(2)}) collective-permute-start(bf16[500,512]{1,0:T(8,128)(2,1)S(1)} %get-tuple-element.12), channel_id=1, source_target_pairs={{0,128},{128,256},{256,384},{384,0},{1,129},{129,257},{257,385},{3... | collective-permute-start | bytes 1536008 | tf_op jit(solution)/shard_map/ppermute | solution.py:30
  55.6 3.4 %collective-permute-start.7 = (bf16[500,512]{1,0:T(8,128)(2,1)S(1)}, bf16[500,512]{1,0:T(8,128)(2,1)}, u32[]{:S(2)}, u32[]{:S(2)}) collective-permute-start(bf16[500,512]{1,0:T(8,128)(2,1)S(1)} %get-tuple-element.13), channel_id=1, source_target_pairs={{0,384},{128,0},{256,128},{384,256},{1,385},{129,1},{257,129},{385... | collective-permute-start | bytes 1536008 | tf_op jit(solution)/shard_map/ppermute | solution.py:30
  59.1 7.0 %collective-permute-start = (bf16[1,32,512]{2,1,0:T(8,128)(2,1)S(1)}, bf16[1,32,512]{2,1,0:T(8,128)(2,1)S(1)}, u32[]{:S(2)}, u32[]{:S(2)}) collective-permute-start(bf16[1,32,512]{2,1,0:T(8,128)(2,1)S(1)} %select_bitcast_fusion.10), channel_id=1, source_target_pairs={{0,64},{16,80},{32,96},{48,112},{64,0},{80,16},{96,32},{112,48},{1... | collective-permute-start | bytes 98312 | tf_op jit(solution)/shard_map/ppermute | solution.py:38
  66.1 15.2 %collective-permute-done = bf16[1,32,512]{2,1,0:T(8,128)(2,1)S(1)} collective-permute-done((bf16[1,32,512]{2,1,0:T(8,128)(2,1)S(1)}, bf16[1,32,512]{2,1,0:T(8,128)(2,1)S(1)}, u32[]{:S(2)}, u32[]{:S(2)}) %collective-permute-start) | collective-permute-done | bytes 32800 | tf_op jit(solution)/shard_map/ppermute | solution.py:38
  81.2 1.9 collective-permute-start.1
  83.2 2.7 %collective-permute-start.6 = (bf16[500,512]{1,0:T(8,128)(2,1)S(1)}, bf16[500,512]{1,0:T(8,128)(2,1)S(1)}, u32[]{:S(2)}, u32[]{:S(2)}) collective-permute-start(bf16[500,512]{1,0:T(8,128)(2,1)S(1)} %collective-permute-done.5), channel_id=1, source_target_pairs={{0,128},{128,256},{256,384},{384,0},{1,129},{129,257},{257,385},{3... | collective-permute-start | bytes 1536008 | tf_op jit(solution)/shard_map/ppermute | solution.py:30
  85.9 3.8 %collective-permute-start.8 = (bf16[500,512]{1,0:T(8,128)(2,1)}, bf16[500,512]{1,0:T(8,128)(2,1)S(1)}, u32[]{:S(2)}, u32[]{:S(2)}) collective-permute-start(bf16[500,512]{1,0:T(8,128)(2,1)} %collective-permute-done.7), channel_id=1, source_target_pairs={{0,384},{128,0},{256,128},{384,256},{1,385},{129,1},{257,129},{385... | collective-permute-start | bytes 1536008 | tf_op jit(solution)/shard_map/ppermute | solution.py:30
  89.8 2.9 %collective-permute-start.2 = (bf16[4,32,512]{2,1,0:T(8,128)(2,1)S(1)}, bf16[4,32,512]{2,1,0:T(8,128)(2,1)S(1)}, u32[]{:S(2)}, u32[]{:S(2)}) collective-permute-start(bf16[4,32,512]{2,1,0:T(8,128)(2,1)S(1)} %bitcast.164), channel_id=1, source_target_pairs={{0,16},{16,0},{32,48},{48,32},{64,80},{80,64},{96,112},{112,96},{1... | collective-permute-start | bytes 393224 | tf_op jit(solution)/shard_map/ppermute | solution.py:38
  92.7 3.0 %collective-permute-done.2 = bf16[4,32,512]{2,1,0:T(8,128)(2,1)S(1)} collective-permute-done((bf16[4,32,512]{2,1,0:T(8,128)(2,1)S(1)}, bf16[4,32,512]{2,1,0:T(8,128)(2,1)S(1)}, u32[]{:S(2)}, u32[]{:S(2)}) %collective-permute-start.2) | collective-permute-done | bytes 131104 | tf_op jit(solution)/shard_map/ppermute | solution.py:38
  95.9 1.9 collective-permute-done.6
  97.8 1.2 collective-permute-done.8
  99.0 0.8 copy-done.4
  99.8 1.9 broadcast_select_fusion.1
  101.8 1.4 convert_reduce_fusion.1
  103.3 0.7 broadcast_in_dim.46
  103.9 6.5 %all-to-all-start.2 = ((f32[16,16,128]{2,1,0:T(8,128)}), f32[16,16,128]{2,1,0:T(8,128)S(1)}, u32[]{:S(2)}, u32[]{:S(2)}) async-start(f32[16,16,128]{2,1,0:T(8,128)} %broadcast_in_dim.46), calls=%async_computation.2 | async-start | bytes 262144 | tf_op jit(solution)/shard_map/all_to_all | solution.py:13
  110.4 1.5 pad_maximum_fusion
  111.9 2.1 collective-permute-start.10
  114.1 5.5 %all-to-all-done.2 = f32[16,16,128]{2,1,0:T(8,128)S(1)} async-done(((f32[16,16,128]{2,1,0:T(8,128)}), f32[16,16,128]{2,1,0:T(8,128)S(1)}, u32[]{:S(2)}, u32[]{:S(2)}) %all-to-all-start.2) | async-done | bytes 131104 | tf_op jit(solution)/shard_map/all_to_all | solution.py:13
  119.6 1.5 fusion.9
  121.2 2.8 %collective-permute-start.4 = (bf16[8,32,512]{2,1,0:T(8,128)(2,1)}, bf16[8,32,512]{2,1,0:T(8,128)(2,1)}, u32[]{:S(2)}, u32[]{:S(2)}) collective-permute-start(bf16[8,32,512]{2,1,0:T(8,128)(2,1)} %fusion.9), channel_id=1, source_target_pairs={{0,128},{128,0},{1,129},{129,1},{2,130},{130,2},{3,131},{131,3},{4... | collective-permute-start | bytes 786440 | tf_op jit(solution)/shard_map/ppermute | solution.py:106
  124.0 0.8 multiply_convert_fusion.2
  124.7 0.8 broadcast_in_dim.47
  125.6 5.7 %all-to-all-start.3 = ((bf16[16,32,512]{2,1,0:T(8,128)(2,1)}), bf16[16,32,512]{2,1,0:T(8,128)(2,1)S(1)}, u32[]{:S(2)}, u32[]{:S(2)}) async-start(bf16[16,32,512]{2,1,0:T(8,128)(2,1)} %broadcast_in_dim.47), calls=%async_computation.3 | async-start | bytes 1048576 | tf_op jit(solution)/shard_map/all_to_all | solution.py:13
  131.3 0.3 collective-permute-done.4
  131.6 1.3 broadcast_select_fusion.7
  133.0 2.4 collective-permute-start.9
  135.4 0.5 fusion.5
  135.9 0.7 collective-permute-done.9
  136.6 1.7 fusion.1
  138.3 7.8 %all-to-all-done.3 = bf16[16,32,512]{2,1,0:T(8,128)(2,1)S(1)} async-done(((bf16[16,32,512]{2,1,0:T(8,128)(2,1)}), bf16[16,32,512]{2,1,0:T(8,128)(2,1)S(1)}, u32[]{:S(2)}, u32[]{:S(2)}) %all-to-all-start.3) | async-done | bytes 524320 | tf_op jit(solution)/shard_map/all_to_all | solution.py:13
  146.1 3.4 %collective-permute-start.11 = (bf16[8,32,512]{2,1,0:T(8,128)(2,1)S(1)}, bf16[8,32,512]{2,1,0:T(8,128)(2,1)S(1)}, u32[]{:S(2)}, u32[]{:S(2)}) collective-permute-start(bf16[8,32,512]{2,1,0:T(8,128)(2,1)S(1)} %select_bitcast_fusion.2), channel_id=1, source_target_pairs={{0,1},{1,0},{2,3},{3,2},{4,5},{5,4},{6,7},{7,6},{8,9},{9,8},{10,11... | collective-permute-start | bytes 786440 | tf_op jit(solution)/shard_map/ppermute | solution.py:21
  149.6 0.5 fusion.3
  150.0 0.7 collective-permute-done.11
  150.7 1.7 fusion.2
  152.4 1.3 pad_maximum_fusion.2
  153.7 3.6 %all-to-all-start.4 = ((f16[8,64,1000]{2,1,0:T(8,128)(2,1)}), f16[8,64,1000]{2,1,0:T(8,128)(2,1)S(1)}, u32[]{:S(2)}, u32[]{:S(2)}) async-start(f16[8,64,1000]{2,1,0:T(8,128)(2,1)} %pad_maximum_fusion.2), calls=%async_computation.4 | async-start | bytes 2097152 | tf_op jit(solution)/shard_map/all_to_all | solution.py:13
  157.3 0.7 fusion.22
  158.6 0.6 compare_convert_fusion
  159.2 27.2 %all-to-all-done.4 = f16[8,64,1000]{2,1,0:T(8,128)(2,1)S(1)} async-done(((f16[8,64,1000]{2,1,0:T(8,128)(2,1)}), f16[8,64,1000]{2,1,0:T(8,128)(2,1)S(1)}, u32[]{:S(2)}, u32[]{:S(2)}) %all-to-all-start.4) | async-done | bytes 1024032 | tf_op jit(solution)/shard_map/all_to_all | solution.py:13
  186.5 0.2 convert_reduce_fusion
  186.8 0.2 exponential_reduce_fusion
  187.3 0.1 fusion.18
  187.4 0.6 broadcast_in_dim.49
  188.1 4.6 %all-to-all-start.5 = ((f32[16,8,128]{2,1,0:T(8,128)}), f32[16,8,128]{2,1,0:T(8,128)S(1)}, u32[]{:S(2)}, u32[]{:S(2)}) async-start(f32[16,8,128]{2,1,0:T(8,128)} %broadcast_in_dim.49), calls=%async_computation.5 | async-start | bytes 131072 | tf_op jit(solution)/shard_map/all_to_all | solution.py:13
  192.8 7.3 %all-to-all-done.5 = f32[16,8,128]{2,1,0:T(8,128)S(1)} async-done(((f32[16,8,128]{2,1,0:T(8,128)}), f32[16,8,128]{2,1,0:T(8,128)S(1)}, u32[]{:S(2)}, u32[]{:S(2)}) %all-to-all-start.5) | async-done | bytes 65568 | tf_op jit(solution)/shard_map/all_to_all | solution.py:13
  200.4 1.1 broadcast_in_dim.51
  201.5 4.0 %all-to-all-start.6 = ((bf16[16,32,1000]{2,1,0:T(8,128)(2,1)}), bf16[16,32,1000]{2,1,0:T(8,128)(2,1)S(1)}, u32[]{:S(2)}, u32[]{:S(2)}) async-start(bf16[16,32,1000]{2,1,0:T(8,128)(2,1)} %bitcast.41), calls=%async_computation.6 | async-start | bytes 2097152 | tf_op jit(solution)/shard_map/all_to_all | solution.py:13
  205.5 4.8 %collective-permute-start.12 = (bf16[16,32,512]{2,1,0:T(8,128)(2,1)S(1)}, bf16[16,32,512]{2,1,0:T(8,128)(2,1)}, u32[]{:S(2)}, u32[]{:S(2)}) collective-permute-start(bf16[16,32,512]{2,1,0:T(8,128)(2,1)S(1)} %all-to-all-done.3), channel_id=1, source_target_pairs={{0,256},{256,0},{1,257},{257,1},{2,258},{258,2},{3,259},{259,3},{4... | collective-permute-start | bytes 1572872 | tf_op jit(solution)/shard_map/ppermute | solution.py:25
  210.3 21.6 %collective-permute-done.12 = bf16[16,32,512]{2,1,0:T(8,128)(2,1)} collective-permute-done((bf16[16,32,512]{2,1,0:T(8,128)(2,1)S(1)}, bf16[16,32,512]{2,1,0:T(8,128)(2,1)}, u32[]{:S(2)}, u32[]{:S(2)}) %collective-permute-start.12) | collective-permute-done | bytes 524320 | tf_op jit(solution)/shard_map/ppermute | solution.py:25
  232.0 1.1 broadcast_select_fusion.3
  233.1 3.6 %collective-permute-start.13 = (bf16[16,32,1000]{2,1,0:T(8,128)(2,1)S(1)}, bf16[16,32,1000]{2,1,0:T(8,128)(2,1)S(1)}, u32[]{:S(2)}, u32[]{:S(2)}) collective-permute-start(bf16[16,32,1000]{2,1,0:T(8,128)(2,1)S(1)} %all-to-all-done.6), channel_id=1, source_target_pairs={{0,1},{1,0},{2,3},{3,2},{4,5},{5,4},{6,7},{7,6},{8,9},{9,8},{10,11... | collective-permute-start | bytes 3072008 | tf_op jit(solution)/shard_map/ppermute | solution.py:21
  236.8 2.7 %collective-permute-start.14 = (f32[32]{0:T(128)S(1)}, f32[32]{0:T(128)S(1)}, u32[]{:S(2)}, u32[]{:S(2)}) collective-permute-start(f32[32]{0:T(128)S(1)} %multiply_reduce_fusion.2), channel_id=1, source_target_pairs={{0,256},{256,0},{1,257},{257,1},{2,258},{258,2},{3,259},{259,3},{4... | collective-permute-start | bytes 392 | tf_op jit(solution)/shard_map/ppermute | solution.py:25
  239.5 3.0 %collective-permute-done.14 = f32[32]{0:T(128)S(1)} collective-permute-done((f32[32]{0:T(128)S(1)}, f32[32]{0:T(128)S(1)}, u32[]{:S(2)}, u32[]{:S(2)}) %collective-permute-start.14) | collective-permute-done | bytes 160 | tf_op jit(solution)/shard_map/ppermute | solution.py:25
  242.6 1.2 maximum_multiply_fusion
  243.8 0.7 fusion.24
  244.5 1.7 fusion
  (62 shorter events, 1.8 us)
Async XLA Ops:
  0.6 36.6 %copy-start = (bf16[3,256,512]{2,1,0:T(8,128)(2,1)S(1)}, bf16[3,256,512]{2,1,0:T(8,128)(2,1)}, u32[]{:S(2)}) copy-start(bf16[3,256,512]{2,1,0:T(8,128)(2,1)} %param.8) | copy-start | bytes 2359300
  29.6 7.4 %collective-permute-start.3 = (bf16[8,64,768]{2,1,0:T(8,128)(2,1)S(1)}, bf16[8,64,768]{2,1,0:T(8,128)(2,1)S(1)}, u32[]{:S(2)}, u32[]{:S(2)}) collective-permute-start(bf16[8,64,768]{2,1,0:T(8,128)(2,1)S(1)} %all_to_all.35), channel_id=1, source_target_pairs={{0,1},{1,0},{2,3},{3,2},{4,5},{5,4},{6,7},{7,6},{8,9},{9,8},{10,11... | collective-permute-start | bytes 2359304 | tf_op jit(solution)/shard_map/ppermute | solution.py:21
  39.2 13.2 %copy-start.2 = (bf16[1,1000,512]{2,1,0:T(8,128)(2,1)S(1)}, bf16[1,1000,512]{2,1,0:T(8,128)(2,1)}, u32[]{:S(2)}) copy-start(bf16[1,1000,512]{2,1,0:T(8,128)(2,1)} %param.9) | copy-start | bytes 3072004
  39.2 19.8 %copy-start.5 = (bf16[64,512]{1,0:T(8,128)(2,1)S(1)}, bf16[64,512]{1,0:T(8,128)(2,1)}, u32[]{:S(2)}) copy-start(bf16[64,512]{1,0:T(8,128)(2,1)} %param.10) | copy-start | bytes 196612
  39.2 62.5 %all-to-all-start.1 = ((f16[32,32,512]{2,1,0:T(8,128)(2,1)}), f16[32,32,512]{2,1,0:T(8,128)(2,1)}, u32[]{:S(2)}, u32[]{:S(2)}) async-start(f16[32,32,512]{2,1,0:T(8,128)(2,1)} %bitcast.18), calls=%async_computation.1 | async-start | bytes 2097152 | tf_op jit(solution)/shard_map/all_to_all | solution.py:13
  52.5 30.7 %collective-permute-start.5 = (bf16[500,512]{1,0:T(8,128)(2,1)S(1)}, bf16[500,512]{1,0:T(8,128)(2,1)S(1)}, u32[]{:S(2)}, u32[]{:S(2)}) collective-permute-start(bf16[500,512]{1,0:T(8,128)(2,1)S(1)} %get-tuple-element.12), channel_id=1, source_target_pairs={{0,128},{128,256},{256,384},{384,0},{1,129},{129,257},{257,385},{3... | collective-permute-start | bytes 1536008 | tf_op jit(solution)/shard_map/ppermute | solution.py:30
  55.6 30.3 %collective-permute-start.7 = (bf16[500,512]{1,0:T(8,128)(2,1)S(1)}, bf16[500,512]{1,0:T(8,128)(2,1)}, u32[]{:S(2)}, u32[]{:S(2)}) collective-permute-start(bf16[500,512]{1,0:T(8,128)(2,1)S(1)} %get-tuple-element.13), channel_id=1, source_target_pairs={{0,384},{128,0},{256,128},{384,256},{1,385},{129,1},{257,129},{385... | collective-permute-start | bytes 1536008 | tf_op jit(solution)/shard_map/ppermute | solution.py:30
  59.1 22.1 %collective-permute-start = (bf16[1,32,512]{2,1,0:T(8,128)(2,1)S(1)}, bf16[1,32,512]{2,1,0:T(8,128)(2,1)S(1)}, u32[]{:S(2)}, u32[]{:S(2)}) collective-permute-start(bf16[1,32,512]{2,1,0:T(8,128)(2,1)S(1)} %select_bitcast_fusion.10), channel_id=1, source_target_pairs={{0,64},{16,80},{32,96},{48,112},{64,0},{80,16},{96,32},{112,48},{1... | collective-permute-start | bytes 98312 | tf_op jit(solution)/shard_map/ppermute | solution.py:38
  81.2 8.5 %collective-permute-start.1 = (bf16[2,32,512]{2,1,0:T(8,128)(2,1)S(1)}, bf16[2,32,512]{2,1,0:T(8,128)(2,1)S(1)}, u32[]{:S(2)}, u32[]{:S(2)}) collective-permute-start(bf16[2,32,512]{2,1,0:T(8,128)(2,1)S(1)} %maximum_bitcast_fusion), channel_id=1, source_target_pairs={{0,32},{16,48},{32,0},{48,16},{64,96},{80,112},{96,64},{112,80},{1... | collective-permute-start | bytes 196616 | tf_op jit(solution)/shard_map/ppermute | solution.py:38
  83.2 14.6 %collective-permute-start.6 = (bf16[500,512]{1,0:T(8,128)(2,1)S(1)}, bf16[500,512]{1,0:T(8,128)(2,1)S(1)}, u32[]{:S(2)}, u32[]{:S(2)}) collective-permute-start(bf16[500,512]{1,0:T(8,128)(2,1)S(1)} %collective-permute-done.5), channel_id=1, source_target_pairs={{0,128},{128,256},{256,384},{384,0},{1,129},{129,257},{257,385},{3... | collective-permute-start | bytes 1536008 | tf_op jit(solution)/shard_map/ppermute | solution.py:30
  85.9 13.1 %collective-permute-start.8 = (bf16[500,512]{1,0:T(8,128)(2,1)}, bf16[500,512]{1,0:T(8,128)(2,1)S(1)}, u32[]{:S(2)}, u32[]{:S(2)}) collective-permute-start(bf16[500,512]{1,0:T(8,128)(2,1)} %collective-permute-done.7), channel_id=1, source_target_pairs={{0,384},{128,0},{256,128},{384,256},{1,385},{129,1},{257,129},{385... | collective-permute-start | bytes 1536008 | tf_op jit(solution)/shard_map/ppermute | solution.py:30
  89.8 6.0 %collective-permute-start.2 = (bf16[4,32,512]{2,1,0:T(8,128)(2,1)S(1)}, bf16[4,32,512]{2,1,0:T(8,128)(2,1)S(1)}, u32[]{:S(2)}, u32[]{:S(2)}) collective-permute-start(bf16[4,32,512]{2,1,0:T(8,128)(2,1)S(1)} %bitcast.164), channel_id=1, source_target_pairs={{0,16},{16,0},{32,48},{48,32},{64,80},{80,64},{96,112},{112,96},{1... | collective-permute-start | bytes 393224 | tf_op jit(solution)/shard_map/ppermute | solution.py:38
  97.8 1.2 copy-start.3
  99.0 0.8 copy-start.4
  103.9 15.6 %all-to-all-start.2 = ((f32[16,16,128]{2,1,0:T(8,128)}), f32[16,16,128]{2,1,0:T(8,128)S(1)}, u32[]{:S(2)}, u32[]{:S(2)}) async-start(f32[16,16,128]{2,1,0:T(8,128)} %broadcast_in_dim.46), calls=%async_computation.2 | async-start | bytes 262144 | tf_op jit(solution)/shard_map/all_to_all | solution.py:13
  111.9 24.0 %collective-permute-start.10 = (bf16[2,1000,512]{2,1,0:T(8,128)(2,1)}, bf16[2,1000,512]{2,1,0:T(8,128)(2,1)}, u32[]{:S(2)}, u32[]{:S(2)}) collective-permute-start(bf16[2,1000,512]{2,1,0:T(8,128)(2,1)} %pad_maximum_fusion), channel_id=1, source_target_pairs={{0,1},{1,0},{2,3},{3,2},{4,5},{5,4},{6,7},{7,6},{8,9},{9,8},{10,11... | collective-permute-start | bytes 6144008 | tf_op jit(solution)/shard_map/ppermute | solution.py:21
  114.1 11.4 %copy-start.1 = (f32[4,2,32,512]{3,2,1,0:T(8,128)}, f32[4,2,32,512]{3,2,1,0:T(8,128)S(1)}, u32[]{:S(2)}) copy-start(f32[4,2,32,512]{3,2,1,0:T(8,128)S(1)} %copy.67) | copy-start | bytes 1572868
  119.6 12.0 %copy-start.6 = (f32[512]{0:T(512)S(1)}, f32[512]{0:T(512)}, u32[]{:S(2)}) copy-start(f32[512]{0:T(512)} %param.11) | copy-start | bytes 6148
  121.2 10.4 %collective-permute-start.4 = (bf16[8,32,512]{2,1,0:T(8,128)(2,1)}, bf16[8,32,512]{2,1,0:T(8,128)(2,1)}, u32[]{:S(2)}, u32[]{:S(2)}) collective-permute-start(bf16[8,32,512]{2,1,0:T(8,128)(2,1)} %fusion.9), channel_id=1, source_target_pairs={{0,128},{128,0},{1,129},{129,1},{2,130},{130,2},{3,131},{131,3},{4... | collective-permute-start | bytes 786440 | tf_op jit(solution)/shard_map/ppermute | solution.py:106
  125.6 20.5 %all-to-all-start.3 = ((bf16[16,32,512]{2,1,0:T(8,128)(2,1)}), bf16[16,32,512]{2,1,0:T(8,128)(2,1)S(1)}, u32[]{:S(2)}, u32[]{:S(2)}) async-start(bf16[16,32,512]{2,1,0:T(8,128)(2,1)} %broadcast_in_dim.47), calls=%async_computation.3 | async-start | bytes 1048576 | tf_op jit(solution)/shard_map/all_to_all | solution.py:13
  133.0 3.6 %collective-permute-start.9 = (bf16[8,32,512]{2,1,0:T(8,128)(2,1)S(1)}, bf16[8,32,512]{2,1,0:T(8,128)(2,1)S(1)}, u32[]{:S(2)}, u32[]{:S(2)}) collective-permute-start(bf16[8,32,512]{2,1,0:T(8,128)(2,1)S(1)} %select_bitcast_fusion.3), channel_id=1, source_target_pairs={{0,1},{1,0},{2,3},{3,2},{4,5},{5,4},{6,7},{7,6},{8,9},{9,8},{10,11... | collective-permute-start | bytes 786440 | tf_op jit(solution)/shard_map/ppermute | solution.py:21
  146.1 4.6 %collective-permute-start.11 = (bf16[8,32,512]{2,1,0:T(8,128)(2,1)S(1)}, bf16[8,32,512]{2,1,0:T(8,128)(2,1)S(1)}, u32[]{:S(2)}, u32[]{:S(2)}) collective-permute-start(bf16[8,32,512]{2,1,0:T(8,128)(2,1)S(1)} %select_bitcast_fusion.2), channel_id=1, source_target_pairs={{0,1},{1,0},{2,3},{3,2},{4,5},{5,4},{6,7},{7,6},{8,9},{9,8},{10,11... | collective-permute-start | bytes 786440 | tf_op jit(solution)/shard_map/ppermute | solution.py:21
  152.4 4.9 %copy-start.7 = (s32[16]{0:T(128)S(1)}, s32[16]{0:T(128)}, u32[]{:S(2)}) copy-start(s32[16]{0:T(128)} %param.13) | copy-start | bytes 196
  153.7 32.8 %all-to-all-start.4 = ((f16[8,64,1000]{2,1,0:T(8,128)(2,1)}), f16[8,64,1000]{2,1,0:T(8,128)(2,1)S(1)}, u32[]{:S(2)}, u32[]{:S(2)}) async-start(f16[8,64,1000]{2,1,0:T(8,128)(2,1)} %pad_maximum_fusion.2), calls=%async_computation.4 | async-start | bytes 2097152 | tf_op jit(solution)/shard_map/all_to_all | solution.py:13
  188.1 12.0 %all-to-all-start.5 = ((f32[16,8,128]{2,1,0:T(8,128)}), f32[16,8,128]{2,1,0:T(8,128)S(1)}, u32[]{:S(2)}, u32[]{:S(2)}) async-start(f32[16,8,128]{2,1,0:T(8,128)} %broadcast_in_dim.49), calls=%async_computation.5 | async-start | bytes 131072 | tf_op jit(solution)/shard_map/all_to_all | solution.py:13
  201.5 31.6 %all-to-all-start.6 = ((bf16[16,32,1000]{2,1,0:T(8,128)(2,1)}), bf16[16,32,1000]{2,1,0:T(8,128)(2,1)S(1)}, u32[]{:S(2)}, u32[]{:S(2)}) async-start(bf16[16,32,1000]{2,1,0:T(8,128)(2,1)} %bitcast.41), calls=%async_computation.6 | async-start | bytes 2097152 | tf_op jit(solution)/shard_map/all_to_all | solution.py:13
  205.5 26.4 %collective-permute-start.12 = (bf16[16,32,512]{2,1,0:T(8,128)(2,1)S(1)}, bf16[16,32,512]{2,1,0:T(8,128)(2,1)}, u32[]{:S(2)}, u32[]{:S(2)}) collective-permute-start(bf16[16,32,512]{2,1,0:T(8,128)(2,1)S(1)} %all-to-all-done.3), channel_id=1, source_target_pairs={{0,256},{256,0},{1,257},{257,1},{2,258},{258,2},{3,259},{259,3},{4... | collective-permute-start | bytes 1572872 | tf_op jit(solution)/shard_map/ppermute | solution.py:25
  233.1 11.4 %collective-permute-start.13 = (bf16[16,32,1000]{2,1,0:T(8,128)(2,1)S(1)}, bf16[16,32,1000]{2,1,0:T(8,128)(2,1)S(1)}, u32[]{:S(2)}, u32[]{:S(2)}) collective-permute-start(bf16[16,32,1000]{2,1,0:T(8,128)(2,1)S(1)} %all-to-all-done.6), channel_id=1, source_target_pairs={{0,1},{1,0},{2,3},{3,2},{4,5},{5,4},{6,7},{7,6},{8,9},{9,8},{10,11... | collective-permute-start | bytes 3072008 | tf_op jit(solution)/shard_map/ppermute | solution.py:21
  236.8 5.8 %collective-permute-start.14 = (f32[32]{0:T(128)S(1)}, f32[32]{0:T(128)S(1)}, u32[]{:S(2)}, u32[]{:S(2)}) collective-permute-start(f32[32]{0:T(128)S(1)} %multiply_reduce_fusion.2), channel_id=1, source_target_pairs={{0,256},{256,0},{1,257},{257,1},{2,258},{258,2},{3,259},{259,3},{4... | collective-permute-start | bytes 392 | tf_op jit(solution)/shard_map/ppermute | solution.py:25

commit v7 on v5

--- a/solution.py
+++ b/solution.py
@@ -46,6 +46,12 @@
     return jnp.concatenate([jnp.where(low, pieces, other), jnp.where(low, other, pieces)])
 
 
+def copied_small(table, axes):
+    rows, lanes = table.shape
+    tile = jnp.pad(table, ((0, -rows % 8), (0, -lanes % 128)))
+    return copied(tile, axes)[:, :rows, :lanes]
+
+
 def per_device(captured, unite_weight, heads, final_hidden, target_gain, draft_gain, lengths):
     f32, bf16, half = jnp.float32, jnp.bfloat16, jnp.float16
     columns = final_hidden.shape[1]
@@ -90,15 +96,17 @@
     received = exchanged(pieces, (*SLABS, "grp"))
     united = jnp.sum(received.astype(f32), axis=0)
 
+    united_squares = jnp.pad(jnp.sum(united * united, axis=1), (0, 128 - part))
     squares = jnp.concatenate(
-        [jnp.sum(hidden_rows * hidden_rows, axis=2), jnp.sum(united * united, axis=1)[None]]
-    )
-    squares = copied(squares, COLUMNS)
+        [jnp.sum(hidden_rows * hidden_rows, axis=2).reshape(-1, 128), united_squares[None]]
+    )
+    squares = copied_small(squares, COLUMNS)
     scales = lax.rsqrt(jnp.sum(squares, axis=0) / model_width + EPSILON)
-    draft_part = (united * scales[-1][:, None] * draft_gain[None, :]).astype(bf16)
+    draft_part = (united * scales[-1, :part, None] * draft_gain[None, :]).astype(bf16)
+    hidden_scale = scales[:-1].reshape(-1, part, 1)
     draft_rows = copied(draft_part, SLABS)
     other_rows = from_other_group(draft_rows)
-    target_rows = (hidden_rows * scales[:-1][:, :, None] * target_gain).astype(bf16)
+    target_rows = (hidden_rows * hidden_scale * target_gain).astype(bf16)
 
     def split_by_core(rows):
         by_core = rows.reshape(n_y, 2, part, columns)
@@ -112,9 +120,7 @@
 
     kept, given = split_by_core(target_rows)
     taken = from_other_core(given)
-    target_partial = (
-        share_of(kept, both_heads[0]) + share_of(taken, core_heads[0])
-    ).astype(half)
+    target_partial = (share_of(kept, both_heads[0]) + share_of(taken, core_heads[0])).astype(half)
     kept, given = split_by_core(draft_rows)
     taken = from_other_core(given)
     own_share = share_of(kept, both_heads[1])
@@ -128,7 +134,7 @@
     raised = jnp.exp(shifted)
     local_total = jnp.sum(raised, axis=2)
     crossed = jnp.sum(raised[0] * shifted[1], axis=1)
-    stats = copied(jnp.concatenate([local_top, local_total, crossed[None]]), SLABS)
+    stats = copied_small(jnp.concatenate([local_top, local_total, crossed[None]]), SLABS)
     tops, totals, crosses = stats[:, 0:2], stats[:, 2:4], stats[:, 4]
     top = jnp.max(tops, axis=0)
     total = jnp.sum(totals * jnp.exp(tops - top[None]), axis=0)
@@ -162,10 +168,7 @@
     core_gathered = from_other_core(gathered)
 
     all_rows = jnp.stack(
-        [
-            jnp.where(is_target, draft_rows, other_rows),
-            jnp.where(is_target, other_rows, draft_rows),
-        ]
+        [jnp.where(is_target, draft_rows, other_rows), jnp.where(is_target, other_rows, draft_rows)]
     ).reshape(2, n_y, 2, part, columns)
     own_side = jnp.where(is_first, all_rows[:, :, 0], all_rows[:, :, 1])
     core_side = jnp.where(is_first, all_rows[:, :, 1], all_rows[:, :, 0])

time: 249 us -> 257 us (1.032)
  waiting for transfers between devices: 92.6 us -> 102 us
    ppermute x4, waiting for transfers between devices: 0.09 us -> 8.86 us  [along_x(): lax.ppermute(shard, ('grp', 'xl'), [(i, (i + step) % n) for i in range(n)])]
  transfers between devices with their start and end apart: 21 -> 21, of which waited for: 11 -> 12; matrix products, arithmetic and copies ran while one was open for 8% -> 7% of each run, Pallas kernels for 0% -> 0%
where the time goes in v7:
time: 257 us; the launch traced here: 256 us
  waiting for transfers between devices  102 us (40%)
  starting transfers between devices  95.8 us (37%)
  blocking collectives  27.9 us (11%)
  other arithmetic  14.3 us (6%)
  matrix products  8.71 us (3%)
  local copies, waits for them, and re-layouts  5.61 us (2%)
    all_to_all x6, waiting for transfers between devices, exchanged(): return lax.all_to_all(tiles, axes, split_axis=0, concat_axis=0, tiled=True)  48.3 us
    all_to_all x6, starting transfers between devices, exchanged(): return lax.all_to_all(tiles, axes, split_axis=0, concat_axis=0, tiled=True)  32.6 us
    all_to_all x1, blocking collectives, exchanged(): return lax.all_to_all(tiles, axes, split_axis=0, concat_axis=0, tiled=True)  27.9 us
    ppermute x2, waiting for transfers between devices, from_other_group(): return lax.ppermute(shard, 'grp', [(0, 1), (1, 0)])  24.7 us
    ppermute x5, starting transfers between devices, from_other_core(): return lax.ppermute(shard, 'core', [(0, 1), (1, 0)])  21 us
    ppermute x3, starting transfers between devices, doubled(): other = lax.ppermute(pieces, 'z', pairs)  18.6 us
    ppermute x3, waiting for transfers between devices, doubled(): other = lax.ppermute(pieces, 'z', pairs)  18.4 us
    ppermute x4, starting transfers between devices, along_x(): lax.ppermute(shard, ('grp', 'xl'), [(i, (i + step) % n) for i in range(n)])  13 us
  transfers between devices with their start and end apart: 21, of which 12 were waited for; matrix products, arithmetic and copies ran while one was open for 7% of the time, Pallas kernels for 0%

profile of v7, /device:TPU:1, one launch (start us, length us, event | category | flops | bytes accessed | tf_op | source)
XLA Modules:
  0.0 255.9 jit_solution(8431043279036835547)
XLA Ops:
  0.7 1.0 copy.65
  1.7 27.9 %all_to_all.35 = bf16[8,64,768]{2,1,0:T(8,128)(2,1)S(1)} all-to-all(bf16[8,64,768]{2,1,0:T(8,128)(2,1)S(1)} %broadcast_in_dim.43), channel_id=1, replica_groups=mesh['grp'=2,'xl'=2,'z'=8,'y'=8,'core'=2] {'y'}, dimensions={0} | all-to-all | bytes 1572864 | tf_op jit(solution)/shard_map/all_to_all | solution.py:13
  29.6 5.5 %collective-permute-start.4 = (bf16[8,64,768]{2,1,0:T(8,128)(2,1)S(1)}, bf16[8,64,768]{2,1,0:T(8,128)(2,1)S(1)}, u32[]{:S(2)}, u32[]{:S(2)}) collective-permute-start(bf16[8,64,768]{2,1,0:T(8,128)(2,1)S(1)} %all_to_all.35), channel_id=1, source_target_pairs={{0,1},{1,0},{2,3},{3,2},{4,5},{5,4},{6,7},{7,6},{8,9},{9,8},{10,11... | collective-permute-start | bytes 2359304 | tf_op jit(solution)/shard_map/ppermute | solution.py:21
  35.1 10.6 %collective-permute-start = (bf16[1,32,512]{2,1,0:T(8,128)(2,1)S(1)}, bf16[1,32,512]{2,1,0:T(8,128)(2,1)S(1)}, u32[]{:S(2)}, u32[]{:S(2)}) collective-permute-start(bf16[1,32,512]{2,1,0:T(8,128)(2,1)S(1)} %select_bitcast_fusion.10), channel_id=1, source_target_pairs={{0,64},{16,80},{32,96},{48,112},{64,0},{80,16},{96,32},{112,48},{1... | collective-permute-start | bytes 98312 | tf_op jit(solution)/shard_map/ppermute | solution.py:38
  45.8 1.7 collective-permute-done
  47.6 4.9 %collective-permute-start.1 = (bf16[2,32,512]{2,1,0:T(8,128)(2,1)S(1)}, bf16[2,32,512]{2,1,0:T(8,128)(2,1)S(1)}, u32[]{:S(2)}, u32[]{:S(2)}) collective-permute-start(bf16[2,32,512]{2,1,0:T(8,128)(2,1)S(1)} %maximum_bitcast_fusion), channel_id=1, source_target_pairs={{0,32},{16,48},{32,0},{48,16},{64,96},{80,112},{96,64},{112,80},{1... | collective-permute-start | bytes 196616 | tf_op jit(solution)/shard_map/ppermute | solution.py:38
  52.6 0.1 pad_maximum_fusion.1
  52.7 2.0 convolution_convert_fusion
  54.7 9.4 %all-to-all-start.1 = ((f16[32,32,512]{2,1,0:T(8,128)(2,1)}), f16[32,32,512]{2,1,0:T(8,128)(2,1)}, u32[]{:S(2)}, u32[]{:S(2)}) async-start(f16[32,32,512]{2,1,0:T(8,128)(2,1)} %bitcast.18), calls=%async_computation.1 | async-start | bytes 2097152 | tf_op jit(solution)/shard_map/all_to_all | solution.py:13
  64.2 3.1 %collective-permute-start.2 = (bf16[4,32,512]{2,1,0:T(8,128)(2,1)S(1)}, bf16[4,32,512]{2,1,0:T(8,128)(2,1)S(1)}, u32[]{:S(2)}, u32[]{:S(2)}) collective-permute-start(bf16[4,32,512]{2,1,0:T(8,128)(2,1)S(1)} %bitcast.145), channel_id=1, source_target_pairs={{0,16},{16,0},{32,48},{48,32},{64,80},{80,64},{96,112},{112,96},{1... | collective-permute-start | bytes 393224 | tf_op jit(solution)/shard_map/ppermute | solution.py:38
  67.3 0.1 slice_bitcast_fusion.5
  67.4 3.1 %collective-permute-start.5 = (bf16[500,512]{1,0:T(8,128)(2,1)S(1)}, bf16[500,512]{1,0:T(8,128)(2,1)}, u32[]{:S(2)}, u32[]{:S(2)}) collective-permute-start(bf16[500,512]{1,0:T(8,128)(2,1)S(1)} %get-tuple-element.12), channel_id=1, source_target_pairs={{0,128},{128,256},{256,384},{384,0},{1,129},{129,257},{257,385},{3... | collective-permute-start | bytes 1536008 | tf_op jit(solution)/shard_map/ppermute | solution.py:30
  70.5 3.4 %collective-permute-start.7 = (bf16[500,512]{1,0:T(8,128)(2,1)S(1)}, bf16[500,512]{1,0:T(8,128)(2,1)}, u32[]{:S(2)}, u32[]{:S(2)}) collective-permute-start(bf16[500,512]{1,0:T(8,128)(2,1)S(1)} %get-tuple-element.13), channel_id=1, source_target_pairs={{0,384},{128,0},{256,128},{384,256},{1,385},{129,1},{257,129},{385... | collective-permute-start | bytes 1536008 | tf_op jit(solution)/shard_map/ppermute | solution.py:30
  73.9 16.7 %collective-permute-done.2 = bf16[4,32,512]{2,1,0:T(8,128)(2,1)S(1)} collective-permute-done((bf16[4,32,512]{2,1,0:T(8,128)(2,1)S(1)}, bf16[4,32,512]{2,1,0:T(8,128)(2,1)S(1)}, u32[]{:S(2)}, u32[]{:S(2)}) %collective-permute-start.2) | collective-permute-done | bytes 131104 | tf_op jit(solution)/shard_map/ppermute | solution.py:38
  90.7 3.1 %collective-permute-start.3 = (bf16[8,32,512]{2,1,0:T(8,128)(2,1)S(1)}, bf16[8,32,512]{2,1,0:T(8,128)(2,1)S(1)}, u32[]{:S(2)}, u32[]{:S(2)}) collective-permute-start(bf16[8,32,512]{2,1,0:T(8,128)(2,1)S(1)} %bitcast.144), channel_id=1, source_target_pairs={{0,128},{128,0},{1,129},{129,1},{2,130},{130,2},{3,131},{131,3},{4... | collective-permute-start | bytes 786440 | tf_op jit(solution)/shard_map/ppermute | solution.py:44
  93.8 2.2 collective-permute-start.6
  96.0 4.3 %collective-permute-start.8 = (bf16[500,512]{1,0:T(8,128)(2,1)}, bf16[500,512]{1,0:T(8,128)(2,1)S(1)}, u32[]{:S(2)}, u32[]{:S(2)}) collective-permute-start(bf16[500,512]{1,0:T(8,128)(2,1)} %collective-permute-done.7), channel_id=1, source_target_pairs={{0,384},{128,0},{256,128},{384,256},{1,385},{129,1},{257,129},{385... | collective-permute-start | bytes 1536008 | tf_op jit(solution)/shard_map/ppermute | solution.py:30
  100.4 0.2 multiply_reduce_fusion
  100.7 8.3 %collective-permute-done.6 = bf16[500,512]{1,0:T(8,128)(2,1)S(1)} collective-permute-done((bf16[500,512]{1,0:T(8,128)(2,1)}, bf16[500,512]{1,0:T(8,128)(2,1)S(1)}, u32[]{:S(2)}, u32[]{:S(2)}) %collective-permute-start.6) | collective-permute-done | bytes 512032 | tf_op jit(solution)/shard_map/ppermute | solution.py:30
  109.0 0.6 collective-permute-done.8
  109.5 0.2 copy-done.2
  109.8 0.6 copy-done.3
  110.3 1.9 broadcast_select_fusion.1
  112.2 1.5 pad_maximum_fusion
  113.8 5.1 %collective-permute-start.10 = (bf16[2,1000,512]{2,1,0:T(8,128)(2,1)}, bf16[2,1000,512]{2,1,0:T(8,128)(2,1)}, u32[]{:S(2)}, u32[]{:S(2)}) collective-permute-start(bf16[2,1000,512]{2,1,0:T(8,128)(2,1)} %pad_maximum_fusion), channel_id=1, source_target_pairs={{0,1},{1,0},{2,3},{3,2},{4,5},{5,4},{6,7},{7,6},{8,9},{9,8},{10,11... | collective-permute-start | bytes 6144008 | tf_op jit(solution)/shard_map/ppermute | solution.py:21
  118.9 1.4 convert_reduce_fusion.1
  120.4 0.6 broadcast_in_dim.45
  121.0 3.4 %all-to-all-start.2 = ((f32[16,8,128]{2,1,0:T(8,128)}), f32[16,8,128]{2,1,0:T(8,128)S(1)}, u32[]{:S(2)}, u32[]{:S(2)}) async-start(f32[16,8,128]{2,1,0:T(8,128)} %broadcast_in_dim.45), calls=%async_computation.2 | async-start | bytes 131072 | tf_op jit(solution)/shard_map/all_to_all | solution.py:13
  124.4 1.0 maximum_convert_fusion
  125.5 6.7 %all-to-all-done.2 = f32[16,8,128]{2,1,0:T(8,128)S(1)} async-done(((f32[16,8,128]{2,1,0:T(8,128)}), f32[16,8,128]{2,1,0:T(8,128)S(1)}, u32[]{:S(2)}, u32[]{:S(2)}) %all-to-all-start.2) | async-done | bytes 65568 | tf_op jit(solution)/shard_map/all_to_all | solution.py:13
  132.4 0.8 broadcast_in_dim.46
  133.2 7.5 %all-to-all-start.3 = ((bf16[16,32,512]{2,1,0:T(8,128)(2,1)}), bf16[16,32,512]{2,1,0:T(8,128)(2,1)S(1)}, u32[]{:S(2)}, u32[]{:S(2)}) async-start(bf16[16,32,512]{2,1,0:T(8,128)(2,1)} %broadcast_in_dim.46), calls=%async_computation.3 | async-start | bytes 1048576 | tf_op jit(solution)/shard_map/all_to_all | solution.py:13
  140.8 1.4 fusion.4
  142.2 2.4 collective-permute-start.9
  144.5 0.5 fusion.7
  145.0 0.7 collective-permute-done.9
  145.7 1.7 fusion.1
  147.4 7.1 %all-to-all-done.3 = bf16[16,32,512]{2,1,0:T(8,128)(2,1)S(1)} async-done(((bf16[16,32,512]{2,1,0:T(8,128)(2,1)}), bf16[16,32,512]{2,1,0:T(8,128)(2,1)S(1)}, u32[]{:S(2)}, u32[]{:S(2)}) %all-to-all-start.3) | async-done | bytes 524320 | tf_op jit(solution)/shard_map/all_to_all | solution.py:13
  154.5 4.6 %collective-permute-start.11 = (bf16[8,32,512]{2,1,0:T(8,128)(2,1)S(1)}, bf16[8,32,512]{2,1,0:T(8,128)(2,1)S(1)}, u32[]{:S(2)}, u32[]{:S(2)}) collective-permute-start(bf16[8,32,512]{2,1,0:T(8,128)(2,1)S(1)} %select_bitcast_fusion.2), channel_id=1, source_target_pairs={{0,1},{1,0},{2,3},{3,2},{4,5},{5,4},{6,7},{7,6},{8,9},{9,8},{10,11... | collective-permute-start | bytes 786440 | tf_op jit(solution)/shard_map/ppermute | solution.py:21
  159.1 0.5 fusion.5
  159.6 0.7 collective-permute-done.11
  160.2 1.7 fusion.2
  161.9 1.3 pad_maximum_fusion.2
  163.2 3.6 %all-to-all-start.4 = ((f16[8,64,1000]{2,1,0:T(8,128)(2,1)}), f16[8,64,1000]{2,1,0:T(8,128)(2,1)S(1)}, u32[]{:S(2)}, u32[]{:S(2)}) async-start(f16[8,64,1000]{2,1,0:T(8,128)(2,1)} %pad_maximum_fusion.2), calls=%async_computation.4 | async-start | bytes 2097152 | tf_op jit(solution)/shard_map/all_to_all | solution.py:13
  166.8 0.7 fusion.24
  168.1 0.6 compare_convert_fusion
  168.7 27.2 %all-to-all-done.4 = f16[8,64,1000]{2,1,0:T(8,128)(2,1)S(1)} async-done(((f16[8,64,1000]{2,1,0:T(8,128)(2,1)}), f16[8,64,1000]{2,1,0:T(8,128)(2,1)S(1)}, u32[]{:S(2)}, u32[]{:S(2)}) %all-to-all-start.4) | async-done | bytes 1024032 | tf_op jit(solution)/shard_map/all_to_all | solution.py:13
  196.0 0.2 convert_reduce_fusion
  196.3 0.2 exponential_reduce_fusion
  196.8 0.1 fusion.20
  197.0 0.6 broadcast_in_dim.48
  197.6 4.5 %all-to-all-start.5 = ((f32[16,8,128]{2,1,0:T(8,128)}), f32[16,8,128]{2,1,0:T(8,128)S(1)}, u32[]{:S(2)}, u32[]{:S(2)}) async-start(f32[16,8,128]{2,1,0:T(8,128)} %broadcast_in_dim.48), calls=%async_computation.5 | async-start | bytes 131072 | tf_op jit(solution)/shard_map/all_to_all | solution.py:13
  202.2 7.3 %all-to-all-done.5 = f32[16,8,128]{2,1,0:T(8,128)S(1)} async-done(((f32[16,8,128]{2,1,0:T(8,128)}), f32[16,8,128]{2,1,0:T(8,128)S(1)}, u32[]{:S(2)}, u32[]{:S(2)}) %all-to-all-start.5) | async-done | bytes 65568 | tf_op jit(solution)/shard_map/all_to_all | solution.py:13
  209.8 1.1 broadcast_in_dim.50
  210.9 4.3 %all-to-all-start.6 = ((bf16[16,32,1000]{2,1,0:T(8,128)(2,1)}), bf16[16,32,1000]{2,1,0:T(8,128)(2,1)S(1)}, u32[]{:S(2)}, u32[]{:S(2)}) async-start(bf16[16,32,1000]{2,1,0:T(8,128)(2,1)} %bitcast.40), calls=%async_computation.6 | async-start | bytes 2097152 | tf_op jit(solution)/shard_map/all_to_all | solution.py:13
  215.2 4.8 %collective-permute-start.12 = (bf16[16,32,512]{2,1,0:T(8,128)(2,1)S(1)}, bf16[16,32,512]{2,1,0:T(8,128)(2,1)}, u32[]{:S(2)}, u32[]{:S(2)}) collective-permute-start(bf16[16,32,512]{2,1,0:T(8,128)(2,1)S(1)} %all-to-all-done.3), channel_id=1, source_target_pairs={{0,256},{256,0},{1,257},{257,1},{2,258},{258,2},{3,259},{259,3},{4... | collective-permute-start | bytes 1572872 | tf_op jit(solution)/shard_map/ppermute | solution.py:25
  220.0 21.6 %collective-permute-done.12 = bf16[16,32,512]{2,1,0:T(8,128)(2,1)} collective-permute-done((bf16[16,32,512]{2,1,0:T(8,128)(2,1)S(1)}, bf16[16,32,512]{2,1,0:T(8,128)(2,1)}, u32[]{:S(2)}, u32[]{:S(2)}) %collective-permute-start.12) | collective-permute-done | bytes 524320 | tf_op jit(solution)/shard_map/ppermute | solution.py:25
  241.6 1.1 broadcast_select_fusion.3
  242.8 3.6 %collective-permute-start.13 = (bf16[16,32,1000]{2,1,0:T(8,128)(2,1)S(1)}, bf16[16,32,1000]{2,1,0:T(8,128)(2,1)S(1)}, u32[]{:S(2)}, u32[]{:S(2)}) collective-permute-start(bf16[16,32,1000]{2,1,0:T(8,128)(2,1)S(1)} %all-to-all-done.6), channel_id=1, source_target_pairs={{0,1},{1,0},{2,3},{3,2},{4,5},{5,4},{6,7},{7,6},{8,9},{9,8},{10,11... | collective-permute-start | bytes 3072008 | tf_op jit(solution)/shard_map/ppermute | solution.py:21
  246.4 2.7 %collective-permute-start.14 = (f32[32]{0:T(128)S(1)}, f32[32]{0:T(128)S(1)}, u32[]{:S(2)}, u32[]{:S(2)}) collective-permute-start(f32[32]{0:T(128)S(1)} %multiply_reduce_fusion.2), channel_id=1, source_target_pairs={{0,256},{256,0},{1,257},{257,1},{2,258},{258,2},{3,259},{259,3},{4... | collective-permute-start | bytes 392 | tf_op jit(solution)/shard_map/ppermute | solution.py:25
  249.2 3.0 %collective-permute-done.14 = f32[32]{0:T(128)S(1)} collective-permute-done((f32[32]{0:T(128)S(1)}, f32[32]{0:T(128)S(1)}, u32[]{:S(2)}, u32[]{:S(2)}) %collective-permute-start.14) | collective-permute-done | bytes 160 | tf_op jit(solution)/shard_map/ppermute | solution.py:25
  252.2 1.2 maximum_multiply_fusion
  253.4 0.7 fusion.26
  254.2 1.7 fusion
  (65 shorter events, 1.8 us)
Async XLA Ops:
  0.6 52.1 %copy-start = (bf16[3,256,512]{2,1,0:T(8,128)(2,1)S(1)}, bf16[3,256,512]{2,1,0:T(8,128)(2,1)}, u32[]{:S(2)}) copy-start(bf16[3,256,512]{2,1,0:T(8,128)(2,1)} %param.8) | copy-start | bytes 2359300
  0.6 34.5 %copy-start.4 = (bf16[64,512]{1,0:T(8,128)(2,1)S(1)}, bf16[64,512]{1,0:T(8,128)(2,1)}, u32[]{:S(2)}) copy-start(bf16[64,512]{1,0:T(8,128)(2,1)} %param.10) | copy-start | bytes 196612
  29.6 22.8 %collective-permute-start.4 = (bf16[8,64,768]{2,1,0:T(8,128)(2,1)S(1)}, bf16[8,64,768]{2,1,0:T(8,128)(2,1)S(1)}, u32[]{:S(2)}, u32[]{:S(2)}) collective-permute-start(bf16[8,64,768]{2,1,0:T(8,128)(2,1)S(1)} %all_to_all.35), channel_id=1, source_target_pairs={{0,1},{1,0},{2,3},{3,2},{4,5},{5,4},{6,7},{7,6},{8,9},{9,8},{10,11... | collective-permute-start | bytes 2359304 | tf_op jit(solution)/shard_map/ppermute | solution.py:21
  35.1 12.4 %collective-permute-start = (bf16[1,32,512]{2,1,0:T(8,128)(2,1)S(1)}, bf16[1,32,512]{2,1,0:T(8,128)(2,1)S(1)}, u32[]{:S(2)}, u32[]{:S(2)}) collective-permute-start(bf16[1,32,512]{2,1,0:T(8,128)(2,1)S(1)} %select_bitcast_fusion.10), channel_id=1, source_target_pairs={{0,64},{16,80},{32,96},{48,112},{64,0},{80,16},{96,32},{112,48},{1... | collective-permute-start | bytes 98312 | tf_op jit(solution)/shard_map/ppermute | solution.py:38
  47.6 16.6 %collective-permute-start.1 = (bf16[2,32,512]{2,1,0:T(8,128)(2,1)S(1)}, bf16[2,32,512]{2,1,0:T(8,128)(2,1)S(1)}, u32[]{:S(2)}, u32[]{:S(2)}) collective-permute-start(bf16[2,32,512]{2,1,0:T(8,128)(2,1)S(1)} %maximum_bitcast_fusion), channel_id=1, source_target_pairs={{0,32},{16,48},{32,0},{48,16},{64,96},{80,112},{96,64},{112,80},{1... | collective-permute-start | bytes 196616 | tf_op jit(solution)/shard_map/ppermute | solution.py:38
  54.7 12.6 %copy-start.1 = (bf16[1,1000,512]{2,1,0:T(8,128)(2,1)S(1)}, bf16[1,1000,512]{2,1,0:T(8,128)(2,1)}, u32[]{:S(2)}) copy-start(bf16[1,1000,512]{2,1,0:T(8,128)(2,1)} %param.9) | copy-start | bytes 3072004
  54.7 64.1 %all-to-all-start.1 = ((f16[32,32,512]{2,1,0:T(8,128)(2,1)}), f16[32,32,512]{2,1,0:T(8,128)(2,1)}, u32[]{:S(2)}, u32[]{:S(2)}) async-start(f16[32,32,512]{2,1,0:T(8,128)(2,1)} %bitcast.18), calls=%async_computation.1 | async-start | bytes 2097152 | tf_op jit(solution)/shard_map/all_to_all | solution.py:13
  64.2 26.4 %collective-permute-start.2 = (bf16[4,32,512]{2,1,0:T(8,128)(2,1)S(1)}, bf16[4,32,512]{2,1,0:T(8,128)(2,1)S(1)}, u32[]{:S(2)}, u32[]{:S(2)}) collective-permute-start(bf16[4,32,512]{2,1,0:T(8,128)(2,1)S(1)} %bitcast.145), channel_id=1, source_target_pairs={{0,16},{16,0},{32,48},{48,32},{64,80},{80,64},{96,112},{112,96},{1... | collective-permute-start | bytes 393224 | tf_op jit(solution)/shard_map/ppermute | solution.py:38
  67.4 26.4 %collective-permute-start.5 = (bf16[500,512]{1,0:T(8,128)(2,1)S(1)}, bf16[500,512]{1,0:T(8,128)(2,1)}, u32[]{:S(2)}, u32[]{:S(2)}) collective-permute-start(bf16[500,512]{1,0:T(8,128)(2,1)S(1)} %get-tuple-element.12), channel_id=1, source_target_pairs={{0,128},{128,256},{256,384},{384,0},{1,129},{129,257},{257,385},{3... | collective-permute-start | bytes 1536008 | tf_op jit(solution)/shard_map/ppermute | solution.py:30
  70.5 25.5 %collective-permute-start.7 = (bf16[500,512]{1,0:T(8,128)(2,1)S(1)}, bf16[500,512]{1,0:T(8,128)(2,1)}, u32[]{:S(2)}, u32[]{:S(2)}) collective-permute-start(bf16[500,512]{1,0:T(8,128)(2,1)S(1)} %get-tuple-element.13), channel_id=1, source_target_pairs={{0,384},{128,0},{256,128},{384,256},{1,385},{129,1},{257,129},{385... | collective-permute-start | bytes 1536008 | tf_op jit(solution)/shard_map/ppermute | solution.py:30
  90.7 9.6 %collective-permute-start.3 = (bf16[8,32,512]{2,1,0:T(8,128)(2,1)S(1)}, bf16[8,32,512]{2,1,0:T(8,128)(2,1)S(1)}, u32[]{:S(2)}, u32[]{:S(2)}) collective-permute-start(bf16[8,32,512]{2,1,0:T(8,128)(2,1)S(1)} %bitcast.144), channel_id=1, source_target_pairs={{0,128},{128,0},{1,129},{129,1},{2,130},{130,2},{3,131},{131,3},{4... | collective-permute-start | bytes 786440 | tf_op jit(solution)/shard_map/ppermute | solution.py:44
  93.8 15.2 %collective-permute-start.6 = (bf16[500,512]{1,0:T(8,128)(2,1)}, bf16[500,512]{1,0:T(8,128)(2,1)S(1)}, u32[]{:S(2)}, u32[]{:S(2)}) collective-permute-start(bf16[500,512]{1,0:T(8,128)(2,1)} %collective-permute-done.5), channel_id=1, source_target_pairs={{0,128},{128,256},{256,384},{384,0},{1,129},{129,257},{257,385},{3... | collective-permute-start | bytes 1536008 | tf_op jit(solution)/shard_map/ppermute | solution.py:30
  96.0 13.5 %collective-permute-start.8 = (bf16[500,512]{1,0:T(8,128)(2,1)}, bf16[500,512]{1,0:T(8,128)(2,1)S(1)}, u32[]{:S(2)}, u32[]{:S(2)}) collective-permute-start(bf16[500,512]{1,0:T(8,128)(2,1)} %collective-permute-done.7), channel_id=1, source_target_pairs={{0,384},{128,0},{256,128},{384,256},{1,385},{129,1},{257,129},{385... | collective-permute-start | bytes 1536008 | tf_op jit(solution)/shard_map/ppermute | solution.py:30
  109.0 0.8 copy-start.2
  109.5 0.8 copy-start.3
  113.8 18.5 %copy-start.6 = (f32[512]{0:T(512)S(1)}, f32[512]{0:T(512)}, u32[]{:S(2)}) copy-start(f32[512]{0:T(512)} %param.12) | copy-start | bytes 6148
  113.8 31.2 %collective-permute-start.10 = (bf16[2,1000,512]{2,1,0:T(8,128)(2,1)}, bf16[2,1000,512]{2,1,0:T(8,128)(2,1)}, u32[]{:S(2)}, u32[]{:S(2)}) collective-permute-start(bf16[2,1000,512]{2,1,0:T(8,128)(2,1)} %pad_maximum_fusion), channel_id=1, source_target_pairs={{0,1},{1,0},{2,3},{3,2},{4,5},{5,4},{6,7},{7,6},{8,9},{9,8},{10,11... | collective-permute-start | bytes 6144008 | tf_op jit(solution)/shard_map/ppermute | solution.py:21
  120.3 20.5 %copy-start.5 = (f32[512]{0:T(512)S(1)}, f32[512]{0:T(512)}, u32[]{:S(2)}) copy-start(f32[512]{0:T(512)} %param.11) | copy-start | bytes 6148
  121.0 11.1 %all-to-all-start.2 = ((f32[16,8,128]{2,1,0:T(8,128)}), f32[16,8,128]{2,1,0:T(8,128)S(1)}, u32[]{:S(2)}, u32[]{:S(2)}) async-start(f32[16,8,128]{2,1,0:T(8,128)} %broadcast_in_dim.45), calls=%async_computation.2 | async-start | bytes 131072 | tf_op jit(solution)/shard_map/all_to_all | solution.py:13
  133.2 21.2 %all-to-all-start.3 = ((bf16[16,32,512]{2,1,0:T(8,128)(2,1)}), bf16[16,32,512]{2,1,0:T(8,128)(2,1)S(1)}, u32[]{:S(2)}, u32[]{:S(2)}) async-start(bf16[16,32,512]{2,1,0:T(8,128)(2,1)} %broadcast_in_dim.46), calls=%async_computation.3 | async-start | bytes 1048576 | tf_op jit(solution)/shard_map/all_to_all | solution.py:13
  142.2 3.5 %collective-permute-start.9 = (bf16[8,32,512]{2,1,0:T(8,128)(2,1)S(1)}, bf16[8,32,512]{2,1,0:T(8,128)(2,1)S(1)}, u32[]{:S(2)}, u32[]{:S(2)}) collective-permute-start(bf16[8,32,512]{2,1,0:T(8,128)(2,1)S(1)} %select_bitcast_fusion.3), channel_id=1, source_target_pairs={{0,1},{1,0},{2,3},{3,2},{4,5},{5,4},{6,7},{7,6},{8,9},{9,8},{10,11... | collective-permute-start | bytes 786440 | tf_op jit(solution)/shard_map/ppermute | solution.py:21
  154.5 5.7 %collective-permute-start.11 = (bf16[8,32,512]{2,1,0:T(8,128)(2,1)S(1)}, bf16[8,32,512]{2,1,0:T(8,128)(2,1)S(1)}, u32[]{:S(2)}, u32[]{:S(2)}) collective-permute-start(bf16[8,32,512]{2,1,0:T(8,128)(2,1)S(1)} %select_bitcast_fusion.2), channel_id=1, source_target_pairs={{0,1},{1,0},{2,3},{3,2},{4,5},{5,4},{6,7},{7,6},{8,9},{9,8},{10,11... | collective-permute-start | bytes 786440 | tf_op jit(solution)/shard_map/ppermute | solution.py:21
  161.9 4.9 %copy-start.7 = (s32[16]{0:T(128)S(1)}, s32[16]{0:T(128)}, u32[]{:S(2)}) copy-start(s32[16]{0:T(128)} %param.13) | copy-start | bytes 196
  163.2 32.8 %all-to-all-start.4 = ((f16[8,64,1000]{2,1,0:T(8,128)(2,1)}), f16[8,64,1000]{2,1,0:T(8,128)(2,1)S(1)}, u32[]{:S(2)}, u32[]{:S(2)}) async-start(f16[8,64,1000]{2,1,0:T(8,128)(2,1)} %pad_maximum_fusion.2), calls=%async_computation.4 | async-start | bytes 2097152 | tf_op jit(solution)/shard_map/all_to_all | solution.py:13
  197.6 11.9 %all-to-all-start.5 = ((f32[16,8,128]{2,1,0:T(8,128)}), f32[16,8,128]{2,1,0:T(8,128)S(1)}, u32[]{:S(2)}, u32[]{:S(2)}) async-start(f32[16,8,128]{2,1,0:T(8,128)} %broadcast_in_dim.48), calls=%async_computation.5 | async-start | bytes 131072 | tf_op jit(solution)/shard_map/all_to_all | solution.py:13
  210.9 31.9 %all-to-all-start.6 = ((bf16[16,32,1000]{2,1,0:T(8,128)(2,1)}), bf16[16,32,1000]{2,1,0:T(8,128)(2,1)S(1)}, u32[]{:S(2)}, u32[]{:S(2)}) async-start(bf16[16,32,1000]{2,1,0:T(8,128)(2,1)} %bitcast.40), calls=%async_computation.6 | async-start | bytes 2097152 | tf_op jit(solution)/shard_map/all_to_all | solution.py:13
  215.2 26.4 %collective-permute-start.12 = (bf16[16,32,512]{2,1,0:T(8,128)(2,1)S(1)}, bf16[16,32,512]{2,1,0:T(8,128)(2,1)}, u32[]{:S(2)}, u32[]{:S(2)}) collective-permute-start(bf16[16,32,512]{2,1,0:T(8,128)(2,1)S(1)} %all-to-all-done.3), channel_id=1, source_target_pairs={{0,256},{256,0},{1,257},{257,1},{2,258},{258,2},{3,259},{259,3},{4... | collective-permute-start | bytes 1572872 | tf_op jit(solution)/shard_map/ppermute | solution.py:25
  242.8 11.4 %collective-permute-start.13 = (bf16[16,32,1000]{2,1,0:T(8,128)(2,1)S(1)}, bf16[16,32,1000]{2,1,0:T(8,128)(2,1)S(1)}, u32[]{:S(2)}, u32[]{:S(2)}) collective-permute-start(bf16[16,32,1000]{2,1,0:T(8,128)(2,1)S(1)} %all-to-all-done.6), channel_id=1, source_target_pairs={{0,1},{1,0},{2,3},{3,2},{4,5},{5,4},{6,7},{7,6},{8,9},{9,8},{10,11... | collective-permute-start | bytes 3072008 | tf_op jit(solution)/shard_map/ppermute | solution.py:21
  246.4 5.8 %collective-permute-start.14 = (f32[32]{0:T(128)S(1)}, f32[32]{0:T(128)S(1)}, u32[]{:S(2)}, u32[]{:S(2)}) collective-permute-start(f32[32]{0:T(128)S(1)} %multiply_reduce_fusion.2), channel_id=1, source_target_pairs={{0,256},{256,0},{1,257},{257,1},{2,258},{258,2},{3,259},{259,3},{4... | collective-permute-start | bytes 392 | tf_op jit(solution)/shard_map/ppermute | solution.py:25

commit v8 on v7

--- a/solution.py
+++ b/solution.py
@@ -72,13 +72,10 @@
     first_half = along_x(first_half, 1)
     second_half = along_x(second_half, -1)
     other_heads = jnp.concatenate([first_half, second_half])
-    both_heads = jnp.stack(
-        [
-            jnp.where(is_target, own_heads, other_heads),
-            jnp.where(is_target, other_heads, own_heads),
-        ]
-    )
-    core_heads = from_other_core(both_heads)
+    target_head = jnp.where(is_target, own_heads, other_heads)
+    draft_head = jnp.where(is_target, other_heads, own_heads)
+    core_target_head = from_other_core(target_head)
+    core_draft_head = from_other_core(draft_head)
 
     hidden_part = jnp.where(is_target, final_hidden[:part], final_hidden[part:])
     hidden_rows = doubled(hidden_part).astype(f32)
@@ -120,11 +117,11 @@
 
     kept, given = split_by_core(target_rows)
     taken = from_other_core(given)
-    target_partial = (share_of(kept, both_heads[0]) + share_of(taken, core_heads[0])).astype(half)
-    kept, given = split_by_core(draft_rows)
-    taken = from_other_core(given)
-    own_share = share_of(kept, both_heads[1])
-    draft_partial = (own_share + share_of(taken, core_heads[1])).astype(half)
+    target_partial = (share_of(kept, target_head) + share_of(taken, core_target_head)).astype(half)
+    core_rows = from_other_core(draft_rows)
+    kept, taken = split_by_core(draft_rows)[0], split_by_core(core_rows)[0]
+    own_share = share_of(kept, draft_head)
+    draft_partial = (own_share + share_of(taken, core_draft_head)).astype(half)
     partials = jnp.concatenate([target_partial, draft_partial], axis=1)
     partials = exchanged(partials, "y")
     logits = jnp.sum(partials.astype(f32), axis=0).reshape(2, part, vocab)

time: 257 us -> 259 us (level)
  starting transfers between devices: 95.8 us -> 101 us
  waiting for transfers between devices: 102 us -> 98.6 us
  other arithmetic: 14.3 us -> 11.2 us
  matrix products: 8.71 us -> 11.4 us
    ppermute x3, waiting for transfers between devices: 18.4 us -> 25.3 us  [doubled(): other = lax.ppermute(pieces, 'z', pairs)]
    all_to_all x6, waiting for transfers between devices: 48.3 us -> 42.6 us  [exchanged(): return lax.all_to_all(tiles, axes, split_axis=0, concat_axis=0, tiled=True)]
    all_to_all x6, starting transfers between devices: 32.6 us -> 37 us  [exchanged(): return lax.all_to_all(tiles, axes, split_axis=0, concat_axis=0, tiled=True)]
    ppermute x4, waiting for transfers between devices: 8.86 us -> 5.74 us  [along_x(): lax.ppermute(shard, ('grp', 'xl'), [(i, (i + step) % n) for i in range(n)])]
    dot_general x4, matrix products: 4.3 us -> 7.05 us  [share_of(): return jnp.einsum('ytd,vd->ytv', rows, head, preferred_element_type=f32)]
    ppermute x5 -> x6, starting transfers between devices: 21 us -> 23.5 us  [from_other_core(): return lax.ppermute(shard, 'core', [(0, 1), (1, 0)])]
  transfers between devices with their start and end apart: 21 -> 22, of which waited for: 12 -> 8; matrix products, arithmetic and copies ran while one was open for 7% -> 8% of each run, Pallas kernels for 0% -> 0%
where the time goes in v8:
time: 259 us; the launch traced here: 258 us
  starting transfers between devices  101 us (39%)
  waiting for transfers between devices  98.6 us (38%)
  blocking collectives  27.9 us (11%)
  matrix products  11.4 us (4%)
  other arithmetic  11.2 us (4%)
  local copies, waits for them, and re-layouts  5.78 us (2%)
    all_to_all x6, waiting for transfers between devices, exchanged(): return lax.all_to_all(tiles, axes, split_axis=0, concat_axis=0, tiled=True)  42.6 us
    all_to_all x6, starting transfers between devices, exchanged(): return lax.all_to_all(tiles, axes, split_axis=0, concat_axis=0, tiled=True)  37 us
    all_to_all x1, blocking collectives, exchanged(): return lax.all_to_all(tiles, axes, split_axis=0, concat_axis=0, tiled=True)  27.9 us
    ppermute x3, waiting for transfers between devices, doubled(): other = lax.ppermute(pieces, 'z', pairs)  25.3 us
    ppermute x2, waiting for transfers between devices, from_other_group(): return lax.ppermute(shard, 'grp', [(0, 1), (1, 0)])  24.9 us
    ppermute x6, starting transfers between devices, from_other_core(): return lax.ppermute(shard, 'core', [(0, 1), (1, 0)])  23.5 us
    ppermute x3, starting transfers between devices, doubled(): other = lax.ppermute(pieces, 'z', pairs)  17.1 us
    ppermute x4, starting transfers between devices, along_x(): lax.ppermute(shard, ('grp', 'xl'), [(i, (i + step) % n) for i in range(n)])  13.3 us
  transfers between devices with their start and end apart: 22, of which 8 were waited for; matrix products, arithmetic and copies ran while one was open for 8% of the time, Pallas kernels for 0%

profile of v8, /device:TPU:1, one launch (start us, length us, event | category | flops | bytes accessed | tf_op | source)
XLA Modules:
  0.0 257.6 jit_solution(1517572441067500424)
XLA Ops:
  0.7 1.0 copy.75
  1.7 27.9 %all_to_all.35 = bf16[8,64,768]{2,1,0:T(8,128)(2,1)S(1)} all-to-all(bf16[8,64,768]{2,1,0:T(8,128)(2,1)S(1)} %broadcast_in_dim.43), channel_id=1, replica_groups=mesh['grp'=2,'xl'=2,'z'=8,'y'=8,'core'=2] {'y'}, dimensions={0} | all-to-all | bytes 1572864 | tf_op jit(solution)/shard_map/all_to_all | solution.py:13
  29.6 5.5 %collective-permute-start.4 = (bf16[8,64,768]{2,1,0:T(8,128)(2,1)S(1)}, bf16[8,64,768]{2,1,0:T(8,128)(2,1)S(1)}, u32[]{:S(2)}, u32[]{:S(2)}) collective-permute-start(bf16[8,64,768]{2,1,0:T(8,128)(2,1)S(1)} %all_to_all.35), channel_id=1, source_target_pairs={{0,1},{1,0},{2,3},{3,2},{4,5},{5,4},{6,7},{7,6},{8,9},{9,8},{10,11... | collective-permute-start | bytes 2359304 | tf_op jit(solution)/shard_map/ppermute | solution.py:21
  35.1 10.6 %collective-permute-start = (bf16[1,32,512]{2,1,0:T(8,128)(2,1)S(1)}, bf16[1,32,512]{2,1,0:T(8,128)(2,1)S(1)}, u32[]{:S(2)}, u32[]{:S(2)}) collective-permute-start(bf16[1,32,512]{2,1,0:T(8,128)(2,1)S(1)} %select_bitcast_fusion.9), channel_id=1, source_target_pairs={{0,64},{16,80},{32,96},{48,112},{64,0},{80,16},{96,32},{112,48},{1... | collective-permute-start | bytes 98312 | tf_op jit(solution)/shard_map/ppermute | solution.py:38
  45.8 0.1 select_bitcast_fusion.1
  45.9 0.1 pad_maximum_fusion
  46.1 2.0 convolution_convert_fusion
  48.1 7.3 %all-to-all-start.1 = ((f16[32,32,512]{2,1,0:T(8,128)(2,1)}), f16[32,32,512]{2,1,0:T(8,128)(2,1)S(1)}, u32[]{:S(2)}, u32[]{:S(2)}) async-start(f16[32,32,512]{2,1,0:T(8,128)(2,1)} %bitcast.154), calls=%async_computation.1 | async-start | bytes 2097152 | tf_op jit(solution)/shard_map/all_to_all | solution.py:13
  55.4 4.0 %collective-permute-start.1 = (bf16[2,32,512]{2,1,0:T(8,128)(2,1)S(1)}, bf16[2,32,512]{2,1,0:T(8,128)(2,1)S(1)}, u32[]{:S(2)}, u32[]{:S(2)}) collective-permute-start(bf16[2,32,512]{2,1,0:T(8,128)(2,1)S(1)} %maximum_bitcast_fusion), channel_id=1, source_target_pairs={{0,32},{16,48},{32,0},{48,16},{64,96},{80,112},{96,64},{112,80},{1... | collective-permute-start | bytes 196616 | tf_op jit(solution)/shard_map/ppermute | solution.py:38
  59.4 22.0 %collective-permute-done.1 = bf16[2,32,512]{2,1,0:T(8,128)(2,1)S(1)} collective-permute-done((bf16[2,32,512]{2,1,0:T(8,128)(2,1)S(1)}, bf16[2,32,512]{2,1,0:T(8,128)(2,1)S(1)}, u32[]{:S(2)}, u32[]{:S(2)}) %collective-permute-start.1) | collective-permute-done | bytes 65568 | tf_op jit(solution)/shard_map/ppermute | solution.py:38
  81.4 2.4 collective-permute-start.2
  83.9 3.3 %collective-permute-done.2 = bf16[4,32,512]{2,1,0:T(8,128)(2,1)S(1)} collective-permute-done((bf16[4,32,512]{2,1,0:T(8,128)(2,1)S(1)}, bf16[4,32,512]{2,1,0:T(8,128)(2,1)S(1)}, u32[]{:S(2)}, u32[]{:S(2)}) %collective-permute-start.2) | collective-permute-done | bytes 131104 | tf_op jit(solution)/shard_map/ppermute | solution.py:38
  87.3 2.6 %collective-permute-start.3 = (bf16[8,32,512]{2,1,0:T(8,128)(2,1)S(1)}, bf16[8,32,512]{2,1,0:T(8,128)(2,1)}, u32[]{:S(2)}, u32[]{:S(2)}) collective-permute-start(bf16[8,32,512]{2,1,0:T(8,128)(2,1)S(1)} %bitcast.155), channel_id=1, source_target_pairs={{0,128},{128,0},{1,129},{129,1},{2,130},{130,2},{3,131},{131,3},{4... | collective-permute-start | bytes 786440 | tf_op jit(solution)/shard_map/ppermute | solution.py:44
  89.9 1.1 slice_bitcast_fusion.1
  91.0 2.7 %collective-permute-start.5 = (bf16[500,512]{1,0:T(8,128)(2,1)}, bf16[500,512]{1,0:T(8,128)(2,1)}, u32[]{:S(2)}, u32[]{:S(2)}) collective-permute-start(bf16[500,512]{1,0:T(8,128)(2,1)} %get-tuple-element.12), channel_id=1, source_target_pairs={{0,128},{128,256},{256,384},{384,0},{1,129},{129,257},{257,385},{3... | collective-permute-start | bytes 1536008 | tf_op jit(solution)/shard_map/ppermute | solution.py:30
  93.7 3.8 %collective-permute-start.7 = (bf16[500,512]{1,0:T(8,128)(2,1)}, bf16[500,512]{1,0:T(8,128)(2,1)}, u32[]{:S(2)}, u32[]{:S(2)}) collective-permute-start(bf16[500,512]{1,0:T(8,128)(2,1)} %get-tuple-element.13), channel_id=1, source_target_pairs={{0,384},{128,0},{256,128},{384,256},{1,385},{129,1},{257,129},{385... | collective-permute-start | bytes 1536008 | tf_op jit(solution)/shard_map/ppermute | solution.py:30
  97.5 1.1 broadcast_select_fusion.5
  98.6 5.7 %collective-permute-done.5 = bf16[500,512]{1,0:T(8,128)(2,1)} collective-permute-done((bf16[500,512]{1,0:T(8,128)(2,1)}, bf16[500,512]{1,0:T(8,128)(2,1)}, u32[]{:S(2)}, u32[]{:S(2)}) %collective-permute-start.5) | collective-permute-done | bytes 512032 | tf_op jit(solution)/shard_map/ppermute | solution.py:30
  104.3 4.1 %collective-permute-start.6 = (bf16[500,512]{1,0:T(8,128)(2,1)}, bf16[500,512]{1,0:T(8,128)(2,1)}, u32[]{:S(2)}, u32[]{:S(2)}) collective-permute-start(bf16[500,512]{1,0:T(8,128)(2,1)} %collective-permute-done.5), channel_id=1, source_target_pairs={{0,128},{128,256},{256,384},{384,0},{1,129},{129,257},{257,385},{3... | collective-permute-start | bytes 1536008 | tf_op jit(solution)/shard_map/ppermute | solution.py:30
  108.4 2.7 %collective-permute-start.8 = (bf16[500,512]{1,0:T(8,128)(2,1)}, bf16[500,512]{1,0:T(8,128)(2,1)}, u32[]{:S(2)}, u32[]{:S(2)}) collective-permute-start(bf16[500,512]{1,0:T(8,128)(2,1)} %collective-permute-done.7), channel_id=1, source_target_pairs={{0,384},{128,0},{256,128},{384,256},{1,385},{129,1},{257,129},{385... | collective-permute-start | bytes 1536008 | tf_op jit(solution)/shard_map/ppermute | solution.py:30
  111.2 0.2 multiply_reduce_fusion
  111.4 0.2 convert_reduce_fusion.1
  111.6 0.1 multiply_reduce_fusion.1
  111.7 0.6 broadcast_in_dim.45
  112.4 8.1 %all-to-all-start.2 = ((f32[16,8,128]{2,1,0:T(8,128)}), f32[16,8,128]{2,1,0:T(8,128)S(1)}, u32[]{:S(2)}, u32[]{:S(2)}) async-start(f32[16,8,128]{2,1,0:T(8,128)} %broadcast_in_dim.45), calls=%async_computation.2 | async-start | bytes 131072 | tf_op jit(solution)/shard_map/all_to_all | solution.py:13
  120.5 2.9 %bitcast_select_fusion.1 = (bf16[1000,512]{1,0:T(8,128)(2,1)}, bf16[1000,512]{1,0:T(8,128)(2,1)}) fusion(bf16[1,1000,512]{2,1,0:T(8,128)(2,1)S(1)} %copy-done.1, pred[]{:T(512)S(6)} %eq.24, bf16[500,512]{1,0:T(8,128)(2,1)} %collective-permute-done.8, bf16[500,512]{1,0:T(8,128)(2,1)} %collective-permute-done.6), kind=kLoop, calls=%fused_computation.24 | loop fusion | flops 3072000 | bytes 4096001 | tf_op jit(solution)/shard_map/jit(_where)/select_n | solution.py:75
  123.5 6.3 %collective-permute-start.10 = (bf16[1000,512]{1,0:T(8,128)(2,1)}, bf16[1000,512]{1,0:T(8,128)(2,1)}, u32[]{:S(2)}, u32[]{:S(2)}) collective-permute-start(bf16[1000,512]{1,0:T(8,128)(2,1)} %get-tuple-element.4), channel_id=1, source_target_pairs={{0,1},{1,0},{2,3},{3,2},{4,5},{5,4},{6,7},{7,6},{8,9},{9,8},{10,11... | collective-permute-start | bytes 3072008 | tf_op jit(solution)/shard_map/ppermute | solution.py:21
  129.9 0.8 broadcast_in_dim.46
  130.7 8.7 %all-to-all-start.3 = ((bf16[16,32,512]{2,1,0:T(8,128)(2,1)}), bf16[16,32,512]{2,1,0:T(8,128)(2,1)}, u32[]{:S(2)}, u32[]{:S(2)}) async-start(bf16[16,32,512]{2,1,0:T(8,128)(2,1)} %broadcast_in_dim.46), calls=%async_computation.3 | async-start | bytes 1048576 | tf_op jit(solution)/shard_map/all_to_all | solution.py:13
  139.6 2.2 collective-permute-start.12
  141.9 0.2 fusion.4
  142.1 2.1 collective-permute-start.9
  144.2 1.8 fusion.9
  146.0 8.0 %all-to-all-done.3 = bf16[16,32,512]{2,1,0:T(8,128)(2,1)} async-done(((bf16[16,32,512]{2,1,0:T(8,128)(2,1)}), bf16[16,32,512]{2,1,0:T(8,128)(2,1)}, u32[]{:S(2)}, u32[]{:S(2)}) %all-to-all-start.3) | async-done | bytes 524320 | tf_op jit(solution)/shard_map/all_to_all | solution.py:13
  154.0 3.9 %collective-permute-start.11 = (bf16[16,32,512]{2,1,0:T(8,128)(2,1)}, bf16[16,32,512]{2,1,0:T(8,128)(2,1)S(1)}, u32[]{:S(2)}, u32[]{:S(2)}) collective-permute-start(bf16[16,32,512]{2,1,0:T(8,128)(2,1)} %all-to-all-done.3), channel_id=1, source_target_pairs={{0,1},{1,0},{2,3},{3,2},{4,5},{5,4},{6,7},{7,6},{8,9},{9,8},{10,11... | collective-permute-start | bytes 1572872 | tf_op jit(solution)/shard_map/ppermute | solution.py:21
  157.8 1.7 fusion.1
  159.5 1.9 fusion.6
  161.5 1.7 fusion.2
  163.2 1.3 pad_maximum_fusion.1
  164.5 3.6 %all-to-all-start.4 = ((f16[8,64,1000]{2,1,0:T(8,128)(2,1)}), f16[8,64,1000]{2,1,0:T(8,128)(2,1)S(1)}, u32[]{:S(2)}, u32[]{:S(2)}) async-start(f16[8,64,1000]{2,1,0:T(8,128)(2,1)} %pad_maximum_fusion.1), calls=%async_computation.4 | async-start | bytes 2097152 | tf_op jit(solution)/shard_map/all_to_all | solution.py:13
  168.0 0.6 fusion.37
  169.3 0.6 compare_convert_fusion
  169.9 27.3 %all-to-all-done.4 = f16[8,64,1000]{2,1,0:T(8,128)(2,1)S(1)} async-done(((f16[8,64,1000]{2,1,0:T(8,128)(2,1)}), f16[8,64,1000]{2,1,0:T(8,128)(2,1)S(1)}, u32[]{:S(2)}, u32[]{:S(2)}) %all-to-all-start.4) | async-done | bytes 1024032 | tf_op jit(solution)/shard_map/all_to_all | solution.py:13
  197.2 0.2 convert_reduce_fusion
  197.5 0.1 reduce_max.20
  197.6 0.2 exponential_reduce_fusion
  198.0 0.1 broadcast_subtract_fusion
  198.1 0.1 fusion.31
  198.2 0.6 broadcast_in_dim.48
  198.8 4.6 %all-to-all-start.5 = ((f32[16,8,128]{2,1,0:T(8,128)}), f32[16,8,128]{2,1,0:T(8,128)S(1)}, u32[]{:S(2)}, u32[]{:S(2)}) async-start(f32[16,8,128]{2,1,0:T(8,128)} %broadcast_in_dim.48), calls=%async_computation.5 | async-start | bytes 131072 | tf_op jit(solution)/shard_map/all_to_all | solution.py:13
  203.5 7.3 %all-to-all-done.5 = f32[16,8,128]{2,1,0:T(8,128)S(1)} async-done(((f32[16,8,128]{2,1,0:T(8,128)}), f32[16,8,128]{2,1,0:T(8,128)S(1)}, u32[]{:S(2)}, u32[]{:S(2)}) %all-to-all-start.5) | async-done | bytes 65568 | tf_op jit(solution)/shard_map/all_to_all | solution.py:13
  210.8 0.1 exponential_divide_fusion
  211.1 1.1 broadcast_in_dim.50
  212.2 4.7 %all-to-all-start.6 = ((bf16[16,32,1000]{2,1,0:T(8,128)(2,1)}), bf16[16,32,1000]{2,1,0:T(8,128)(2,1)S(1)}, u32[]{:S(2)}, u32[]{:S(2)}) async-start(bf16[16,32,1000]{2,1,0:T(8,128)(2,1)} %bitcast.40), calls=%async_computation.6 | async-start | bytes 2097152 | tf_op jit(solution)/shard_map/all_to_all | solution.py:13
  216.9 4.8 %collective-permute-start.13 = (bf16[16,32,512]{2,1,0:T(8,128)(2,1)}, bf16[16,32,512]{2,1,0:T(8,128)(2,1)S(1)}, u32[]{:S(2)}, u32[]{:S(2)}) collective-permute-start(bf16[16,32,512]{2,1,0:T(8,128)(2,1)} %all-to-all-done.3), channel_id=1, source_target_pairs={{0,256},{256,0},{1,257},{257,1},{2,258},{258,2},{3,259},{259,3},{4... | collective-permute-start | bytes 1572872 | tf_op jit(solution)/shard_map/ppermute | solution.py:25
  221.7 21.7 %collective-permute-done.13 = bf16[16,32,512]{2,1,0:T(8,128)(2,1)S(1)} collective-permute-done((bf16[16,32,512]{2,1,0:T(8,128)(2,1)}, bf16[16,32,512]{2,1,0:T(8,128)(2,1)S(1)}, u32[]{:S(2)}, u32[]{:S(2)}) %collective-permute-start.13) | collective-permute-done | bytes 524320 | tf_op jit(solution)/shard_map/ppermute | solution.py:25
  243.4 1.1 broadcast_select_fusion.1
  244.6 3.6 %collective-permute-start.14 = (bf16[16,32,1000]{2,1,0:T(8,128)(2,1)S(1)}, bf16[16,32,1000]{2,1,0:T(8,128)(2,1)S(1)}, u32[]{:S(2)}, u32[]{:S(2)}) collective-permute-start(bf16[16,32,1000]{2,1,0:T(8,128)(2,1)S(1)} %all-to-all-done.6), channel_id=1, source_target_pairs={{0,1},{1,0},{2,3},{3,2},{4,5},{5,4},{6,7},{7,6},{8,9},{9,8},{10,11... | collective-permute-start | bytes 3072008 | tf_op jit(solution)/shard_map/ppermute | solution.py:21
  248.2 2.5 collective-permute-start.15
  250.7 0.1 broadcast_select_fusion.2
  250.8 3.2 %collective-permute-done.15 = f32[32]{0:T(128)S(1)} collective-permute-done((f32[32]{0:T(128)S(1)}, f32[32]{0:T(128)S(1)}, u32[]{:S(2)}, u32[]{:S(2)}) %collective-permute-start.15) | collective-permute-done | bytes 160 | tf_op jit(solution)/shard_map/ppermute | solution.py:25
  254.1 1.2 maximum_multiply_fusion
  255.2 0.7 fusion.39
  255.9 1.7 fusion
  (63 shorter events, 1.1 us)
Async XLA Ops:
  0.6 45.5 %copy-start = (bf16[3,256,512]{2,1,0:T(8,128)(2,1)S(1)}, bf16[3,256,512]{2,1,0:T(8,128)(2,1)}, u32[]{:S(2)}) copy-start(bf16[3,256,512]{2,1,0:T(8,128)(2,1)} %param.8) | copy-start | bytes 2359300
  0.6 34.5 %copy-start.3 = (bf16[64,512]{1,0:T(8,128)(2,1)S(1)}, bf16[64,512]{1,0:T(8,128)(2,1)}, u32[]{:S(2)}) copy-start(bf16[64,512]{1,0:T(8,128)(2,1)} %param.10) | copy-start | bytes 196612
  29.6 16.2 %collective-permute-start.4 = (bf16[8,64,768]{2,1,0:T(8,128)(2,1)S(1)}, bf16[8,64,768]{2,1,0:T(8,128)(2,1)S(1)}, u32[]{:S(2)}, u32[]{:S(2)}) collective-permute-start(bf16[8,64,768]{2,1,0:T(8,128)(2,1)S(1)} %all_to_all.35), channel_id=1, source_target_pairs={{0,1},{1,0},{2,3},{3,2},{4,5},{5,4},{6,7},{7,6},{8,9},{9,8},{10,11... | collective-permute-start | bytes 2359304 | tf_op jit(solution)/shard_map/ppermute | solution.py:21
  35.1 20.2 %collective-permute-start = (bf16[1,32,512]{2,1,0:T(8,128)(2,1)S(1)}, bf16[1,32,512]{2,1,0:T(8,128)(2,1)S(1)}, u32[]{:S(2)}, u32[]{:S(2)}) collective-permute-start(bf16[1,32,512]{2,1,0:T(8,128)(2,1)S(1)} %select_bitcast_fusion.9), channel_id=1, source_target_pairs={{0,64},{16,80},{32,96},{48,112},{64,0},{80,16},{96,32},{112,48},{1... | collective-permute-start | bytes 98312 | tf_op jit(solution)/shard_map/ppermute | solution.py:38
  48.0 41.8 %copy-start.1 = (bf16[1,1000,512]{2,1,0:T(8,128)(2,1)S(1)}, bf16[1,1000,512]{2,1,0:T(8,128)(2,1)}, u32[]{:S(2)}) copy-start(bf16[1,1000,512]{2,1,0:T(8,128)(2,1)} %param.9) | copy-start | bytes 3072004
  48.1 63.4 %all-to-all-start.1 = ((f16[32,32,512]{2,1,0:T(8,128)(2,1)}), f16[32,32,512]{2,1,0:T(8,128)(2,1)S(1)}, u32[]{:S(2)}, u32[]{:S(2)}) async-start(f16[32,32,512]{2,1,0:T(8,128)(2,1)} %bitcast.154), calls=%async_computation.1 | async-start | bytes 2097152 | tf_op jit(solution)/shard_map/all_to_all | solution.py:13
  55.4 26.0 %collective-permute-start.1 = (bf16[2,32,512]{2,1,0:T(8,128)(2,1)S(1)}, bf16[2,32,512]{2,1,0:T(8,128)(2,1)S(1)}, u32[]{:S(2)}, u32[]{:S(2)}) collective-permute-start(bf16[2,32,512]{2,1,0:T(8,128)(2,1)S(1)} %maximum_bitcast_fusion), channel_id=1, source_target_pairs={{0,32},{16,48},{32,0},{48,16},{64,96},{80,112},{96,64},{112,80},{1... | collective-permute-start | bytes 196616 | tf_op jit(solution)/shard_map/ppermute | solution.py:38
  81.4 5.7 %collective-permute-start.2 = (bf16[4,32,512]{2,1,0:T(8,128)(2,1)S(1)}, bf16[4,32,512]{2,1,0:T(8,128)(2,1)S(1)}, u32[]{:S(2)}, u32[]{:S(2)}) collective-permute-start(bf16[4,32,512]{2,1,0:T(8,128)(2,1)S(1)} %bitcast.156), channel_id=1, source_target_pairs={{0,16},{16,0},{32,48},{48,32},{64,80},{80,64},{96,112},{112,96},{1... | collective-permute-start | bytes 393224 | tf_op jit(solution)/shard_map/ppermute | solution.py:38
  87.3 10.2 %copy-start.2 = (bf16[4,2,32,512]{3,2,1,0:T(8,128)(2,1)}, bf16[4,2,32,512]{3,2,1,0:T(8,128)(2,1)S(1)}, u32[]{:S(2)}) copy-start(bf16[4,2,32,512]{3,2,1,0:T(8,128)(2,1)S(1)} %copy.50) | copy-start | bytes 786436
  87.3 10.2 %collective-permute-start.3 = (bf16[8,32,512]{2,1,0:T(8,128)(2,1)S(1)}, bf16[8,32,512]{2,1,0:T(8,128)(2,1)}, u32[]{:S(2)}, u32[]{:S(2)}) collective-permute-start(bf16[8,32,512]{2,1,0:T(8,128)(2,1)S(1)} %bitcast.155), channel_id=1, source_target_pairs={{0,128},{128,0},{1,129},{129,1},{2,130},{130,2},{3,131},{131,3},{4... | collective-permute-start | bytes 786440 | tf_op jit(solution)/shard_map/ppermute | solution.py:44
  91.0 13.3 %collective-permute-start.5 = (bf16[500,512]{1,0:T(8,128)(2,1)}, bf16[500,512]{1,0:T(8,128)(2,1)}, u32[]{:S(2)}, u32[]{:S(2)}) collective-permute-start(bf16[500,512]{1,0:T(8,128)(2,1)} %get-tuple-element.12), channel_id=1, source_target_pairs={{0,128},{128,256},{256,384},{384,0},{1,129},{129,257},{257,385},{3... | collective-permute-start | bytes 1536008 | tf_op jit(solution)/shard_map/ppermute | solution.py:30
  93.7 14.8 %collective-permute-start.7 = (bf16[500,512]{1,0:T(8,128)(2,1)}, bf16[500,512]{1,0:T(8,128)(2,1)}, u32[]{:S(2)}, u32[]{:S(2)}) collective-permute-start(bf16[500,512]{1,0:T(8,128)(2,1)} %get-tuple-element.13), channel_id=1, source_target_pairs={{0,384},{128,0},{256,128},{384,256},{1,385},{129,1},{257,129},{385... | collective-permute-start | bytes 1536008 | tf_op jit(solution)/shard_map/ppermute | solution.py:30
  104.3 16.2 %collective-permute-start.6 = (bf16[500,512]{1,0:T(8,128)(2,1)}, bf16[500,512]{1,0:T(8,128)(2,1)}, u32[]{:S(2)}, u32[]{:S(2)}) collective-permute-start(bf16[500,512]{1,0:T(8,128)(2,1)} %collective-permute-done.5), channel_id=1, source_target_pairs={{0,128},{128,256},{256,384},{384,0},{1,129},{129,257},{257,385},{3... | collective-permute-start | bytes 1536008 | tf_op jit(solution)/shard_map/ppermute | solution.py:30
  108.4 12.1 %collective-permute-start.8 = (bf16[500,512]{1,0:T(8,128)(2,1)}, bf16[500,512]{1,0:T(8,128)(2,1)}, u32[]{:S(2)}, u32[]{:S(2)}) collective-permute-start(bf16[500,512]{1,0:T(8,128)(2,1)} %collective-permute-done.7), channel_id=1, source_target_pairs={{0,384},{128,0},{256,128},{384,256},{1,385},{129,1},{257,129},{385... | collective-permute-start | bytes 1536008 | tf_op jit(solution)/shard_map/ppermute | solution.py:30
  112.4 17.4 %all-to-all-start.2 = ((f32[16,8,128]{2,1,0:T(8,128)}), f32[16,8,128]{2,1,0:T(8,128)S(1)}, u32[]{:S(2)}, u32[]{:S(2)}) async-start(f32[16,8,128]{2,1,0:T(8,128)} %broadcast_in_dim.45), calls=%async_computation.2 | async-start | bytes 131072 | tf_op jit(solution)/shard_map/all_to_all | solution.py:13
  120.5 9.3 %copy-start.5 = (f32[512]{0:T(512)S(1)}, f32[512]{0:T(512)}, u32[]{:S(2)}) copy-start(f32[512]{0:T(512)} %param.12) | copy-start | bytes 6148
  123.5 18.4 %copy-start.4 = (f32[512]{0:T(512)S(1)}, f32[512]{0:T(512)}, u32[]{:S(2)}) copy-start(f32[512]{0:T(512)} %param.11) | copy-start | bytes 6148
  123.5 34.4 %collective-permute-start.10 = (bf16[1000,512]{1,0:T(8,128)(2,1)}, bf16[1000,512]{1,0:T(8,128)(2,1)}, u32[]{:S(2)}, u32[]{:S(2)}) collective-permute-start(bf16[1000,512]{1,0:T(8,128)(2,1)} %get-tuple-element.4), channel_id=1, source_target_pairs={{0,1},{1,0},{2,3},{3,2},{4,5},{5,4},{6,7},{7,6},{8,9},{9,8},{10,11... | collective-permute-start | bytes 3072008 | tf_op jit(solution)/shard_map/ppermute | solution.py:21
  130.7 23.2 %all-to-all-start.3 = ((bf16[16,32,512]{2,1,0:T(8,128)(2,1)}), bf16[16,32,512]{2,1,0:T(8,128)(2,1)}, u32[]{:S(2)}, u32[]{:S(2)}) async-start(bf16[16,32,512]{2,1,0:T(8,128)(2,1)} %broadcast_in_dim.46), calls=%async_computation.3 | async-start | bytes 1048576 | tf_op jit(solution)/shard_map/all_to_all | solution.py:13
  139.6 21.9 %collective-permute-start.12 = (bf16[1000,512]{1,0:T(8,128)(2,1)}, bf16[1000,512]{1,0:T(8,128)(2,1)}, u32[]{:S(2)}, u32[]{:S(2)}) collective-permute-start(bf16[1000,512]{1,0:T(8,128)(2,1)} %get-tuple-element.5), channel_id=1, source_target_pairs={{0,1},{1,0},{2,3},{3,2},{4,5},{5,4},{6,7},{7,6},{8,9},{9,8},{10,11... | collective-permute-start | bytes 3072008 | tf_op jit(solution)/shard_map/ppermute | solution.py:21
  142.1 15.8 %collective-permute-start.9 = (bf16[8,32,512]{2,1,0:T(8,128)(2,1)S(1)}, bf16[8,32,512]{2,1,0:T(8,128)(2,1)S(1)}, u32[]{:S(2)}, u32[]{:S(2)}) collective-permute-start(bf16[8,32,512]{2,1,0:T(8,128)(2,1)S(1)} %select_bitcast_fusion.2), channel_id=1, source_target_pairs={{0,1},{1,0},{2,3},{3,2},{4,5},{5,4},{6,7},{7,6},{8,9},{9,8},{10,11... | collective-permute-start | bytes 786440 | tf_op jit(solution)/shard_map/ppermute | solution.py:21
  154.0 7.5 %collective-permute-start.11 = (bf16[16,32,512]{2,1,0:T(8,128)(2,1)}, bf16[16,32,512]{2,1,0:T(8,128)(2,1)S(1)}, u32[]{:S(2)}, u32[]{:S(2)}) collective-permute-start(bf16[16,32,512]{2,1,0:T(8,128)(2,1)} %all-to-all-done.3), channel_id=1, source_target_pairs={{0,1},{1,0},{2,3},{3,2},{4,5},{5,4},{6,7},{7,6},{8,9},{9,8},{10,11... | collective-permute-start | bytes 1572872 | tf_op jit(solution)/shard_map/ppermute | solution.py:21
  163.2 4.8 %copy-start.6 = (s32[16]{0:T(128)S(1)}, s32[16]{0:T(128)}, u32[]{:S(2)}) copy-start(s32[16]{0:T(128)} %param.13) | copy-start | bytes 196
  164.5 32.8 %all-to-all-start.4 = ((f16[8,64,1000]{2,1,0:T(8,128)(2,1)}), f16[8,64,1000]{2,1,0:T(8,128)(2,1)S(1)}, u32[]{:S(2)}, u32[]{:S(2)}) async-start(f16[8,64,1000]{2,1,0:T(8,128)(2,1)} %pad_maximum_fusion.1), calls=%async_computation.4 | async-start | bytes 2097152 | tf_op jit(solution)/shard_map/all_to_all | solution.py:13
  198.8 11.9 %all-to-all-start.5 = ((f32[16,8,128]{2,1,0:T(8,128)}), f32[16,8,128]{2,1,0:T(8,128)S(1)}, u32[]{:S(2)}, u32[]{:S(2)}) async-start(f32[16,8,128]{2,1,0:T(8,128)} %broadcast_in_dim.48), calls=%async_computation.5 | async-start | bytes 131072 | tf_op jit(solution)/shard_map/all_to_all | solution.py:13
  212.2 32.4 %all-to-all-start.6 = ((bf16[16,32,1000]{2,1,0:T(8,128)(2,1)}), bf16[16,32,1000]{2,1,0:T(8,128)(2,1)S(1)}, u32[]{:S(2)}, u32[]{:S(2)}) async-start(bf16[16,32,1000]{2,1,0:T(8,128)(2,1)} %bitcast.40), calls=%async_computation.6 | async-start | bytes 2097152 | tf_op jit(solution)/shard_map/all_to_all | solution.py:13
  216.9 26.5 %collective-permute-start.13 = (bf16[16,32,512]{2,1,0:T(8,128)(2,1)}, bf16[16,32,512]{2,1,0:T(8,128)(2,1)S(1)}, u32[]{:S(2)}, u32[]{:S(2)}) collective-permute-start(bf16[16,32,512]{2,1,0:T(8,128)(2,1)} %all-to-all-done.3), channel_id=1, source_target_pairs={{0,256},{256,0},{1,257},{257,1},{2,258},{258,2},{3,259},{259,3},{4... | collective-permute-start | bytes 1572872 | tf_op jit(solution)/shard_map/ppermute | solution.py:25
  244.6 11.3 %collective-permute-start.14 = (bf16[16,32,1000]{2,1,0:T(8,128)(2,1)S(1)}, bf16[16,32,1000]{2,1,0:T(8,128)(2,1)S(1)}, u32[]{:S(2)}, u32[]{:S(2)}) collective-permute-start(bf16[16,32,1000]{2,1,0:T(8,128)(2,1)S(1)} %all-to-all-done.6), channel_id=1, source_target_pairs={{0,1},{1,0},{2,3},{3,2},{4,5},{5,4},{6,7},{7,6},{8,9},{9,8},{10,11... | collective-permute-start | bytes 3072008 | tf_op jit(solution)/shard_map/ppermute | solution.py:21
  248.2 5.8 %collective-permute-start.15 = (f32[32]{0:T(128)S(1)}, f32[32]{0:T(128)S(1)}, u32[]{:S(2)}, u32[]{:S(2)}) collective-permute-start(f32[32]{0:T(128)S(1)} %multiply_reduce_fusion.2), channel_id=1, source_target_pairs={{0,256},{256,0},{1,257},{257,1},{2,258},{258,2},{3,259},{259,3},{4... | collective-permute-start | bytes 392 | tf_op jit(solution)/shard_map/ppermute | solution.py:25
